TPU v7x, 256 devices: a whole 4x4x8 slice. The times are simulated.
256 devices in a mesh: pair: 32 (over z, x), virt: 8 (over y, core).
Axes of the slice: x: 4, y: 4, z: 8, core: 2. Of those that a mesh axis runs over, the one named last changes fastest.
Arguments:
- amplitudes: float32 [16, 256, 128, 128], P('virt', 'pair'), may hold values from -6 to 6
- factors: float32 [6, 16, 128, 128], replicated, may hold values from -0.5 to 0.5
- integral_quadruple_table: int32 [6, 16, 16, 3], replicated, may hold values from 0 to 15
- pair_region: int32 [128], replicated, may hold values from 0 to 5
- owner_map: int32 [256], replicated, may hold values from 0 to 31, as said below
Outputs:
- residual: float32 [16, 512, 128, 128], P('virt', 'pair')
Inputs may be any that keep to these rules, and one draw needn't show every extreme that they name: `owner_map`: home h holds pairs 8 * h to 8 * h + 7. No two pairs of one home share an owner, so every home sends exactly 1 pair to each owner it uses; no owner has more than 16 pairs, and some owners have exactly 16.
All inputs are finite; a program needn't handle non-finite values.
Results may differ from a plain program's by a relative error of at most 0.0003.
Values sent between devices are 32-bit elements; how exact they have to be, the bound alone decides.
No kernel may reach another device: no remote copies, remote signals or barrier semaphores. Data moves between devices by JAX's collectives and lax.ppermute only.
A program may use at most 128 MiB of HBM per device.

v0:
```python
import jax
import jax.numpy as jnp
from jax import lax
from jax.sharding import PartitionSpec as P

DOM = 4


def from_behind(block, axis, distance):
    devices = range(lax.axis_size(axis))
    route = [((i - distance) % len(devices), i) for i in devices]
    return lax.ppermute(block, axis, route)


def bucket_rows(value_entries, positions, alive_mask, width):
    items = positions.shape[0]
    matches = (positions[None, :] == jnp.arange(width)[:, None]) & alive_mask[None, :]
    anchor = jnp.sum(jnp.where(matches, jnp.arange(items)[None, :], 0), axis=1)
    filled = jnp.any(matches, axis=1)
    return jnp.where(filled[None, :, None, None], jnp.take(value_entries, anchor, axis=1), 0.0)


def on_device(amplitudes, factors, integral_quadruple_table, pair_region, owner_map):
    pair_count = lax.axis_size("pair")
    virt_count = lax.axis_size("virt")
    my_pair = lax.axis_index("pair")
    my_virt = lax.axis_index("virt")
    per_home = amplitudes.shape[1]
    local_slots = amplitudes.shape[0]
    slot_total = integral_quadruple_table.shape[1]
    pair_total = owner_map.shape[0]
    send_most = max(1, 2 * per_home // pair_count)
    own_most = 2 * per_home
    bucket_width = pair_count * send_most
    region = jnp.concatenate([pair_region, pair_region])
    home_of = jnp.arange(pair_total) // per_home
    owners_home = owner_map.reshape(pair_count, per_home)
    same_owner = owners_home[:, :, None] == owners_home[:, None, :]
    before = jnp.arange(per_home)[None, :] < jnp.arange(per_home)[:, None]
    rank_home = jnp.sum(same_owner & before[None, :, :], axis=2).reshape(pair_total)
    owner_pos = owner_map * send_most + rank_home
    home_pos = home_of * send_most + rank_home
    owned_mask = owner_map == my_pair
    own_rank = jnp.cumsum(owned_mask.astype(jnp.int32)) - 1
    chosen = owned_mask[None, :] & (own_rank[None, :] == jnp.arange(own_most)[:, None])
    slot_live = jnp.any(chosen, axis=1)
    slot_pair = jnp.sum(jnp.where(chosen, jnp.arange(pair_total)[None, :], 0), axis=1)
    local_ids = my_pair * per_home + jnp.arange(per_home)
    all_alive = jnp.ones((per_home,), bool)

    def one_pair(packed):
        amp_tiles, reg = packed
        quad_rows = integral_quadruple_table[reg]
        left_tiles = factors[reg][quad_rows[..., 1]]
        right_tiles = factors[reg][quad_rows[..., 2]]
        inner_prod = jnp.einsum(
            "skab,sbc->skac", left_tiles, amp_tiles, precision=lax.Precision.HIGHEST
        )
        product = jnp.einsum(
            "skac,skdc->skad", inner_prod, right_tiles, precision=lax.Precision.HIGHEST
        )
        onehot = (quad_rows[..., 0][..., None] == jnp.arange(slot_total)[None, None, :]).astype(
            jnp.float32
        )
        return jnp.einsum("sko,skad->oad", onehot, product, precision=lax.Precision.HIGHEST)

    outgoing = bucket_rows(amplitudes, owner_pos[local_ids], all_alive, bucket_width)
    incoming = lax.all_to_all(outgoing, "pair", split_axis=1, concat_axis=1, tiled=True)
    owned_tiles = jnp.where(
        slot_live[None, :, None, None], jnp.take(incoming, home_pos[slot_pair], axis=1), 0.0
    )
    group_size = owned_tiles.shape[1] // virt_count
    spread_across = lax.all_to_all(owned_tiles, "virt", split_axis=1, concat_axis=0, tiled=True)
    my_regions = lax.dynamic_slice_in_dim(region[slot_pair], my_virt * group_size, group_size, 0)
    results = lax.map(one_pair, (jnp.swapaxes(spread_across, 0, 1), my_regions))
    owner_result = lax.all_to_all(
        jnp.swapaxes(results, 0, 1), "virt", split_axis=0, concat_axis=1, tiled=True
    )
    returned = bucket_rows(owner_result, home_pos[slot_pair], slot_live, bucket_width)
    arrived = lax.all_to_all(returned, "pair", split_axis=1, concat_axis=1, tiled=True)
    home_result = jnp.take(arrived, owner_pos[local_ids], axis=1)
    mirrored = from_behind(home_result, "pair", pair_count // 2)
    global_slot = my_virt * local_slots + jnp.arange(local_slots)
    partner = (
        jnp.where(global_slot < DOM * (DOM - 1), global_slot ^ 1, global_slot)
        - my_virt * local_slots
    )
    outgoing = bucket_rows(
        home_result + jnp.swapaxes(jnp.take(mirrored, partner, axis=0), -1, -2),
        owner_pos[local_ids],
        all_alive,
        bucket_width,
    )
    incoming = lax.all_to_all(outgoing, "pair", split_axis=1, concat_axis=1, tiled=True)
    gathered = jnp.take(incoming, home_pos[slot_pair], axis=1)
    return jnp.where(slot_live[None, :, None, None], gathered, 0.0)


def solution(mesh):
    return jax.shard_map(
        on_device,
        mesh=mesh,
        in_specs=(P("virt", "pair", None, None), P(), P(), P(), P()),
        out_specs=P("virt", "pair", None, None),
        check_vma=False,
    )
```

profile of v0, /device:TPU:2, one launch (start us, length us, event | category | flops | bytes accessed | tf_op | source)
XLA Modules:
  0.0 680.7 jit_solution(17382013134529848554)
XLA Ops:
  0.0 0.8 eq.50
  1.2 0.7 fusion.17
  2.8 2.8 gather_fusion.8
  5.6 5.1 bitcast_select_fusion.1
  10.7 11.8 %all-to-all-start = ((f32[2,32,128,128]{3,2,0,1:T(8,128)}), f32[2,32,128,128]{3,2,0,1:T(8,128)}, u32[]{:S(2)}, u32[]{:S(2)}) async-start(f32[2,32,128,128]{3,2,0,1:T(8,128)} %bitcast_select_fusion.1), calls=%async_computation | async-start | bytes 8388608 | tf_op jit(solution)/shard_map/all_to_all | solution.py:68
  23.3 0.7 gather_fusion.3
  24.1 92.2 %all-to-all-done = f32[2,32,128,128]{3,2,0,1:T(8,128)} async-done(((f32[2,32,128,128]{3,2,0,1:T(8,128)}), f32[2,32,128,128]{3,2,0,1:T(8,128)}, u32[]{:S(2)}, u32[]{:S(2)}) %all-to-all-start) | async-done | bytes 4194336 | tf_op jit(solution)/shard_map/all_to_all | solution.py:68
  116.3 4.7 copy.44
  121.0 2.9 gather_fusion.9
  123.9 1.7 bitcast_select_fusion.3
  125.6 4.5 all-to-all-start.1
  130.8 26.4 %all-to-all-done.1 = f32[2,16,128,128]{3,2,0,1:T(8,128)S(1)} async-done(((f32[2,16,128,128]{3,2,0,1:T(8,128)}), f32[2,16,128,128]{3,2,0,1:T(8,128)S(1)}, u32[]{:S(2)}, u32[]{:S(2)}) %all-to-all-start.1) | async-done | bytes 2097184 | tf_op jit(solution)/shard_map/all_to_all | solution.py:73
  157.3 1.3 copy-done.2
  158.6 1.7 copy.45
  160.3 204.7 %while.11 = (s32[]{:T(128)}, f32[2,16,128,128]{3,2,0,1:T(8,128)}, s32[2]{0:T(128)S(1)}, s32[6,16,16,3]{2,1,3,0:T(8,128)}, f32[6,16,128,128]{3,2,1,0:T(8,128)}, /*index=5*/f32[2,16,128,128]{3,2,1,0:T(8,128)S(1)}) while((s32[]{:T(128)}, f32[2,16,128,128]{3,2,0,1:T(8,128)}, s32[2]{0:T(128)S(1)}, s32[6,16,16,3]{2,1,3,0:T(8,128)}, ...), condition=%wide.region_10.13_spmd.clone, body=%wide.region_9.12_spmd.sunk.clone | while | flops 13690216448 | bytes 174096000 | solution.py:75
  163.0 0.7 dynamic-slice_bitcast_fusion.7
  163.8 1.3 dynamic-slice_bitcast_fusion.6
  165.1 7.3 %gather_fusion = f32[256,128,128]{2,1,0:T(8,128)} fusion(f32[16,128,128]{2,1,0:T(8,128)S(1)} %dynamic-slice_bitcast_fusion.6, s32[1024]{0:T(1024)S(1)} %pad_clamp_fusion.13), kind=kCustom, calls=%fused_computation.2.clone.1.clone | custom fusion | bytes 33555456 | tf_op jit(solution)/shard_map/while/body/eval_jaxpr/gather | solution.py:54
  172.5 18.8 %fusion.53 = f32[16,16,128,128]{3,2,1,0:T(8,128)} fusion(f32[16,16,128,128]{3,2,1,0:T(8,128)} %bitcast.113, f32[2,16,128,128]{3,2,1,0:T(8,128)S(1)} %get-tuple-element.168, s32[]{:T(128)} %get-tuple-element.157), kind=kOutput, calls=%fused_computation.16.clone.1.clone | convolution fusion | flops 6442450944 | bytes 34603012 | tf_op jit(solution)/shard_map/while/body/eval_jaxpr/skab,sbc->skac/dot_general | solution.py:56
  191.4 7.3 %gather_fusion.1 = f32[256,128,128]{2,1,0:T(8,128)} fusion(f32[16,128,128]{2,1,0:T(8,128)S(1)} %dynamic-slice_bitcast_fusion.6, s32[1024]{0:T(1024)S(1)} %pad_clamp_fusion.14), kind=kCustom, calls=%fused_computation.3.clone.1.clone | custom fusion | bytes 33555456 | tf_op jit(solution)/shard_map/while/body/eval_jaxpr/gather | solution.py:55
  198.7 40.8 %fusion.54 = f32[16,16,128,128]{3,2,1,0:T(8,128)} fusion(f32[16,16,128,128]{3,2,1,0:T(8,128)} %fusion.53, f32[16,16,128,128]{3,2,1,0:T(8,128)} %bitcast.112), kind=kOutput, calls=%fused_computation.91.clone.1.clone | convolution fusion | flops 6442450944 | bytes 50331648 | tf_op jit(solution)/shard_map/while/body/eval_jaxpr/skac,skdc->skad/dot_general | solution.py:59
  239.6 21.9 %fusion.55 = f32[1,16,128,128]{3,1,2,0:T(8,128)S(1)} fusion(f32[16,16,128,128]{3,2,1,0:T(8,128)} %fusion.54, s32[16,16]{0,1:T(8,128)S(1)} %copy.72), kind=kOutput, calls=%fused_computation.14.clone.1.clone | convolution fusion | flops 805310464 | bytes 17826816 | tf_op jit(solution)/shard_map/while/body/eval_jaxpr/sko,skad->oad/dot_general | solution.py:65
  261.5 1.3 copy_dynamic-update-slice_fusion.3
  265.2 0.7 dynamic-slice_bitcast_fusion.7
  266.1 1.3 dynamic-slice_bitcast_fusion.6
  267.4 7.3 %gather_fusion = f32[256,128,128]{2,1,0:T(8,128)} fusion(f32[16,128,128]{2,1,0:T(8,128)S(1)} %dynamic-slice_bitcast_fusion.6, s32[1024]{0:T(1024)S(1)} %pad_clamp_fusion.13), kind=kCustom, calls=%fused_computation.2.clone.1.clone | custom fusion | bytes 33555456 | tf_op jit(solution)/shard_map/while/body/eval_jaxpr/gather | solution.py:54
  274.7 18.8 %fusion.53 = f32[16,16,128,128]{3,2,1,0:T(8,128)} fusion(f32[16,16,128,128]{3,2,1,0:T(8,128)} %bitcast.113, f32[2,16,128,128]{3,2,1,0:T(8,128)S(1)} %get-tuple-element.168, s32[]{:T(128)} %get-tuple-element.157), kind=kOutput, calls=%fused_computation.16.clone.1.clone | convolution fusion | flops 6442450944 | bytes 34603012 | tf_op jit(solution)/shard_map/while/body/eval_jaxpr/skab,sbc->skac/dot_general | solution.py:56
  293.6 7.3 %gather_fusion.1 = f32[256,128,128]{2,1,0:T(8,128)} fusion(f32[16,128,128]{2,1,0:T(8,128)S(1)} %dynamic-slice_bitcast_fusion.6, s32[1024]{0:T(1024)S(1)} %pad_clamp_fusion.14), kind=kCustom, calls=%fused_computation.3.clone.1.clone | custom fusion | bytes 33555456 | tf_op jit(solution)/shard_map/while/body/eval_jaxpr/gather | solution.py:55
  301.0 40.8 %fusion.54 = f32[16,16,128,128]{3,2,1,0:T(8,128)} fusion(f32[16,16,128,128]{3,2,1,0:T(8,128)} %fusion.53, f32[16,16,128,128]{3,2,1,0:T(8,128)} %bitcast.112), kind=kOutput, calls=%fused_computation.91.clone.1.clone | convolution fusion | flops 6442450944 | bytes 50331648 | tf_op jit(solution)/shard_map/while/body/eval_jaxpr/skac,skdc->skad/dot_general | solution.py:59
  341.8 21.9 %fusion.55 = f32[1,16,128,128]{3,1,2,0:T(8,128)S(1)} fusion(f32[16,16,128,128]{3,2,1,0:T(8,128)} %fusion.54, s32[16,16]{0,1:T(8,128)S(1)} %copy.72), kind=kOutput, calls=%fused_computation.14.clone.1.clone | convolution fusion | flops 805310464 | bytes 17826816 | tf_op jit(solution)/shard_map/while/body/eval_jaxpr/sko,skad->oad/dot_general | solution.py:65
  363.7 1.3 copy_dynamic-update-slice_fusion.3
  365.0 3.7 all-to-all-start.2
  369.0 26.9 %all-to-all-done.2 = f32[16,2,128,128]{3,2,1,0:T(8,128)S(1)} async-done(((f32[16,2,128,128]{3,2,1,0:T(8,128)}), f32[16,2,128,128]{3,2,1,0:T(8,128)S(1)}, u32[]{:S(2)}, u32[]{:S(2)}) %all-to-all-start.2) | async-done | bytes 2097184 | tf_op jit(solution)/shard_map/all_to_all | solution.py:76
  395.9 1.3 copy-done.3
  397.2 1.7 copy.48
  399.0 2.8 gather_fusion.5
  401.7 5.1 select_bitcast_fusion
  406.9 7.6 %all-to-all-start.3 = ((f32[2,32,128,128]{3,2,0,1:T(8,128)}), f32[2,32,128,128]{3,2,0,1:T(8,128)}, u32[]{:S(2)}, u32[]{:S(2)}) async-start(f32[2,32,128,128]{3,2,0,1:T(8,128)} %select_bitcast_fusion), calls=%async_computation.3 | async-start | bytes 8388608 | tf_op jit(solution)/shard_map/all_to_all | solution.py:80
  414.5 93.4 %all-to-all-done.3 = f32[2,32,128,128]{3,2,0,1:T(8,128)} async-done(((f32[2,32,128,128]{3,2,0,1:T(8,128)}), f32[2,32,128,128]{3,2,0,1:T(8,128)}, u32[]{:S(2)}, u32[]{:S(2)}) %all-to-all-start.3) | async-done | bytes 4194336 | tf_op jit(solution)/shard_map/all_to_all | solution.py:80
  507.9 4.7 copy.49
  512.5 2.8 gather_fusion.6
  516.0 51.0 %collective-permute-done = f32[2,8,128,128]{3,2,0,1:T(8,128)S(1)} collective-permute-done((f32[2,8,128,128]{3,2,0,1:T(8,128)S(1)}, f32[2,8,128,128]{3,2,0,1:T(8,128)S(1)}, u32[]{:S(2)}, u32[]{:S(2)}) %collective-permute-start) | collective-permute-done | bytes 1048608 | tf_op jit(solution)/shard_map/ppermute | solution.py:12
  568.4 2.9 gather_fusion.10
  571.3 3.0 bitcast_select_fusion
  574.3 99.3 %all_to_all.51 = f32[2,32,128,128]{3,2,0,1:T(8,128)S(1)} all-to-all(f32[2,32,128,128]{3,2,0,1:T(8,128)S(1)} %bitcast_select_fusion), channel_id=1, replica_groups=mesh['pair'=32,'virt'=8] {'pair'}, dimensions={1} | all-to-all | bytes 8388608 | tf_op jit(solution)/shard_map/all_to_all | solution.py:94
  673.6 2.2 copy.53
  675.8 3.1 gather_fusion.11
  679.3 1.5 copy.54
  (101 shorter events, 7.2 us)
Async XLA Ops:
  0.0 2.8 copy-start
  2.6 3.0 copy-start.15
  2.7 2.9 copy-start.9
  2.8 2.8 copy-start.11
  2.8 2.8 copy-start.5
  10.7 11.8 %copy-start.4 = (s32[256]{0:T(256)S(1)}, s32[256]{0:T(256)}, u32[]{:S(2)}) copy-start(s32[256]{0:T(256)} %param.15) | copy-start | bytes 3076
  10.7 105.6 %all-to-all-start = ((f32[2,32,128,128]{3,2,0,1:T(8,128)}), f32[2,32,128,128]{3,2,0,1:T(8,128)}, u32[]{:S(2)}, u32[]{:S(2)}) async-start(f32[2,32,128,128]{3,2,0,1:T(8,128)} %bitcast_select_fusion.1), calls=%async_computation | async-start | bytes 8388608 | tf_op jit(solution)/shard_map/all_to_all | solution.py:68
  24.0 97.0 %copy-start.17 = (s32[16]{0:T(128)}, s32[16]{0:T(128)S(1)}, u32[]{:S(2)}) copy-start(s32[16]{0:T(128)S(1)} %gather_fusion.3) | copy-start | bytes 196
  24.0 97.0 %copy-start.6 = (s32[1024]{0:T(1024)}, s32[1024]{0:T(1024)S(1)}, u32[]{:S(2)}) copy-start(s32[1024]{0:T(1024)S(1)} %pad_clamp_fusion.5) | copy-start | bytes 12292
  24.1 99.8 %copy-start.7 = (pred[16]{0:T(512)(128)(4,1)}, pred[16]{0:T(512)(128)(4,1)S(1)}, u32[]{:S(2)}) copy-start(pred[16]{0:T(512)(128)(4,1)S(1)} %fusion.13) | copy-start | bytes 52
  24.1 99.7 %copy-start.13 = (pred[16]{0:T(512)(128)(4,1)}, pred[16]{0:T(512)(128)(4,1)S(1)}, u32[]{:S(2)}) copy-start(pred[16]{0:T(512)(128)(4,1)S(1)} %compare_and_fusion) | copy-start | bytes 52
  123.9 6.2 copy-start.19
  125.6 31.7 %all-to-all-start.1 = ((f32[2,16,128,128]{3,2,0,1:T(8,128)}), f32[2,16,128,128]{3,2,0,1:T(8,128)S(1)}, u32[]{:S(2)}, u32[]{:S(2)}) async-start(f32[2,16,128,128]{3,2,0,1:T(8,128)} %bitcast_select_fusion.3), calls=%async_computation.1 | async-start | bytes 4194304 | tf_op jit(solution)/shard_map/all_to_all | solution.py:73
  157.3 1.3 copy-start.2
  365.0 3.8 copy-start.8
  365.0 3.8 copy-start.18
  365.0 30.9 %all-to-all-start.2 = ((f32[16,2,128,128]{3,2,1,0:T(8,128)}), f32[16,2,128,128]{3,2,1,0:T(8,128)S(1)}, u32[]{:S(2)}, u32[]{:S(2)}) async-start(f32[16,2,128,128]{3,2,1,0:T(8,128)} %bitcast.24), calls=%async_computation.2 | async-start | bytes 4194304 | tf_op jit(solution)/shard_map/all_to_all | solution.py:76
  395.9 1.3 copy-start.3
  406.9 7.6 %copy-start.16 = (s32[8]{0:T(128)S(1)}, s32[8]{0:T(128)}, u32[]{:S(2)}) copy-start(s32[8]{0:T(128)} %copy-done.15) | copy-start | bytes 100
  406.9 101.0 %all-to-all-start.3 = ((f32[2,32,128,128]{3,2,0,1:T(8,128)}), f32[2,32,128,128]{3,2,0,1:T(8,128)}, u32[]{:S(2)}, u32[]{:S(2)}) async-start(f32[2,32,128,128]{3,2,0,1:T(8,128)} %select_bitcast_fusion), calls=%async_computation.3 | async-start | bytes 8388608 | tf_op jit(solution)/shard_map/all_to_all | solution.py:80
  515.5 51.6 %collective-permute-start = (f32[2,8,128,128]{3,2,0,1:T(8,128)S(1)}, f32[2,8,128,128]{3,2,0,1:T(8,128)S(1)}, u32[]{:S(2)}, u32[]{:S(2)}) collective-permute-start(f32[2,8,128,128]{3,2,0,1:T(8,128)S(1)} %select_bitcast_fusion.1), channel_id=1, source_target_pairs={{128,0},{136,8},{144,16},{152,24},{160,32},{168,40},{176,48},{184,... | collective-permute-start | bytes 3145736 | tf_op jit(solution)/shard_map/ppermute | solution.py:12
  568.4 2.9 copy-start.10
  568.4 2.9 copy-start.12
  675.8 3.1 copy-start.14
  675.8 4.9 copy-start.1
where the time goes:
time: 682 us; the launch traced here: 681 us
  waiting for transfers between devices  290 us (43%)
  matrix products  163 us (24%)
  blocking collectives  99.3 us (15%)
  local copies, waits for them, and re-layouts  78.5 us (12%)
  starting transfers between devices  28.1 us (4%)
  other arithmetic  17.7 us (3%)
    all_to_all x1, blocking collectives, on_device(): lax.all_to_all(outgoing, 'pair', split_axis=1, concat_axis=1, tiled=True)  99.3 us
    all_to_all x1, waiting for transfers between devices, on_device(): lax.all_to_all(returned, 'pair', split_axis=1, concat_axis=1, tiled=True)  93.4 us
    all_to_all x1, waiting for transfers between devices, on_device(): lax.all_to_all(outgoing, 'pair', split_axis=1, concat_axis=1, tiled=True)  92.2 us
    dot_general x2, matrix products, one_pair(): jnp.einsum('skac,skdc->skad', inner_prod, right_tiles, precision=lax.Prec...  81.6 us
    ppermute x1, waiting for transfers between devices, from_behind(): return lax.ppermute(block, axis, route)  51 us
    dot_general x2, matrix products, one_pair(): jnp.einsum('sko,skad->oad', onehot, product, precision=lax.Precision.HIGH...  43.8 us
    dot_general x2, matrix products, one_pair(): jnp.einsum('skab,sbc->skac', left_tiles, amp_tiles, precision=lax.Precisi...  37.6 us
    all_to_all x1, waiting for transfers between devices, on_device(): lax.all_to_all(jnp.swapaxes(results, 0, 1), 'virt', split_axis=0, concat_...  26.9 us
  transfers between devices with their start and end apart: 5, of which 5 were waited for; matrix products, arithmetic and copies ran while one was open for 0% of the time, Pallas kernels for 0%

commit v1 on v0

v1 whole, which is shorter than its diff:
```python
import jax
import jax.numpy as jnp
from jax import lax
from jax.experimental import pallas as pl
from jax.experimental.pallas import tpu as pltpu
from jax.sharding import PartitionSpec as P

DOM = 4
OFF_DIAG = DOM * (DOM - 1)
F32 = jnp.float32
BF16 = jnp.bfloat16


def halves(x):
    high = x.astype(BF16)
    return high, (x - high.astype(F32)).astype(BF16)


def ladder_body(
    codes, info, even, odd, fac, out, f_pair, f_turn, amp_high, amp_low, prod, grouped
):
    slots, n, _ = out.shape
    mirrored = info[1]

    def split_factor(l, c):
        tile = fac[0, l]
        rows = pl.ds(pl.multiple_of(l * n, n), n)
        high, low = halves(tile)
        f_pair[rows, :n] = high
        f_pair[rows, n:] = low
        high, low = halves(tile.T)
        f_turn[rows, :n] = high
        f_turn[rows, n:] = low
        return c

    lax.fori_loop(0, slots, split_factor, 0)

    def put_amp(i, v, tile):
        high, low = halves(tile)
        amp_high[v, :, i * n : (i + 1) * n] = high
        amp_low[v, :, i * n : (i + 1) * n] = low

    @pl.when(mirrored == 0)
    def _():
        def go(v, c):
            put_amp(0, v, even[v])
            put_amp(1, v, odd[v])
            return c

        lax.fori_loop(0, slots // 2, go, 0)

    @pl.when(mirrored != 0)
    def _():
        def go(v, c):
            put_amp(0, v, even[v].T)
            put_amp(1, v, odd[v].T)
            return c

        lax.fori_loop(0, slots // 2, go, 0)

    def clear(r, c):
        grouped[r] = jnp.zeros(grouped.shape[1:], F32)
        return c

    lax.fori_loop(0, slots, clear, 0)

    def one_amp_pair(v, c):
        high = amp_high[v]
        prod[...] = jnp.dot(
            f_pair[...], jnp.concatenate([high, high], axis=0), preferred_element_type=F32
        ) + jnp.dot(f_pair[:, :n], amp_low[v], preferred_element_type=F32)
        for i in range(2):

            def entry(k, c):
                code = codes[2 * v + i, k]
                o = code // 256
                l = (code // 16) % 16
                r = code % 16
                to = pl.ds(pl.multiple_of(o * n, n), n)
                grouped[r, to, :] += prod[
                    pl.ds(pl.multiple_of(l * n, n), n), i * n : (i + 1) * n
                ]
                return c

            lax.fori_loop(0, codes.shape[1], entry, 0, unroll=4)
        return c

    lax.fori_loop(0, slots // 2, one_amp_pair, 0)

    step = 4

    def one_out(g, c):
        rows = pl.ds(pl.multiple_of(g * (step * n), step * n), step * n)
        parts = [halves(grouped[r, rows, :]) for r in range(slots)]
        high = jnp.concatenate([a for a, _ in parts], axis=1)
        low = jnp.concatenate([b for _, b in parts], axis=1)
        both = jnp.dot(high, f_turn[...], preferred_element_type=F32)
        rest = jnp.dot(low, f_turn[:, :n], preferred_element_type=F32)
        total = both[:, :n] + both[:, n:] + rest
        out[pl.ds(g * step, step)] = total.reshape(step, n, n)
        return c

    lax.fori_loop(0, slots // step, one_out, 0)


def ladder(codes, info, even, odd, factors):
    slots = 2 * even.shape[0]
    n = even.shape[-1]
    whole = pl.BlockSpec((slots // 2, n, n), lambda i, *_: (0, 0, 0))
    wide = slots * n
    return pl.pallas_call(
        ladder_body,
        out_shape=jax.ShapeDtypeStruct((slots, n, n), F32),
        grid_spec=pltpu.PrefetchScalarGridSpec(
            num_scalar_prefetch=2,
            grid=(1,),
            in_specs=[
                whole,
                whole,
                pl.BlockSpec((1, slots, n, n), lambda i, codes, info: (info[0], 0, 0, 0)),
            ],
            out_specs=pl.BlockSpec((slots, n, n), lambda i, *_: (0, 0, 0)),
            scratch_shapes=[
                pltpu.VMEM((wide, 2 * n), BF16),
                pltpu.VMEM((wide, 2 * n), BF16),
                pltpu.VMEM((slots // 2, n, 2 * n), BF16),
                pltpu.VMEM((slots // 2, n, 2 * n), BF16),
                pltpu.VMEM((wide, 2 * n), F32),
                pltpu.VMEM((slots, wide, n), F32),
            ],
        ),
        compiler_params=pltpu.CompilerParams(vmem_limit_bytes=48 << 20),
        cost_estimate=pl.CostEstimate(
            flops=12 * wide * wide * n, bytes_accessed=4 << 20, transcendentals=0
        ),
        name="ladder",
    )(codes, info, even, odd, factors)


def pairs_body(spot, blocks, out, *, per_home):
    count = blocks.shape[0]
    homes = count // per_home
    half = count // 2
    out[...] = jnp.zeros(out.shape, F32)

    def one(q, c):
        row = (q % per_home) * homes + q // per_home
        value = blocks[row] + blocks[row + homes // 2]
        out[spot[q]] = value
        out[spot[q + half]] = value
        return c

    lax.fori_loop(0, half, one, 0, unroll=4)


def join_pairs(spot, blocks, own_slots, per_home):
    def body(spot, blocks, out):
        pairs_body(spot, blocks, out, per_home=per_home)

    return pl.pallas_call(
        body,
        out_shape=jax.ShapeDtypeStruct((own_slots,) + blocks.shape[1:], F32),
        grid_spec=pltpu.PrefetchScalarGridSpec(
            num_scalar_prefetch=1,
            grid=(1,),
            in_specs=[pl.BlockSpec(blocks.shape, lambda i, *_: (0, 0, 0))],
            out_specs=pl.BlockSpec((own_slots,) + blocks.shape[1:], lambda i, *_: (0, 0, 0)),
        ),
        compiler_params=pltpu.CompilerParams(vmem_limit_bytes=16 << 20),
        cost_estimate=pl.CostEstimate(flops=1 << 18, bytes_accessed=3 << 20, transcendentals=0),
        name="join_pairs",
    )(spot, blocks)


def settle(info, blocks, own_most, local_slots, n, group):
    parts = blocks.shape[0]
    per = parts // local_slots

    def body(info, src, out):
        plain = info[0]
        swap = info[1]
        for g in range(group):
            k = pl.program_id(0) * group + g

            @pl.when(k < plain)
            def _():
                for i in range(local_slots):
                    out[i, g] = src[i * per : (i + 1) * per, g].reshape(n, n)

            @pl.when(k >= plain)
            def _():
                for i in range(local_slots):
                    base = jnp.where(swap != 0, local_slots - 1 - i, i) * per
                    out[i, g] = src[pl.ds(base, per), g].reshape(n, n).T

    return pl.pallas_call(
        body,
        out_shape=jax.ShapeDtypeStruct((local_slots, own_most, n, n), F32),
        grid_spec=pltpu.PrefetchScalarGridSpec(
            num_scalar_prefetch=1,
            grid=(own_most // group,),
            in_specs=[
                pl.BlockSpec(
                    (parts, group) + blocks.shape[2:], lambda i, *_: (0, i, 0, 0)
                )
            ],
            out_specs=pl.BlockSpec((local_slots, group, n, n), lambda i, *_: (0, i, 0, 0)),
        ),
        compiler_params=pltpu.CompilerParams(vmem_limit_bytes=16 << 20),
        cost_estimate=pl.CostEstimate(flops=1 << 18, bytes_accessed=4 << 20, transcendentals=0),
        name="settle",
    )(info, blocks)


def on_device(amplitudes, factors, integral_quadruple_table, pair_region, owner_map):
    pair_count = lax.axis_size("pair")
    virt_count = lax.axis_size("virt")
    my_pair = lax.axis_index("pair")
    my_virt = lax.axis_index("virt")
    local_slots, per_home, n, _ = amplitudes.shape
    pair_total = owner_map.shape[0]
    half = pair_total // 2
    own_most = 2 * per_home

    pair = my_pair * per_home + my_virt
    mirrored = (pair >= half).astype(jnp.int32)
    region = pair_region[pair % half]
    rows = integral_quadruple_table[region]
    o, left, right = rows[..., 0], rows[..., 1], rows[..., 2]
    partner = jnp.where(o < OFF_DIAG, o ^ 1, o)
    codes = jnp.where(
        mirrored != 0, partner * 256 + right * 16 + left, o * 256 + left * 16 + right
    )
    info = jnp.stack([region, mirrored])

    same = (owner_map[:, None] == owner_map[None, :]) & (
        jnp.arange(pair_total)[None, :] < jnp.arange(pair_total)[:, None]
    )
    spot = owner_map * own_most + jnp.sum(same.astype(jnp.int32), axis=1)

    even = lax.all_to_all(amplitudes[0], "virt", split_axis=0, concat_axis=0, tiled=True)
    odd = lax.all_to_all(amplitudes[1], "virt", split_axis=0, concat_axis=0, tiled=True)
    result = ladder(codes, info, even, odd, factors)
    sheets = result.reshape(virt_count * pair_count, -1, n)
    spread = lax.all_to_all(sheets, ("virt", "pair"), split_axis=0, concat_axis=0, tiled=True)
    joined = join_pairs(spot, spread, pair_count * own_most, per_home)
    arrived = lax.all_to_all(joined, "pair", split_axis=0, concat_axis=0, tiled=True)
    plain = jnp.sum((owner_map[:half] == my_pair).astype(jnp.int32))
    swap = (my_virt * local_slots < OFF_DIAG).astype(jnp.int32)
    return settle(
        jnp.stack([plain, swap]),
        arrived.reshape(pair_count, own_most, -1, n),
        own_most,
        local_slots,
        n,
        4,
    )


def solution(mesh):
    return jax.shard_map(
        on_device,
        mesh=mesh,
        in_specs=(P("virt", "pair", None, None), P(), P(), P(), P()),
        out_specs=P("virt", "pair", None, None),
        check_vma=False,
    )
```

time: 682 us -> 158 us (0.23)
  waiting for transfers between devices: 290 us -> 85.7 us
  matrix products: 163 us -> 0 us
  blocking collectives: 99.3 us -> 14.7 us
  local copies, waits for them, and re-layouts: 78.5 us -> 4.05 us
  Pallas kernels: 0 us -> 26.1 us
  other arithmetic: 17.7 us -> 2.3 us
    dot_general x6 -> x0, matrix products: 163 us -> none  [the longest x2 81.6 us: one_pair(): jnp.einsum('skac,skdc->skad', inner_prod, right_tiles, precision=lax.Prec...]
    all_to_all x4 -> x3, waiting for transfers between devices: 239 us -> 85.7 us  [the longest x1 48.5 us: on_device(): lax.all_to_all(joined, 'pair', split_axis=0, concat_axis=0, tiled=True)]
    all_to_all x1, blocking collectives: 99.3 us -> 14.7 us  [on_device(): lax.all_to_all(amplitudes[1], 'virt', split_axis=0, concat_axis=0, tiled=...]
    ppermute x1 -> x0, waiting for transfers between devices: 51 us -> none  [from_behind(): return lax.ppermute(block, axis, route)]
    gather x15 -> x0, local copies, waits for them, and re-layouts: 49.5 us -> none  [the longest x2 14.7 us: one_pair(): right_tiles = factors[reg][quad_rows[..., 2]]]
    pallas_call x0 -> x3, Pallas kernels: none -> 26.1 us  [the longest x1 20.7 us: ladder(): pl.pallas_call(ladder_body, out_shape=jax.ShapeDtypeStruct((slots, n, n),...]
    select_n x13 -> x1, other arithmetic: 15.5 us -> 0.01 us  [on_device(): jnp.where(mirrored != 0, partner * 256 + right * 16 + left, o * 256 + lef...]
    all_to_all x5 -> x0, local copies, waits for them, and re-layouts: 15 us -> none  [the longest x2 6.87 us: on_device(): lax.all_to_all(outgoing, 'pair', split_axis=1, concat_axis=1, tiled=True)]
  transfers between devices with their start and end apart: 5 -> 3, of which waited for: 5 -> 3; matrix products, arithmetic and copies ran while one was open for 0% -> 2% of each run, Pallas kernels for 0% -> 0%
where the time goes in v1:
time: 158 us
  waiting for transfers between devices  85.7 us (54%)
  Pallas kernels  26.1 us (17%)
  starting transfers between devices  23.2 us (15%)
  blocking collectives  14.7 us (9%)
  local copies, waits for them, and re-layouts  4.05 us (3%)
  other arithmetic  2.3 us (1%)
  between operations  1.78 us (1%)
    all_to_all x1, waiting for transfers between devices, on_device(): lax.all_to_all(joined, 'pair', split_axis=0, concat_axis=0, tiled=True)  48.5 us
    all_to_all x1, waiting for transfers between devices, on_device(): lax.all_to_all(sheets, ('virt', 'pair'), split_axis=0, concat_axis=0, til...  29.8 us
    pallas_call x1, Pallas kernels, ladder(): pl.pallas_call(ladder_body, out_shape=jax.ShapeDtypeStruct((slots, n, n),...  20.7 us
    all_to_all x1, blocking collectives, on_device(): lax.all_to_all(amplitudes[1], 'virt', split_axis=0, concat_axis=0, tiled=...  14.7 us
    all_to_all x1, starting transfers between devices, on_device(): lax.all_to_all(sheets, ('virt', 'pair'), split_axis=0, concat_axis=0, til...  13.3 us
    all_to_all x1, waiting for transfers between devices, on_device(): lax.all_to_all(amplitudes[0], 'virt', split_axis=0, concat_axis=0, tiled=...  7.32 us
    all_to_all x1, starting transfers between devices, on_device(): lax.all_to_all(joined, 'pair', split_axis=0, concat_axis=0, tiled=True)  6.38 us
    pallas_call x1, Pallas kernels, settle(): pl.pallas_call(body, out_shape=jax.ShapeDtypeStruct((local_slots, own_mos...  3.54 us
  transfers between devices with their start and end apart: 3, of which 3 were waited for; matrix products, arithmetic and copies ran while one was open for 2% of the time, Pallas kernels for 0%

profile of v1, /device:TPU:2, one launch (start us, length us, event | category | flops | bytes accessed | tf_op | source)
XLA Modules:
  0.0 157.7 jit_solution(14611827828172483953)
XLA Ops:
  0.0 0.0 copy-start
  0.0 0.0 copy-start.3
  0.0 2.1 %slice_bitcast_fusion = (f32[8,128,128]{2,1,0:T(8,128)S(1)}, f32[8,128,128]{2,1,0:T(8,128)}) fusion(f32[2,8,128,128]{3,2,1,0:T(8,128)} %param.5), kind=kLoop, calls=%fused_computation | loop fusion | bytes 2097152 | tf_op jit(solution)/shard_map/squeeze | solution.py:242
  2.1 14.7 %all_to_all.20.odd = f32[8,128,128]{2,1,0:T(8,128)S(1)} all-to-all(f32[8,128,128]{2,1,0:T(8,128)S(1)} %get-tuple-element.5), channel_id=1, replica_groups=mesh['pair'=32,'virt'=8] {'virt'}, dimensions={0} | all-to-all | bytes 1048576 | tf_op jit(solution)/shard_map/all_to_all | solution.py:242
  16.8 3.5 %all-to-all-start = ((f32[8,128,128]{2,1,0:T(8,128)}), f32[8,128,128]{2,1,0:T(8,128)S(1)}, u32[]{:S(2)}, u32[]{:S(2)}) async-start(f32[8,128,128]{2,1,0:T(8,128)} %get-tuple-element.6), calls=%async_computation | async-start | bytes 1048576 | tf_op jit(solution)/shard_map/all_to_all | solution.py:241
  20.3 0.0 copy-done.3
  20.3 0.6 dynamic_slice.6
  22.6 0.6 pad_add_fusion.1.info
  23.2 0.0 copy-done
  23.3 7.3 %all-to-all-done.even = f32[8,128,128]{2,1,0:T(8,128)S(1)} async-done(((f32[8,128,128]{2,1,0:T(8,128)}), f32[8,128,128]{2,1,0:T(8,128)S(1)}, u32[]{:S(2)}, u32[]{:S(2)}) %all-to-all-start) | async-done | bytes 524320 | tf_op jit(solution)/shard_map/all_to_all | solution.py:241
  30.6 20.7 %ladder.1 = f32[16,128,128]{2,1,0:T(8,128)} custom-call(s32[16,16]{1,0:T(8,128)S(1)} %fusion.4.codes, s32[2]{0:T(128)S(1)} %pad_add_fusion.1.info, f32[8,128,128]{2,1,0:T(8,128)S(1)} %all-to-all-done.even, f32[8,128,128]{2,1,0:T(8,128)S(1)} %all_to_all.20.odd, f32[6,16,128,128]{3,2,1,0:T(8,128)} %fac.1), custom_call_target="tpu_custom_call" | custom-call | flops 6442450944 | bytes 4194304 | tf_op jit(solution)/shard_map/ladder/pallas_call | solution.py:111
  51.3 0.0 copy-start.2
  51.3 13.3 %all-to-all-start.2 = ((f32[256,8,128]{2,1,0:T(8,128)}), f32[256,8,128]{2,1,0:T(8,128)S(1)}, u32[]{:S(2)}, u32[]{:S(2)}) async-start(f32[256,8,128]{2,1,0:T(8,128)} %bitcast.10), calls=%async_computation.2 | async-start | bytes 2097152 | tf_op jit(solution)/shard_map/all_to_all | solution.py:245
  64.6 0.0 copy-done.2
  64.6 0.2 convert_reduce_fusion
  64.8 29.8 %all-to-all-done.2.blocks = f32[256,8,128]{2,1,0:T(8,128)S(1)} async-done(((f32[256,8,128]{2,1,0:T(8,128)}), f32[256,8,128]{2,1,0:T(8,128)S(1)}, u32[]{:S(2)}, u32[]{:S(2)}) %all-to-all-start.2) | async-done | bytes 1048608 | tf_op jit(solution)/shard_map/all_to_all | solution.py:245
  94.6 1.9 %join_pairs.1 = f32[512,8,128]{2,1,0:T(8,128)S(1)} custom-call(s32[256]{0:T(256)S(1)} %multiply_add_fusion.spot, f32[256,8,128]{2,1,0:T(8,128)S(1)} %all-to-all-done.2.blocks), custom_call_target="tpu_custom_call" | custom-call | flops 262144 | bytes 3145728 | tf_op jit(solution)/shard_map/join_pairs/pallas_call | solution.py:160
  96.5 0.0 copy-start.1
  96.5 1.3 copy-done.1
  97.8 6.4 %all-to-all-start.3 = ((f32[512,8,128]{2,1,0:T(8,128)}), f32[512,8,128]{2,1,0:T(8,128)S(1)}, u32[]{:S(2)}, u32[]{:S(2)}) async-start(f32[512,8,128]{2,1,0:T(8,128)} %copy-done.1), calls=%async_computation.3 | async-start | bytes 4194304 | tf_op jit(solution)/shard_map/all_to_all | solution.py:247
  104.2 0.7 fusion.5
  104.9 0.8 pad_add_fusion.info
  105.7 48.5 %all-to-all-done.3 = f32[512,8,128]{2,1,0:T(8,128)S(1)} async-done(((f32[512,8,128]{2,1,0:T(8,128)}), f32[512,8,128]{2,1,0:T(8,128)S(1)}, u32[]{:S(2)}, u32[]{:S(2)}) %all-to-all-start.3) | async-done | bytes 2097184 | tf_op jit(solution)/shard_map/all_to_all | solution.py:247
  154.2 3.5 %settle.1 = f32[2,16,128,128]{3,2,1,0:T(8,128)} custom-call(s32[2]{0:T(128)S(1)} %pad_add_fusion.info, f32[32,16,8,128]{3,2,1,0:T(8,128)S(1)} %bitcast.24), custom_call_target="tpu_custom_call" | custom-call | flops 262144 | bytes 4194304 | tf_op jit(solution)/shard_map/settle/pallas_call | solution.py:196
  (3 shorter events, 0.0 us)
Async XLA Ops:
  0.0 23.2 %copy-start = (s32[6,16,16,3]{2,1,3,0:T(8,128)S(1)}, s32[6,16,16,3]{2,1,3,0:T(8,128)}, u32[]{:S(2)}) copy-start(s32[6,16,16,3]{2,1,3,0:T(8,128)} %param.7) | copy-start | bytes 55300
  0.0 20.3 %copy-start.3 = (s32[128]{0:T(128)S(1)}, s32[128]{0:T(128)}, u32[]{:S(2)}) copy-start(s32[128]{0:T(128)} %param.8) | copy-start | bytes 1540
  16.8 13.8 %all-to-all-start = ((f32[8,128,128]{2,1,0:T(8,128)}), f32[8,128,128]{2,1,0:T(8,128)S(1)}, u32[]{:S(2)}, u32[]{:S(2)}) async-start(f32[8,128,128]{2,1,0:T(8,128)} %get-tuple-element.6), calls=%async_computation | async-start | bytes 1048576 | tf_op jit(solution)/shard_map/all_to_all | solution.py:241
  51.3 13.3 %copy-start.2 = (s32[256]{0:T(256)S(1)}, s32[256]{0:T(256)}, u32[]{:S(2)}) copy-start(s32[256]{0:T(256)} %param.9) | copy-start | bytes 3076
  51.3 43.3 %all-to-all-start.2 = ((f32[256,8,128]{2,1,0:T(8,128)}), f32[256,8,128]{2,1,0:T(8,128)S(1)}, u32[]{:S(2)}, u32[]{:S(2)}) async-start(f32[256,8,128]{2,1,0:T(8,128)} %bitcast.10), calls=%async_computation.2 | async-start | bytes 2097152 | tf_op jit(solution)/shard_map/all_to_all | solution.py:245
  96.5 1.3 copy-start.1
  97.8 56.4 %all-to-all-start.3 = ((f32[512,8,128]{2,1,0:T(8,128)}), f32[512,8,128]{2,1,0:T(8,128)S(1)}, u32[]{:S(2)}, u32[]{:S(2)}) async-start(f32[512,8,128]{2,1,0:T(8,128)} %copy-done.1), calls=%async_computation.3 | async-start | bytes 4194304 | tf_op jit(solution)/shard_map/all_to_all | solution.py:247

commit v2 on v1

--- a/solution.py
+++ b/solution.py
@@ -16,47 +16,54 @@
     return high, (x - high.astype(F32)).astype(BF16)
 
 
-def ladder_body(
-    codes, info, even, odd, fac, out, f_pair, f_turn, amp_high, amp_low, prod, grouped
-):
+def split_body(info, fac, f_pair, f_turn):
+    slots, n = fac.shape[1], fac.shape[2]
+    for l in range(slots):
+        tile = fac[0, l]
+        rows = slice(l * n, (l + 1) * n)
+        f_pair[rows, :n], f_pair[rows, n:] = halves(tile)
+        f_turn[rows, :n], f_turn[rows, n:] = halves(tile.T)
+
+
+def split_factors(info, factors):
+    _, slots, n, _ = factors.shape
+    shape = jax.ShapeDtypeStruct((slots * n, 2 * n), BF16)
+    spec = pl.BlockSpec(shape.shape, lambda i, *_: (0, 0))
+    return pl.pallas_call(
+        split_body,
+        out_shape=[shape, shape],
+        grid_spec=pltpu.PrefetchScalarGridSpec(
+            num_scalar_prefetch=1,
+            grid=(1,),
+            in_specs=[pl.BlockSpec((1, slots, n, n), lambda i, info: (info[0], 0, 0, 0))],
+            out_specs=[spec, spec],
+        ),
+        compiler_params=pltpu.CompilerParams(vmem_limit_bytes=16 << 20),
+        cost_estimate=pl.CostEstimate(flops=1 << 20, bytes_accessed=3 << 20, transcendentals=0),
+        name="split_factors",
+    )(info, factors)
+
+
+def ladder_body(codes, info, amp, f_pair, f_turn, out, amp_high, amp_low, prod, grouped):
     slots, n, _ = out.shape
     mirrored = info[1]
 
-    def split_factor(l, c):
-        tile = fac[0, l]
-        rows = pl.ds(pl.multiple_of(l * n, n), n)
+    def put(s, tile):
+        v, i = s // 2, s % 2
         high, low = halves(tile)
-        f_pair[rows, :n] = high
-        f_pair[rows, n:] = low
-        high, low = halves(tile.T)
-        f_turn[rows, :n] = high
-        f_turn[rows, n:] = low
-        return c
-
-    lax.fori_loop(0, slots, split_factor, 0)
-
-    def put_amp(i, v, tile):
-        high, low = halves(tile)
-        amp_high[v, :, i * n : (i + 1) * n] = high
+        amp_high[v, :n, i * n : (i + 1) * n] = high
+        amp_high[v, n:, i * n : (i + 1) * n] = high
         amp_low[v, :, i * n : (i + 1) * n] = low
 
     @pl.when(mirrored == 0)
     def _():
-        def go(v, c):
-            put_amp(0, v, even[v])
-            put_amp(1, v, odd[v])
-            return c
-
-        lax.fori_loop(0, slots // 2, go, 0)
+        for s in range(slots):
+            put(s, amp[s])
 
     @pl.when(mirrored != 0)
     def _():
-        def go(v, c):
-            put_amp(0, v, even[v].T)
-            put_amp(1, v, odd[v].T)
-            return c
-
-        lax.fori_loop(0, slots // 2, go, 0)
+        for s in range(slots):
+            put(s, amp[s].T)
 
     def clear(r, c):
         grouped[r] = jnp.zeros(grouped.shape[1:], F32)
@@ -65,31 +72,22 @@
     lax.fori_loop(0, slots, clear, 0)
 
     def one_amp_pair(v, c):
-        high = amp_high[v]
         prod[...] = jnp.dot(
-            f_pair[...], jnp.concatenate([high, high], axis=0), preferred_element_type=F32
+            f_pair[...], amp_high[v], preferred_element_type=F32
         ) + jnp.dot(f_pair[:, :n], amp_low[v], preferred_element_type=F32)
         for i in range(2):
-
-            def entry(k, c):
+            for k in range(codes.shape[1]):
                 code = codes[2 * v + i, k]
-                o = code // 256
-                l = (code // 16) % 16
-                r = code % 16
-                to = pl.ds(pl.multiple_of(o * n, n), n)
-                grouped[r, to, :] += prod[
-                    pl.ds(pl.multiple_of(l * n, n), n), i * n : (i + 1) * n
-                ]
-                return c
-
-            lax.fori_loop(0, codes.shape[1], entry, 0, unroll=4)
+                to = pl.ds(pl.multiple_of((code >> 8) * n, n), n)
+                source = pl.ds(pl.multiple_of(((code >> 4) & 15) * n, n), n)
+                grouped[code & 15, to, :] += prod[source, i * n : (i + 1) * n]
         return c
 
     lax.fori_loop(0, slots // 2, one_amp_pair, 0)
 
-    step = 4
-
-    def one_out(g, c):
+    step = 8
+
+    def some_out(g, c):
         rows = pl.ds(pl.multiple_of(g * (step * n), step * n), step * n)
         parts = [halves(grouped[r, rows, :]) for r in range(slots)]
         high = jnp.concatenate([a for a, _ in parts], axis=1)
@@ -100,30 +98,24 @@
         out[pl.ds(g * step, step)] = total.reshape(step, n, n)
         return c
 
-    lax.fori_loop(0, slots // step, one_out, 0)
-
-
-def ladder(codes, info, even, odd, factors):
-    slots = 2 * even.shape[0]
-    n = even.shape[-1]
-    whole = pl.BlockSpec((slots // 2, n, n), lambda i, *_: (0, 0, 0))
+    lax.fori_loop(0, slots // step, some_out, 0)
+
+
+def ladder(codes, info, amp, f_pair, f_turn):
+    slots, n, _ = amp.shape
     wide = slots * n
+    whole = pl.BlockSpec((slots, n, n), lambda i, *_: (0, 0, 0))
+    table = pl.BlockSpec((wide, 2 * n), lambda i, *_: (0, 0))
     return pl.pallas_call(
         ladder_body,
         out_shape=jax.ShapeDtypeStruct((slots, n, n), F32),
         grid_spec=pltpu.PrefetchScalarGridSpec(
             num_scalar_prefetch=2,
             grid=(1,),
-            in_specs=[
-                whole,
-                whole,
-                pl.BlockSpec((1, slots, n, n), lambda i, codes, info: (info[0], 0, 0, 0)),
-            ],
-            out_specs=pl.BlockSpec((slots, n, n), lambda i, *_: (0, 0, 0)),
+            in_specs=[whole, table, table],
+            out_specs=whole,
             scratch_shapes=[
-                pltpu.VMEM((wide, 2 * n), BF16),
-                pltpu.VMEM((wide, 2 * n), BF16),
-                pltpu.VMEM((slots // 2, n, 2 * n), BF16),
+                pltpu.VMEM((slots // 2, 2 * n, 2 * n), BF16),
                 pltpu.VMEM((slots // 2, n, 2 * n), BF16),
                 pltpu.VMEM((wide, 2 * n), F32),
                 pltpu.VMEM((slots, wide, n), F32),
@@ -134,7 +126,7 @@
             flops=12 * wide * wide * n, bytes_accessed=4 << 20, transcendentals=0
         ),
         name="ladder",
-    )(codes, info, even, odd, factors)
+    )(codes, info, amp, f_pair, f_turn)
 
 
 def pairs_body(spot, blocks, out, *, per_home):
@@ -166,7 +158,7 @@
             in_specs=[pl.BlockSpec(blocks.shape, lambda i, *_: (0, 0, 0))],
             out_specs=pl.BlockSpec((own_slots,) + blocks.shape[1:], lambda i, *_: (0, 0, 0)),
         ),
-        compiler_params=pltpu.CompilerParams(vmem_limit_bytes=16 << 20),
+        compiler_params=pltpu.CompilerParams(vmem_limit_bytes=56 << 20),
         cost_estimate=pl.CostEstimate(flops=1 << 18, bytes_accessed=3 << 20, transcendentals=0),
         name="join_pairs",
     )(spot, blocks)
@@ -238,17 +230,22 @@
     )
     spot = owner_map * own_most + jnp.sum(same.astype(jnp.int32), axis=1)
 
-    even = lax.all_to_all(amplitudes[0], "virt", split_axis=0, concat_axis=0, tiled=True)
-    odd = lax.all_to_all(amplitudes[1], "virt", split_axis=0, concat_axis=0, tiled=True)
-    result = ladder(codes, info, even, odd, factors)
+    plain = jnp.sum((owner_map[:half] == my_pair).astype(jnp.int32))
+    swap = (my_virt * local_slots < OFF_DIAG).astype(jnp.int32)
+    settle_info = jnp.stack([plain, swap])
+
+    amp = lax.all_to_all(amplitudes, "virt", split_axis=1, concat_axis=0, tiled=True)
+    f_pair, f_turn = split_factors(info, factors)
+    amp, codes, info, f_pair, f_turn, spot, settle_info = lax.optimization_barrier(
+        (amp, codes, info, f_pair, f_turn, spot, settle_info)
+    )
+    result = ladder(codes, info, amp.reshape(-1, n, n), f_pair, f_turn)
     sheets = result.reshape(virt_count * pair_count, -1, n)
     spread = lax.all_to_all(sheets, ("virt", "pair"), split_axis=0, concat_axis=0, tiled=True)
     joined = join_pairs(spot, spread, pair_count * own_most, per_home)
     arrived = lax.all_to_all(joined, "pair", split_axis=0, concat_axis=0, tiled=True)
-    plain = jnp.sum((owner_map[:half] == my_pair).astype(jnp.int32))
-    swap = (my_virt * local_slots < OFF_DIAG).astype(jnp.int32)
     return settle(
-        jnp.stack([plain, swap]),
+        settle_info,
         arrived.reshape(pair_count, own_most, -1, n),
         own_most,
         local_slots,

time: 158 us -> 145 us (0.918)
  blocking collectives: 14.7 us -> 99.1 us
  waiting for transfers between devices: 85.7 us -> 7.13 us
  starting transfers between devices: 23.2 us -> 4.47 us
  Pallas kernels: 26.1 us -> 23.5 us
  local copies, waits for them, and re-layouts: 4.05 us -> 5.76 us
    all_to_all x1 -> x2, blocking collectives: 14.7 us -> 99.1 us  [the longest x1 56.4 us: on_device(): lax.all_to_all(joined, 'pair', split_axis=0, concat_axis=0, tiled=True)]
    all_to_all x3 -> x1, waiting for transfers between devices: 85.7 us -> 7.13 us  [on_device(): lax.all_to_all(amplitudes, 'virt', split_axis=1, concat_axis=0, tiled=True)]
    all_to_all x3 -> x1, starting transfers between devices: 23.2 us -> 4.47 us  [on_device(): lax.all_to_all(amplitudes, 'virt', split_axis=1, concat_axis=0, tiled=True)]
    pallas_call x1, Pallas kernels: 20.7 us -> 14.5 us  [ladder(): pl.pallas_call(ladder_body, out_shape=jax.ShapeDtypeStruct((slots, n, n),...]
    unnamed x8 -> x9, local copies, waits for them, and re-layouts: 1.33 us -> 5.13 us
    pallas_call x1, Pallas kernels: 1.88 us -> 4.57 us  [join_pairs(): pl.pallas_call(body, out_shape=jax.ShapeDtypeStruct((own_slots,) + blocks...]
    squeeze x1 -> x0, local copies, waits for them, and re-layouts: 2.14 us -> none  [on_device(): amplitudes[1]]
  transfers between devices with their start and end apart: 3 -> 1, of which waited for: 3 -> 1; matrix products, arithmetic and copies ran while one was open for 2% -> 2% of each run, Pallas kernels for 0% -> 1%
where the time goes in v2:
time: 145 us
  blocking collectives  99.1 us (68%)
  Pallas kernels  23.5 us (16%)
  waiting for transfers between devices  7.13 us (5%)
  local copies, waits for them, and re-layouts  5.76 us (4%)
  starting transfers between devices  4.47 us (3%)
  other arithmetic  2.64 us (2%)
  between operations  1.88 us (1%)
    all_to_all x1, blocking collectives, on_device(): lax.all_to_all(joined, 'pair', split_axis=0, concat_axis=0, tiled=True)  56.4 us
    all_to_all x1, blocking collectives, on_device(): lax.all_to_all(sheets, ('virt', 'pair'), split_axis=0, concat_axis=0, til...  42.7 us
    pallas_call x1, Pallas kernels, ladder(): pl.pallas_call(ladder_body, out_shape=jax.ShapeDtypeStruct((slots, n, n),...  14.5 us
    all_to_all x1, waiting for transfers between devices, on_device(): lax.all_to_all(amplitudes, 'virt', split_axis=1, concat_axis=0, tiled=True)  7.13 us
    unnamed x9, local copies, waits for them, and re-layouts  5.13 us
    pallas_call x1, Pallas kernels, join_pairs(): pl.pallas_call(body, out_shape=jax.ShapeDtypeStruct((own_slots,) + blocks...  4.57 us
    all_to_all x1, starting transfers between devices, on_device(): lax.all_to_all(amplitudes, 'virt', split_axis=1, concat_axis=0, tiled=True)  4.47 us
    pallas_call x1, Pallas kernels, settle(): pl.pallas_call(body, out_shape=jax.ShapeDtypeStruct((local_slots, own_mos...  3.54 us
  transfers between devices with their start and end apart: 1, of which 1 were waited for; matrix products, arithmetic and copies ran while one was open for 2% of the time, Pallas kernels for 1%

profile of v2, /device:TPU:2, one launch (start us, length us, event | category | flops | bytes accessed | tf_op | source)
XLA Modules:
  0.0 144.5 jit_solution(16760486355387294605)
XLA Ops:
  0.0 0.0 copy-start
  0.0 0.0 copy-start.3
  0.0 0.0 copy-start.2
  0.0 2.3 %copy.8 = f32[2,8,128,128]{3,2,0,1:T(8,128)} copy(f32[2,8,128,128]{3,2,1,0:T(8,128)} %param.5) | data formatting | bytes 2097152 | tf_op args[0]
  2.3 4.5 %all-to-all-start = ((f32[2,8,128,128]{3,2,0,1:T(8,128)}), f32[2,8,128,128]{3,2,0,1:T(8,128)S(1)}, u32[]{:S(2)}, u32[]{:S(2)}) async-start(f32[2,8,128,128]{3,2,0,1:T(8,128)} %copy.8), calls=%async_computation | async-start | bytes 2097152 | tf_op jit(solution)/shard_map/all_to_all | solution.py:237
  6.8 0.0 copy-done.3
  6.8 0.6 dynamic_slice.6
  9.3 0.0 copy-done.2
  9.3 0.6 fusion.5
  9.9 1.2 pad_add_fusion
  11.1 0.0 copy-start.1
  11.1 2.8 %copy-done.1 = f32[6,16,128,128]{3,2,1,0:T(8,128)S(1)} copy-done((f32[6,16,128,128]{3,2,1,0:T(8,128)S(1)}, f32[6,16,128,128]{3,2,1,0:T(8,128)}, u32[]{:S(2)}) %copy-start.1) | copy-done | bytes 6291480
  13.9 0.9 split_factors.1
  14.8 0.0 copy-done
  14.9 0.2 convert_reduce_fusion
  15.0 0.6 multiply_add_fusion.spot
  15.6 7.1 %all-to-all-done = f32[2,8,128,128]{3,2,0,1:T(8,128)S(1)} async-done(((f32[2,8,128,128]{3,2,0,1:T(8,128)}), f32[2,8,128,128]{3,2,0,1:T(8,128)S(1)}, u32[]{:S(2)}, u32[]{:S(2)}) %all-to-all-start) | async-done | bytes 1048608 | tf_op jit(solution)/shard_map/all_to_all | solution.py:237
  22.8 14.5 %ladder.1 = f32[16,128,128]{2,1,0:T(8,128)S(1)} custom-call(s32[16,16]{1,0:T(8,128)S(1)} %fusion.4.codes, s32[2]{0:T(128)S(1)} %get-tuple-element.19.info, f32[16,128,128]{2,1,0:T(8,128)S(1)} %bitcast.27, bf16[2048,256]{1,0:T(8,128)(2,1)S(1)} %get-tuple-element.21.f_pair, bf16[2048,256]{1,0:T(8,128)(2,1)S(1)} %get-tuple-element.22.f_turn), custom_call_target="tpu_custom_call" | custom-call | flops 6442450944 | bytes 4194304 | tf_op jit(solution)/shard_map/ladder/pallas_call | solution.py:109
  37.3 42.7 %all_to_all.28.blocks = f32[256,8,128]{2,1,0:T(8,128)} all-to-all(f32[256,8,128]{2,1,0:T(8,128)S(1)} %bitcast.28), channel_id=1, replica_groups=mesh['pair'=32,'virt'=8] {'virt','pair'}, dimensions={0} | all-to-all | bytes 2097152 | tf_op jit(solution)/shard_map/all_to_all | solution.py:244
  80.0 4.6 %join_pairs.1 = f32[512,8,128]{2,1,0:T(8,128)} custom-call(s32[256]{0:T(256)} %multiply_add_fusion.spot, f32[256,8,128]{2,1,0:T(8,128)} %all_to_all.28.blocks), custom_call_target="tpu_custom_call" | custom-call | flops 262144 | bytes 3145728 | tf_op jit(solution)/shard_map/join_pairs/pallas_call | solution.py:152
  84.6 56.4 %all_to_all.29 = f32[512,8,128]{2,1,0:T(8,128)S(1)} all-to-all(f32[512,8,128]{2,1,0:T(8,128)} %join_pairs.1), channel_id=1, replica_groups=mesh['pair'=32,'virt'=8] {'pair'}, dimensions={0} | all-to-all | bytes 4194304 | tf_op jit(solution)/shard_map/all_to_all | solution.py:246
  141.0 3.5 %settle.1 = f32[2,16,128,128]{3,2,1,0:T(8,128)} custom-call(s32[2]{0:T(128)S(1)} %get-tuple-element.16.info, f32[32,16,8,128]{3,2,1,0:T(8,128)S(1)} %bitcast.26), custom_call_target="tpu_custom_call" | custom-call | flops 262144 | bytes 4194304 | tf_op jit(solution)/shard_map/settle/pallas_call | solution.py:188
  (2 shorter events, 0.0 us)
Async XLA Ops:
  0.0 14.8 %copy-start = (s32[6,16,16,3]{2,1,3,0:T(8,128)S(1)}, s32[6,16,16,3]{2,1,3,0:T(8,128)}, u32[]{:S(2)}) copy-start(s32[6,16,16,3]{2,1,3,0:T(8,128)} %param.7) | copy-start | bytes 55300
  0.0 6.8 %copy-start.3 = (s32[128]{0:T(128)S(1)}, s32[128]{0:T(128)}, u32[]{:S(2)}) copy-start(s32[128]{0:T(128)} %param.8) | copy-start | bytes 1540
  0.0 9.3 %copy-start.2 = (s32[256]{0:T(256)S(1)}, s32[256]{0:T(256)}, u32[]{:S(2)}) copy-start(s32[256]{0:T(256)} %param.9) | copy-start | bytes 3076
  2.3 20.4 %all-to-all-start = ((f32[2,8,128,128]{3,2,0,1:T(8,128)}), f32[2,8,128,128]{3,2,0,1:T(8,128)S(1)}, u32[]{:S(2)}, u32[]{:S(2)}) async-start(f32[2,8,128,128]{3,2,0,1:T(8,128)} %copy.8), calls=%async_computation | async-start | bytes 2097152 | tf_op jit(solution)/shard_map/all_to_all | solution.py:237
  11.1 2.8 %copy-start.1 = (f32[6,16,128,128]{3,2,1,0:T(8,128)S(1)}, f32[6,16,128,128]{3,2,1,0:T(8,128)}, u32[]{:S(2)}) copy-start(f32[6,16,128,128]{3,2,1,0:T(8,128)} %fac.1) | copy-start | bytes 18874372

commit v3 on v2

--- a/solution.py
+++ b/solution.py
@@ -1,3 +1,5 @@
+import functools
+
 import jax
 import jax.numpy as jnp
 from jax import lax
@@ -9,6 +11,7 @@
 OFF_DIAG = DOM * (DOM - 1)
 F32 = jnp.float32
 BF16 = jnp.bfloat16
+FIRST = 1 << 12
 
 
 def halves(x):
@@ -44,8 +47,11 @@
     )(info, factors)
 
 
-def ladder_body(codes, info, amp, f_pair, f_turn, out, amp_high, amp_low, prod, grouped):
+def ladder_body(
+    codes, touched, info, amp, f_pair, f_turn, out, amp_high, amp_low, prod_a, prod_b, grouped
+):
     slots, n, _ = out.shape
+    entries = codes.shape[1]
     mirrored = info[1]
 
     def put(s, tile):
@@ -65,43 +71,69 @@
         for s in range(slots):
             put(s, amp[s].T)
 
-    def clear(r, c):
-        grouped[r] = jnp.zeros(grouped.shape[1:], F32)
+    chunks = 4
+    height = slots * n // chunks
+    per = 2 * entries // chunks
+
+    def product(v, prod, q):
+        rows = slice(q * height, (q + 1) * height)
+        prod[rows] = jnp.dot(
+            f_pair[rows], amp_high[v], preferred_element_type=F32
+        ) + jnp.dot(f_pair[rows, :n], amp_low[v], preferred_element_type=F32)
+
+    def collect(v, prod, q):
+        for e in range(q * per, (q + 1) * per):
+            i, k = e // entries, e % entries
+            code = codes[2 * v + i, k]
+            to = pl.ds(pl.multiple_of(((code >> 8) & 15) * n, n), n)
+            source = pl.ds(pl.multiple_of(((code >> 4) & 15) * n, n), n)
+            new = prod[source, i * n : (i + 1) * n]
+            r = code & 15
+            grouped[r, to, :] = jnp.where(code >= FIRST, new, grouped[r, to, :] + new)
+
+    for q in range(chunks):
+        product(0, prod_a, q)
+
+    def two(w, c):
+        v = 2 * w
+        for q in range(chunks):
+            product(v + 1, prod_b, q)
+            collect(v, prod_a, q)
+        for q in range(chunks):
+            product(v + 2, prod_a, q)
+            collect(v + 1, prod_b, q)
         return c
 
-    lax.fori_loop(0, slots, clear, 0)
-
-    def one_amp_pair(v, c):
-        prod[...] = jnp.dot(
-            f_pair[...], amp_high[v], preferred_element_type=F32
-        ) + jnp.dot(f_pair[:, :n], amp_low[v], preferred_element_type=F32)
-        for i in range(2):
-            for k in range(codes.shape[1]):
-                code = codes[2 * v + i, k]
-                to = pl.ds(pl.multiple_of((code >> 8) * n, n), n)
-                source = pl.ds(pl.multiple_of(((code >> 4) & 15) * n, n), n)
-                grouped[code & 15, to, :] += prod[source, i * n : (i + 1) * n]
-        return c
-
-    lax.fori_loop(0, slots // 2, one_amp_pair, 0)
-
-    step = 8
-
-    def some_out(g, c):
-        rows = pl.ds(pl.multiple_of(g * (step * n), step * n), step * n)
-        parts = [halves(grouped[r, rows, :]) for r in range(slots)]
+    lax.fori_loop(0, slots // 4 - 1, two, 0)
+    last = slots // 2 - 1
+    for q in range(chunks):
+        product(last, prod_b, q)
+        collect(last - 1, prod_a, q)
+    for q in range(chunks):
+        collect(last, prod_b, q)
+
+    step = 4
+    for g in range(0, slots, step):
+
+        def block(r):
+            return jnp.concatenate(
+                [
+                    jnp.where(touched[o, r] > 0, grouped[r, o * n : (o + 1) * n, :], 0.0)
+                    for o in range(g, g + step)
+                ],
+                axis=0,
+            )
+
+        parts = [halves(block(r)) for r in range(slots)]
         high = jnp.concatenate([a for a, _ in parts], axis=1)
         low = jnp.concatenate([b for _, b in parts], axis=1)
         both = jnp.dot(high, f_turn[...], preferred_element_type=F32)
         rest = jnp.dot(low, f_turn[:, :n], preferred_element_type=F32)
         total = both[:, :n] + both[:, n:] + rest
-        out[pl.ds(g * step, step)] = total.reshape(step, n, n)
-        return c
-
-    lax.fori_loop(0, slots // step, some_out, 0)
-
-
-def ladder(codes, info, amp, f_pair, f_turn):
+        out[g : g + step] = total.reshape(step, n, n)
+
+
+def ladder(codes, touched, info, amp, f_pair, f_turn):
     slots, n, _ = amp.shape
     wide = slots * n
     whole = pl.BlockSpec((slots, n, n), lambda i, *_: (0, 0, 0))
@@ -110,7 +142,7 @@
         ladder_body,
         out_shape=jax.ShapeDtypeStruct((slots, n, n), F32),
         grid_spec=pltpu.PrefetchScalarGridSpec(
-            num_scalar_prefetch=2,
+            num_scalar_prefetch=3,
             grid=(1,),
             in_specs=[whole, table, table],
             out_specs=whole,
@@ -118,6 +150,7 @@
                 pltpu.VMEM((slots // 2, 2 * n, 2 * n), BF16),
                 pltpu.VMEM((slots // 2, n, 2 * n), BF16),
                 pltpu.VMEM((wide, 2 * n), F32),
+                pltpu.VMEM((wide, 2 * n), F32),
                 pltpu.VMEM((slots, wide, n), F32),
             ],
         ),
@@ -126,7 +159,7 @@
             flops=12 * wide * wide * n, bytes_accessed=4 << 20, transcendentals=0
         ),
         name="ladder",
-    )(codes, info, amp, f_pair, f_turn)
+    )(codes, touched, info, amp, f_pair, f_turn)
 
 
 def pairs_body(spot, blocks, out, *, per_home):
@@ -158,7 +191,7 @@
             in_specs=[pl.BlockSpec(blocks.shape, lambda i, *_: (0, 0, 0))],
             out_specs=pl.BlockSpec((own_slots,) + blocks.shape[1:], lambda i, *_: (0, 0, 0)),
         ),
-        compiler_params=pltpu.CompilerParams(vmem_limit_bytes=56 << 20),
+        compiler_params=pltpu.CompilerParams(vmem_limit_bytes=16 << 20),
         cost_estimate=pl.CostEstimate(flops=1 << 18, bytes_accessed=3 << 20, transcendentals=0),
         name="join_pairs",
     )(spot, blocks)
@@ -171,19 +204,32 @@
     def body(info, src, out):
         plain = info[0]
         swap = info[1]
-        for g in range(group):
-            k = pl.program_id(0) * group + g
-
-            @pl.when(k < plain)
-            def _():
-                for i in range(local_slots):
-                    out[i, g] = src[i * per : (i + 1) * per, g].reshape(n, n)
-
-            @pl.when(k >= plain)
-            def _():
-                for i in range(local_slots):
-                    base = jnp.where(swap != 0, local_slots - 1 - i, i) * per
-                    out[i, g] = src[pl.ds(base, per), g].reshape(n, n).T
+        first = pl.program_id(0) * group
+
+        def as_is(g):
+            for i in range(local_slots):
+                out[i, g] = src[i * per : (i + 1) * per, g].reshape(n, n)
+
+        def turned(g):
+            for i in range(local_slots):
+                base = jnp.where(swap != 0, local_slots - 1 - i, i) * per
+                out[i, g] = src[pl.ds(base, per), g].reshape(n, n).T
+
+        @pl.when(first + group <= plain)
+        def _():
+            for g in range(group):
+                as_is(g)
+
+        @pl.when(first >= plain)
+        def _():
+            for g in range(group):
+                turned(g)
+
+        @pl.when((first < plain) & (first + group > plain))
+        def _():
+            for g in range(group):
+                pl.when(first + g < plain)(functools.partial(as_is, g))
+                pl.when(first + g >= plain)(functools.partial(turned, g))
 
     return pl.pallas_call(
         body,
@@ -224,6 +270,13 @@
         mirrored != 0, partner * 256 + right * 16 + left, o * 256 + left * 16 + right
     )
     info = jnp.stack([region, mirrored])
+    group = ((codes >> 8) * 16 + (codes & 15)).reshape(-1)
+    place = jnp.arange(group.shape[0])
+    met = (group[:, None] == group[None, :]) & (place[None, :] < place[:, None])
+    codes = codes + jnp.where(jnp.any(met, axis=1), 0, FIRST).reshape(codes.shape)
+    slot_total = codes.shape[0]
+    touched = jnp.any(group[None, :] == jnp.arange(slot_total * 16)[:, None], axis=1)
+    touched = touched.astype(jnp.int32).reshape(slot_total, 16)
 
     same = (owner_map[:, None] == owner_map[None, :]) & (
         jnp.arange(pair_total)[None, :] < jnp.arange(pair_total)[:, None]
@@ -236,10 +289,10 @@
 
     amp = lax.all_to_all(amplitudes, "virt", split_axis=1, concat_axis=0, tiled=True)
     f_pair, f_turn = split_factors(info, factors)
-    amp, codes, info, f_pair, f_turn, spot, settle_info = lax.optimization_barrier(
-        (amp, codes, info, f_pair, f_turn, spot, settle_info)
-    )
-    result = ladder(codes, info, amp.reshape(-1, n, n), f_pair, f_turn)
+    amp, codes, touched, info, f_pair, f_turn, spot, settle_info = lax.optimization_barrier(
+        (amp, codes, touched, info, f_pair, f_turn, spot, settle_info)
+    )
+    result = ladder(codes, touched, info, amp.reshape(-1, n, n), f_pair, f_turn)
     sheets = result.reshape(virt_count * pair_count, -1, n)
     spread = lax.all_to_all(sheets, ("virt", "pair"), split_axis=0, concat_axis=0, tiled=True)
     joined = join_pairs(spot, spread, pair_count * own_most, per_home)

time: 145 us -> 139 us (0.959)
  Pallas kernels: 23.5 us -> 17.8 us
    pallas_call x1, Pallas kernels: 4.57 us -> 1.88 us  [join_pairs(): pl.pallas_call(body, out_shape=jax.ShapeDtypeStruct((own_slots,) + blocks...]
    pallas_call x1, Pallas kernels: 14.5 us -> 12.1 us  [ladder(): pl.pallas_call(ladder_body, out_shape=jax.ShapeDtypeStruct((slots, n, n),...]
where the time goes in v3:
time: 139 us; the launch traced here: 138 us
  blocking collectives  98.7 us (71%)
  Pallas kernels  17.8 us (13%)
  waiting for transfers between devices  7.14 us (5%)
  local copies, waits for them, and re-layouts  6.12 us (4%)
  starting transfers between devices  4.47 us (3%)
  other arithmetic  2.39 us (2%)
  between operations  1.77 us (1%)
    all_to_all x1, blocking collectives, on_device(): lax.all_to_all(joined, 'pair', split_axis=0, concat_axis=0, tiled=True)  56.1 us
    all_to_all x1, blocking collectives, on_device(): lax.all_to_all(sheets, ('virt', 'pair'), split_axis=0, concat_axis=0, til...  42.6 us
    pallas_call x1, Pallas kernels, ladder(): pl.pallas_call(ladder_body, out_shape=jax.ShapeDtypeStruct((slots, n, n),...  12.1 us
    all_to_all x1, waiting for transfers between devices, on_device(): lax.all_to_all(amplitudes, 'virt', split_axis=1, concat_axis=0, tiled=True)  7.14 us
    unnamed x9, local copies, waits for them, and re-layouts  5.14 us
    all_to_all x1, starting transfers between devices, on_device(): lax.all_to_all(amplitudes, 'virt', split_axis=1, concat_axis=0, tiled=True)  4.47 us
    pallas_call x1, Pallas kernels, settle(): pl.pallas_call(body, out_shape=jax.ShapeDtypeStruct((local_slots, own_mos...  2.92 us
  transfers between devices with their start and end apart: 1, of which 1 were waited for; matrix products, arithmetic and copies ran while one was open for 2% of the time, Pallas kernels for 1%

profile of v3, /device:TPU:2, one launch (start us, length us, event | category | flops | bytes accessed | tf_op | source)
XLA Modules:
  0.0 138.5 jit_solution(3374885684008888907)
XLA Ops:
  0.0 0.0 copy-start
  0.0 0.0 copy-start.3
  0.0 0.0 copy-start.2
  0.0 2.3 %copy.8 = f32[2,8,128,128]{3,2,0,1:T(8,128)} copy(f32[2,8,128,128]{3,2,1,0:T(8,128)} %param.5) | data formatting | bytes 2097152 | tf_op args[0]
  2.4 4.5 %all-to-all-start = ((f32[2,8,128,128]{3,2,0,1:T(8,128)}), f32[2,8,128,128]{3,2,0,1:T(8,128)S(1)}, u32[]{:S(2)}, u32[]{:S(2)}) async-start(f32[2,8,128,128]{3,2,0,1:T(8,128)} %copy.8), calls=%async_computation | async-start | bytes 2097152 | tf_op jit(solution)/shard_map/all_to_all | solution.py:290
  6.8 0.0 copy-done.3
  6.8 0.6 dynamic_slice.6
  9.1 0.0 copy-done
  9.1 0.1 squeeze.26
  9.2 0.1 squeeze.28
  9.3 0.1 squeeze.27
  9.4 0.2 fusion.3
  9.6 0.1 select_n.65
  9.7 0.1 reshape.109.touched
  9.8 0.0 copy-done.2
  9.8 0.7 fusion.15
  10.5 1.3 pad_add_fusion
  11.7 0.0 copy-start.1
  11.7 2.8 %copy-done.1 = f32[6,16,128,128]{3,2,1,0:T(8,128)S(1)} copy-done((f32[6,16,128,128]{3,2,1,0:T(8,128)S(1)}, f32[6,16,128,128]{3,2,1,0:T(8,128)}, u32[]{:S(2)}) %copy-start.1) | copy-done | bytes 6291480
  14.5 0.9 split_factors.1
  15.4 0.2 convert_reduce_fusion
  15.6 7.1 %all-to-all-done = f32[2,8,128,128]{3,2,0,1:T(8,128)S(1)} async-done(((f32[2,8,128,128]{3,2,0,1:T(8,128)}), f32[2,8,128,128]{3,2,0,1:T(8,128)S(1)}, u32[]{:S(2)}, u32[]{:S(2)}) %all-to-all-start) | async-done | bytes 1048608 | tf_op jit(solution)/shard_map/all_to_all | solution.py:290
  22.8 12.1 %ladder.1 = f32[16,128,128]{2,1,0:T(8,128)S(1)} custom-call(s32[16,16]{1,0:T(8,128)S(1)} %fusion.8.codes, s32[16,16]{1,0:T(8,128)S(1)} %reshape.109.touched, s32[2]{0:T(128)S(1)} %get-tuple-element.21.info, f32[16,128,128]{2,1,0:T(8,128)S(1)} %bitcast.40, bf16[2048,256]{1,0:T(8,128)(2,1)S(1)} %get-tuple-element.23.f_pair, ...), custom_call_target="tpu_custom_call" | custom-call | flops 6442450944 | bytes 4194304 | tf_op jit(solution)/shard_map/ladder/pallas_call | solution.py:141
  34.9 42.6 %all_to_all.28.blocks = f32[256,8,128]{2,1,0:T(8,128)S(1)} all-to-all(f32[256,8,128]{2,1,0:T(8,128)S(1)} %bitcast.41), channel_id=1, replica_groups=mesh['pair'=32,'virt'=8] {'virt','pair'}, dimensions={0} | all-to-all | bytes 2097152 | tf_op jit(solution)/shard_map/all_to_all | solution.py:297
  77.5 1.9 %join_pairs.1 = f32[512,8,128]{2,1,0:T(8,128)S(1)} custom-call(s32[256]{0:T(256)S(1)} %multiply_add_fusion.spot, f32[256,8,128]{2,1,0:T(8,128)S(1)} %all_to_all.28.blocks), custom_call_target="tpu_custom_call" | custom-call | flops 262144 | bytes 3145728 | tf_op jit(solution)/shard_map/join_pairs/pallas_call | solution.py:185
  79.4 56.1 %all_to_all.29 = f32[512,8,128]{2,1,0:T(8,128)S(1)} all-to-all(f32[512,8,128]{2,1,0:T(8,128)S(1)} %join_pairs.1), channel_id=1, replica_groups=mesh['pair'=32,'virt'=8] {'pair'}, dimensions={0} | all-to-all | bytes 4194304 | tf_op jit(solution)/shard_map/all_to_all | solution.py:299
  135.5 2.9 %settle.1 = f32[2,16,128,128]{3,2,1,0:T(8,128)} custom-call(s32[2]{0:T(128)S(1)} %get-tuple-element.17.info, f32[32,16,8,128]{3,2,1,0:T(8,128)S(1)} %bitcast.39), custom_call_target="tpu_custom_call" | custom-call | flops 262144 | bytes 4194304 | tf_op jit(solution)/shard_map/settle/pallas_call | solution.py:234
  (7 shorter events, 0.1 us)
Async XLA Ops:
  0.0 9.1 %copy-start = (s32[6,16,16,3]{2,1,3,0:T(8,128)S(1)}, s32[6,16,16,3]{2,1,3,0:T(8,128)}, u32[]{:S(2)}) copy-start(s32[6,16,16,3]{2,1,3,0:T(8,128)} %param.7) | copy-start | bytes 55300
  0.0 6.8 %copy-start.3 = (s32[128]{0:T(128)S(1)}, s32[128]{0:T(128)}, u32[]{:S(2)}) copy-start(s32[128]{0:T(128)} %param.8) | copy-start | bytes 1540
  0.0 9.8 %copy-start.2 = (s32[256]{0:T(256)S(1)}, s32[256]{0:T(256)}, u32[]{:S(2)}) copy-start(s32[256]{0:T(256)} %param.9) | copy-start | bytes 3076
  2.4 20.4 %all-to-all-start = ((f32[2,8,128,128]{3,2,0,1:T(8,128)}), f32[2,8,128,128]{3,2,0,1:T(8,128)S(1)}, u32[]{:S(2)}, u32[]{:S(2)}) async-start(f32[2,8,128,128]{3,2,0,1:T(8,128)} %copy.8), calls=%async_computation | async-start | bytes 2097152 | tf_op jit(solution)/shard_map/all_to_all | solution.py:290
  11.7 2.8 %copy-start.1 = (f32[6,16,128,128]{3,2,1,0:T(8,128)S(1)}, f32[6,16,128,128]{3,2,1,0:T(8,128)}, u32[]{:S(2)}) copy-start(f32[6,16,128,128]{3,2,1,0:T(8,128)} %fac.1) | copy-start | bytes 18874372

commit v4 on v3

--- a/solution.py
+++ b/solution.py
@@ -48,11 +48,27 @@
 
 
 def ladder_body(
-    codes, touched, info, amp, f_pair, f_turn, out, amp_high, amp_low, prod_a, prod_b, grouped
+    codes,
+    touched,
+    info,
+    amp,
+    f_pair,
+    turn_source,
+    out,
+    amp_high,
+    amp_low,
+    prod_a,
+    prod_b,
+    grouped,
+    f_turn,
+    piece,
+    sems,
 ):
     slots, n, _ = out.shape
     entries = codes.shape[1]
     mirrored = info[1]
+    fetch = pltpu.make_async_copy(turn_source, f_turn, sems.at[0])
+    fetch.start()
 
     def put(s, tile):
         v, i = s // 2, s % 2
@@ -112,7 +128,9 @@
     for q in range(chunks):
         collect(last, prod_b, q)
 
-    step = 4
+    fetch.wait()
+    step = slots // piece.shape[0]
+    copies = []
     for g in range(0, slots, step):
 
         def block(r):
@@ -130,7 +148,13 @@
         both = jnp.dot(high, f_turn[...], preferred_element_type=F32)
         rest = jnp.dot(low, f_turn[:, :n], preferred_element_type=F32)
         total = both[:, :n] + both[:, n:] + rest
-        out[g : g + step] = total.reshape(step, n, n)
+        at = g // step
+        piece[at] = total.reshape(step, n, n)
+        copy = pltpu.make_async_copy(piece.at[at], out.at[pl.ds(g, step)], sems.at[1 + at])
+        copy.start()
+        copies.append(copy)
+    for copy in copies:
+        copy.wait()
 
 
 def ladder(codes, touched, info, amp, f_pair, f_turn):
@@ -144,14 +168,17 @@
         grid_spec=pltpu.PrefetchScalarGridSpec(
             num_scalar_prefetch=3,
             grid=(1,),
-            in_specs=[whole, table, table],
-            out_specs=whole,
+            in_specs=[whole, table, pl.BlockSpec(memory_space=pl.ANY)],
+            out_specs=pl.BlockSpec(memory_space=pl.ANY),
             scratch_shapes=[
                 pltpu.VMEM((slots // 2, 2 * n, 2 * n), BF16),
                 pltpu.VMEM((slots // 2, n, 2 * n), BF16),
                 pltpu.VMEM((wide, 2 * n), F32),
                 pltpu.VMEM((wide, 2 * n), F32),
                 pltpu.VMEM((slots, wide, n), F32),
+                pltpu.VMEM((wide, 2 * n), BF16),
+                pltpu.VMEM((4, slots // 4, n, n), F32),
+                pltpu.SemaphoreType.DMA((5,)),
             ],
         ),
         compiler_params=pltpu.CompilerParams(vmem_limit_bytes=48 << 20),
@@ -168,14 +195,16 @@
     half = count // 2
     out[...] = jnp.zeros(out.shape, F32)
 
-    def one(q, c):
-        row = (q % per_home) * homes + q // per_home
-        value = blocks[row] + blocks[row + homes // 2]
-        out[spot[q]] = value
-        out[spot[q + half]] = value
+    def home(h, c):
+        for v in range(per_home):
+            row = v * homes + h
+            q = h * per_home + v
+            value = blocks[row] + blocks[row + homes // 2]
+            out[spot[q]] = value
+            out[spot[q + half]] = value
         return c
 
-    lax.fori_loop(0, half, one, 0, unroll=4)
+    lax.fori_loop(0, homes // 2, home, 0)
 
 
 def join_pairs(spot, blocks, own_slots, per_home):
@@ -303,7 +332,7 @@
         own_most,
         local_slots,
         n,
-        4,
+        8,
     )
 
 

time: 139 us -> 138 us (level)
  no operation moved by 1% of the time
where the time goes in v4:
time: 138 us; the launch traced here: 137 us
  blocking collectives  98.7 us (72%)
  Pallas kernels  16.8 us (12%)
  waiting for transfers between devices  7.14 us (5%)
  local copies, waits for them, and re-layouts  6.12 us (4%)
  starting transfers between devices  4.47 us (3%)
  other arithmetic  2.39 us (2%)
  between operations  1.78 us (1%)
    all_to_all x1, blocking collectives, on_device(): lax.all_to_all(joined, 'pair', split_axis=0, concat_axis=0, tiled=True)  56.1 us
    all_to_all x1, blocking collectives, on_device(): lax.all_to_all(sheets, ('virt', 'pair'), split_axis=0, concat_axis=0, til...  42.6 us
    pallas_call x1, Pallas kernels, ladder(): pl.pallas_call(ladder_body, out_shape=jax.ShapeDtypeStruct((slots, n, n),...  12.8 us
    all_to_all x1, waiting for transfers between devices, on_device(): lax.all_to_all(amplitudes, 'virt', split_axis=1, concat_axis=0, tiled=True)  7.14 us
    unnamed x9, local copies, waits for them, and re-layouts  5.14 us
    all_to_all x1, starting transfers between devices, on_device(): lax.all_to_all(amplitudes, 'virt', split_axis=1, concat_axis=0, tiled=True)  4.47 us
  transfers between devices with their start and end apart: 1, of which 1 were waited for; matrix products, arithmetic and copies ran while one was open for 2% of the time, Pallas kernels for 1%

profile of v4, /device:TPU:2, one launch (start us, length us, event | category | flops | bytes accessed | tf_op | source)
XLA Modules:
  0.0 137.5 jit_solution(10387656794063047004)
XLA Ops:
  0.0 0.0 copy-start
  0.0 0.0 copy-start.3
  0.0 0.0 copy-start.2
  0.0 2.3 %copy.8 = f32[2,8,128,128]{3,2,0,1:T(8,128)} copy(f32[2,8,128,128]{3,2,1,0:T(8,128)} %param.5) | data formatting | bytes 2097152 | tf_op args[0]
  2.4 4.5 %all-to-all-start = ((f32[2,8,128,128]{3,2,0,1:T(8,128)}), f32[2,8,128,128]{3,2,0,1:T(8,128)S(1)}, u32[]{:S(2)}, u32[]{:S(2)}) async-start(f32[2,8,128,128]{3,2,0,1:T(8,128)} %copy.8), calls=%async_computation | async-start | bytes 2097152 | tf_op jit(solution)/shard_map/all_to_all | solution.py:319
  6.8 0.0 copy-done.3
  6.8 0.6 dynamic_slice.6
  9.1 0.0 copy-done
  9.1 0.1 squeeze.26
  9.2 0.1 squeeze.28
  9.3 0.1 squeeze.27
  9.4 0.2 fusion.3
  9.6 0.1 select_n.65
  9.7 0.1 reshape.109.touched
  9.8 0.0 copy-done.2
  9.8 0.7 fusion.15
  10.5 1.3 pad_add_fusion
  11.7 0.0 copy-start.1
  11.7 2.8 %copy-done.1 = f32[6,16,128,128]{3,2,1,0:T(8,128)S(1)} copy-done((f32[6,16,128,128]{3,2,1,0:T(8,128)S(1)}, f32[6,16,128,128]{3,2,1,0:T(8,128)}, u32[]{:S(2)}) %copy-start.1) | copy-done | bytes 6291480
  14.5 0.9 split_factors.1
  15.4 0.2 convert_reduce_fusion
  15.6 7.1 %all-to-all-done = f32[2,8,128,128]{3,2,0,1:T(8,128)S(1)} async-done(((f32[2,8,128,128]{3,2,0,1:T(8,128)}), f32[2,8,128,128]{3,2,0,1:T(8,128)S(1)}, u32[]{:S(2)}, u32[]{:S(2)}) %all-to-all-start) | async-done | bytes 1048608 | tf_op jit(solution)/shard_map/all_to_all | solution.py:319
  22.8 12.8 %ladder.1 = f32[16,128,128]{2,1,0:T(8,128)S(1)} custom-call(s32[16,16]{1,0:T(8,128)S(1)} %fusion.8.codes, s32[16,16]{1,0:T(8,128)S(1)} %reshape.109.touched, s32[2]{0:T(128)S(1)} %get-tuple-element.21.info, f32[16,128,128]{2,1,0:T(8,128)S(1)} %bitcast.40, bf16[2048,256]{1,0:T(8,128)(2,1)S(1)} %get-tuple-element.23.f_pair, ...), custom_call_target="tpu_custom_call" | custom-call | flops 6442450944 | bytes 4194304 | tf_op jit(solution)/shard_map/ladder/pallas_call | solution.py:165
  35.6 42.6 %all_to_all.28.blocks = f32[256,8,128]{2,1,0:T(8,128)S(1)} all-to-all(f32[256,8,128]{2,1,0:T(8,128)S(1)} %bitcast.41), channel_id=1, replica_groups=mesh['pair'=32,'virt'=8] {'virt','pair'}, dimensions={0} | all-to-all | bytes 2097152 | tf_op jit(solution)/shard_map/all_to_all | solution.py:326
  78.2 1.0 join_pairs.1
  79.2 56.1 %all_to_all.29 = f32[512,8,128]{2,1,0:T(8,128)S(1)} all-to-all(f32[512,8,128]{2,1,0:T(8,128)S(1)} %join_pairs.1), channel_id=1, replica_groups=mesh['pair'=32,'virt'=8] {'pair'}, dimensions={0} | all-to-all | bytes 4194304 | tf_op jit(solution)/shard_map/all_to_all | solution.py:328
  135.3 2.1 %settle.1 = f32[2,16,128,128]{3,2,1,0:T(8,128)} custom-call(s32[2]{0:T(128)S(1)} %get-tuple-element.17.info, f32[32,16,8,128]{3,2,1,0:T(8,128)S(1)} %bitcast.39), custom_call_target="tpu_custom_call" | custom-call | flops 262144 | bytes 4194304 | tf_op jit(solution)/shard_map/settle/pallas_call | solution.py:263
  (7 shorter events, 0.1 us)
Async XLA Ops:
  0.0 9.1 %copy-start = (s32[6,16,16,3]{2,1,3,0:T(8,128)S(1)}, s32[6,16,16,3]{2,1,3,0:T(8,128)}, u32[]{:S(2)}) copy-start(s32[6,16,16,3]{2,1,3,0:T(8,128)} %param.7) | copy-start | bytes 55300
  0.0 6.8 %copy-start.3 = (s32[128]{0:T(128)S(1)}, s32[128]{0:T(128)}, u32[]{:S(2)}) copy-start(s32[128]{0:T(128)} %param.8) | copy-start | bytes 1540
  0.0 9.8 %copy-start.2 = (s32[256]{0:T(256)S(1)}, s32[256]{0:T(256)}, u32[]{:S(2)}) copy-start(s32[256]{0:T(256)} %param.9) | copy-start | bytes 3076
  2.4 20.4 %all-to-all-start = ((f32[2,8,128,128]{3,2,0,1:T(8,128)}), f32[2,8,128,128]{3,2,0,1:T(8,128)S(1)}, u32[]{:S(2)}, u32[]{:S(2)}) async-start(f32[2,8,128,128]{3,2,0,1:T(8,128)} %copy.8), calls=%async_computation | async-start | bytes 2097152 | tf_op jit(solution)/shard_map/all_to_all | solution.py:319
  11.7 2.8 %copy-start.1 = (f32[6,16,128,128]{3,2,1,0:T(8,128)S(1)}, f32[6,16,128,128]{3,2,1,0:T(8,128)}, u32[]{:S(2)}) copy-start(f32[6,16,128,128]{3,2,1,0:T(8,128)} %fac.1) | copy-start | bytes 18874372

commit v5 on v3

--- a/solution.py
+++ b/solution.py
@@ -47,29 +47,82 @@
     )(info, factors)
 
 
+def deal_body(info, source, *refs):
+    outs, held, sems = refs[:-2], refs[-2], refs[-1]
+    count = len(outs)
+    local = source.shape[0]
+    taken, given = [], []
+    for d, out in enumerate(outs):
+        to = lax.rem(info[2] + d, count)
+        taken.append(
+            [
+                pltpu.make_async_copy(source.at[i, to], held.at[d, i], sems.at[d, i])
+                for i in range(local)
+            ]
+        )
+        given.append(pltpu.make_async_copy(held.at[d], out, sems.at[d, local]))
+    for copies in taken:
+        for copy in copies:
+            copy.start()
+    for copies, copy in zip(taken, given):
+        for each in copies:
+            each.wait()
+        copy.start()
+    for copy in given:
+        copy.wait()
+
+
+def deal(info, amplitudes):
+    local, count, n, _ = amplitudes.shape
+    anywhere = pl.BlockSpec(memory_space=pl.ANY)
+    return pl.pallas_call(
+        deal_body,
+        out_shape=[jax.ShapeDtypeStruct((local, n, n), F32)] * count,
+        grid_spec=pltpu.PrefetchScalarGridSpec(
+            num_scalar_prefetch=1,
+            grid=(1,),
+            in_specs=[anywhere],
+            out_specs=[anywhere] * count,
+            scratch_shapes=[
+                pltpu.VMEM((count, local, n, n), F32),
+                pltpu.SemaphoreType.DMA((count, local + 1)),
+            ],
+        ),
+        compiler_params=pltpu.CompilerParams(vmem_limit_bytes=56 << 20),
+        cost_estimate=pl.CostEstimate(flops=0, bytes_accessed=2 << 20, transcendentals=0),
+        name="deal",
+    )(info, amplitudes)
+
+
 def ladder_body(
-    codes, touched, info, amp, f_pair, f_turn, out, amp_high, amp_low, prod_a, prod_b, grouped
+    codes, touched, info, *refs
 ):
+    f_pair, f_turn, out, amp_high, amp_low, prod_a, prod_b, grouped = refs[-8:]
+    amps = refs[:-8]
     slots, n, _ = out.shape
     entries = codes.shape[1]
     mirrored = info[1]
 
-    def put(s, tile):
-        v, i = s // 2, s % 2
+    def put(v, i, tile):
         high, low = halves(tile)
         amp_high[v, :n, i * n : (i + 1) * n] = high
         amp_high[v, n:, i * n : (i + 1) * n] = high
         amp_low[v, :, i * n : (i + 1) * n] = low
 
+    count = len(amps)
+    origins = [lax.rem(info[2] + (count - d), count) for d in range(count)]
+
     @pl.when(mirrored == 0)
     def _():
-        for s in range(slots):
-            put(s, amp[s])
+        for v, amp in zip(origins, amps):
+            for i in range(amp.shape[0]):
+                put(v, i, amp[i])
 
     @pl.when(mirrored != 0)
     def _():
-        for s in range(slots):
-            put(s, amp[s].T)
+        for v, amp in zip(origins, amps):
+            for i in range(amp.shape[0]):
+                put(v, i, amp[i].T)
 
     chunks = 4
     height = slots * n // chunks
@@ -133,9 +186,11 @@
         out[g : g + step] = total.reshape(step, n, n)
 
 
-def ladder(codes, touched, info, amp, f_pair, f_turn):
-    slots, n, _ = amp.shape
+def ladder(codes, touched, info, amps, f_pair, f_turn):
+    local, n, _ = amps[0].shape
+    slots = local * len(amps)
     wide = slots * n
+    few = pl.BlockSpec((local, n, n), lambda i, *_: (0, 0, 0))
     whole = pl.BlockSpec((slots, n, n), lambda i, *_: (0, 0, 0))
     table = pl.BlockSpec((wide, 2 * n), lambda i, *_: (0, 0))
     return pl.pallas_call(
@@ -144,7 +199,7 @@
         grid_spec=pltpu.PrefetchScalarGridSpec(
             num_scalar_prefetch=3,
             grid=(1,),
-            in_specs=[whole, table, table],
+            in_specs=[few] * len(amps) + [table, table],
             out_specs=whole,
             scratch_shapes=[
                 pltpu.VMEM((slots // 2, 2 * n, 2 * n), BF16),
@@ -159,7 +214,7 @@
             flops=12 * wide * wide * n, bytes_accessed=4 << 20, transcendentals=0
         ),
         name="ladder",
-    )(codes, touched, info, amp, f_pair, f_turn)
+    )(codes, touched, info, *amps, f_pair, f_turn)
 
 
 def pairs_body(spot, blocks, out, *, per_home):
@@ -168,14 +223,16 @@
     half = count // 2
     out[...] = jnp.zeros(out.shape, F32)
 
-    def one(q, c):
-        row = (q % per_home) * homes + q // per_home
-        value = blocks[row] + blocks[row + homes // 2]
-        out[spot[q]] = value
-        out[spot[q + half]] = value
+    def home(h, c):
+        for v in range(per_home):
+            row = v * homes + h
+            q = h * per_home + v
+            value = blocks[row] + blocks[row + homes // 2]
+            out[spot[q]] = value
+            out[spot[q + half]] = value
         return c
 
-    lax.fori_loop(0, half, one, 0, unroll=4)
+    lax.fori_loop(0, homes // 2, home, 0)
 
 
 def join_pairs(spot, blocks, own_slots, per_home):
@@ -269,7 +326,7 @@
     codes = jnp.where(
         mirrored != 0, partner * 256 + right * 16 + left, o * 256 + left * 16 + right
     )
-    info = jnp.stack([region, mirrored])
+    info = jnp.stack([region, mirrored, my_virt])
     group = ((codes >> 8) * 16 + (codes & 15)).reshape(-1)
     place = jnp.arange(group.shape[0])
     met = (group[:, None] == group[None, :]) & (place[None, :] < place[:, None])
@@ -287,12 +344,17 @@
     swap = (my_virt * local_slots < OFF_DIAG).astype(jnp.int32)
     settle_info = jnp.stack([plain, swap])
 
-    amp = lax.all_to_all(amplitudes, "virt", split_axis=1, concat_axis=0, tiled=True)
+    pieces = deal(jnp.stack([my_virt] * 3), amplitudes)
+    amps = {0: pieces[0]}
+    for d in sorted(range(1, virt_count), key=lambda d: -min(d, virt_count - d)):
+        route = [(i, (i + d) % virt_count) for i in range(virt_count)]
+        amps[d] = lax.ppermute(pieces[d], "virt", route)
+    amps = [amps[d] for d in range(virt_count)]
     f_pair, f_turn = split_factors(info, factors)
-    amp, codes, touched, info, f_pair, f_turn, spot, settle_info = lax.optimization_barrier(
-        (amp, codes, touched, info, f_pair, f_turn, spot, settle_info)
-    )
-    result = ladder(codes, touched, info, amp.reshape(-1, n, n), f_pair, f_turn)
+    amps, codes, touched, info, f_pair, f_turn, spot, settle_info = lax.optimization_barrier(
+        (amps, codes, touched, info, f_pair, f_turn, spot, settle_info)
+    )
+    result = ladder(codes, touched, info, amps, f_pair, f_turn)
     sheets = result.reshape(virt_count * pair_count, -1, n)
     spread = lax.all_to_all(sheets, ("virt", "pair"), split_axis=0, concat_axis=0, tiled=True)
     joined = join_pairs(spot, spread, pair_count * own_most, per_home)
@@ -303,7 +365,7 @@
         own_most,
         local_slots,
         n,
-        4,
+        8,
     )
 
 

time: 139 us -> 140 us (level)
  waiting for transfers between devices: 7.14 us -> 0.02 us
  starting transfers between devices: 4.47 us -> 8.89 us
  other arithmetic: 2.39 us -> 4.61 us
  Pallas kernels: 17.8 us -> 19.5 us
    ppermute x0 -> x7, starting transfers between devices: none -> 8.89 us  [on_device(): amps[d] = lax.ppermute(pieces[d], 'virt', route)]
    all_to_all x1 -> x0, waiting for transfers between devices: 7.14 us -> none  [on_device(): lax.all_to_all(amplitudes, 'virt', split_axis=1, concat_axis=0, tiled=True)]
    all_to_all x1 -> x0, starting transfers between devices: 4.47 us -> none  [on_device(): lax.all_to_all(amplitudes, 'virt', split_axis=1, concat_axis=0, tiled=True)]
    pallas_call x0 -> x1, Pallas kernels: none -> 2.77 us  [deal(): pl.pallas_call(deal_body, out_shape=[jax.ShapeDtypeStruct((local, n, n),...]
    unnamed x9 -> x6, local copies, waits for them, and re-layouts: 5.14 us -> 2.8 us
  transfers between devices with their start and end apart: 1 -> 7, of which waited for: 1 -> 0; matrix products, arithmetic and copies ran while one was open for 2% -> 4% of each run, Pallas kernels for 1% -> 1%
where the time goes in v5:
time: 140 us; the launch traced here: 139 us
  blocking collectives  99.6 us (71%)
  Pallas kernels  19.5 us (14%)
  starting transfers between devices  8.89 us (6%)
  local copies, waits for them, and re-layouts  4.99 us (4%)
  other arithmetic  4.61 us (3%)
  between operations  1.79 us (1%)
    all_to_all x1, blocking collectives, on_device(): lax.all_to_all(joined, 'pair', split_axis=0, concat_axis=0, tiled=True)  56.1 us
    all_to_all x1, blocking collectives, on_device(): lax.all_to_all(sheets, ('virt', 'pair'), split_axis=0, concat_axis=0, til...  43.5 us
    pallas_call x1, Pallas kernels, ladder(): pl.pallas_call(ladder_body, out_shape=jax.ShapeDtypeStruct((slots, n, n),...  12.2 us
    ppermute x7, starting transfers between devices, on_device(): amps[d] = lax.ppermute(pieces[d], 'virt', route)  8.89 us
  transfers between devices with their start and end apart: 7, of which 0 were waited for; matrix products, arithmetic and copies ran while one was open for 4% of the time, Pallas kernels for 1%

profile of v5, /device:TPU:2, one launch (start us, length us, event | category | flops | bytes accessed | tf_op | source)
XLA Modules:
  0.0 139.3 jit_solution(8152061027590178063)
XLA Ops:
  0.0 0.0 copy-start
  0.0 0.6 stack.27.info
  0.6 2.8 %deal.1 = (f32[2,128,128]{2,1,0:T(8,128)}, f32[2,128,128]{2,1,0:T(8,128)}, f32[2,128,128]{2,1,0:T(8,128)}, f32[2,128,128]{2,1,0:T(8,128)}, f32[2,128,128]{2,1,0:...) custom-call(s32[3]{0:T(128)} %stack.27.info, f32[2,8,128,128]{3,2,1,0:T(8,128)} %source.1), custom_call_target="tpu_custom_call" | custom-call | bytes 2097152 | tf_op jit(solution)/shard_map/deal/pallas_call | solution.py:78
  3.4 0.0 collective-permute-start
  3.4 1.7 %collective-permute-start.1 = (f32[2,128,128]{2,1,0:T(8,128)}, f32[2,128,128]{2,1,0:T(8,128)S(1)}, u32[]{:S(2)}, u32[]{:S(2)}) collective-permute-start(f32[2,128,128]{2,1,0:T(8,128)} %get-tuple-element.32), channel_id=1, source_target_pairs={{0,2},{1,3},{2,4},{3,5},{4,6},{5,7},{6,0},{7,1},{8,10},{9,11},{10,... | collective-permute-start | bytes 393224 | tf_op jit(solution)/shard_map/ppermute | solution.py:351
  5.0 2.2 %collective-permute-start.2 = (f32[2,128,128]{2,1,0:T(8,128)}, f32[2,128,128]{2,1,0:T(8,128)S(1)}, u32[]{:S(2)}, u32[]{:S(2)}) collective-permute-start(f32[2,128,128]{2,1,0:T(8,128)} %get-tuple-element.33), channel_id=1, source_target_pairs={{0,3},{1,4},{2,5},{3,6},{4,7},{5,0},{6,1},{7,2},{8,11},{9,12},{10,... | collective-permute-start | bytes 393224 | tf_op jit(solution)/shard_map/ppermute | solution.py:351
  7.2 1.8 %collective-permute-start.3 = (f32[2,128,128]{2,1,0:T(8,128)}, f32[2,128,128]{2,1,0:T(8,128)S(1)}, u32[]{:S(2)}, u32[]{:S(2)}) collective-permute-start(f32[2,128,128]{2,1,0:T(8,128)} %get-tuple-element.34), channel_id=1, source_target_pairs={{0,4},{1,5},{2,6},{3,7},{4,0},{5,1},{6,2},{7,3},{8,12},{9,13},{10,... | collective-permute-start | bytes 393224 | tf_op jit(solution)/shard_map/ppermute | solution.py:351
  9.1 1.8 %collective-permute-start.4 = (f32[2,128,128]{2,1,0:T(8,128)}, f32[2,128,128]{2,1,0:T(8,128)S(1)}, u32[]{:S(2)}, u32[]{:S(2)}) collective-permute-start(f32[2,128,128]{2,1,0:T(8,128)} %get-tuple-element.35), channel_id=1, source_target_pairs={{0,5},{1,6},{2,7},{3,0},{4,1},{5,2},{6,3},{7,4},{8,13},{9,14},{10,... | collective-permute-start | bytes 393224 | tf_op jit(solution)/shard_map/ppermute | solution.py:351
  10.9 1.2 dynamic_slice.6
  13.2 0.9 convert_reduce_fusion
  14.7 0.0 copy-done
  14.8 0.1 squeeze.26
  14.8 0.1 squeeze.28
  14.9 0.1 squeeze.27
  15.0 0.2 fusion.3
  15.2 0.1 select_n.65
  15.3 0.7 multiply_add_fusion.spot
  16.0 1.4 fusion.15
  17.4 0.0 collective-permute-done.refs_1_
  17.4 1.3 collective-permute-start.5
  18.7 0.0 collective-permute-done.1.refs_2_
  18.7 0.0 collective-permute-start.6
  18.8 0.6 pad_add_fusion.info
  19.4 0.1 reshape.107.touched
  19.5 0.0 copy-start.1
  19.5 2.8 %copy-done.1 = f32[6,16,128,128]{3,2,1,0:T(8,128)S(1)} copy-done((f32[6,16,128,128]{3,2,1,0:T(8,128)S(1)}, f32[6,16,128,128]{3,2,1,0:T(8,128)}, u32[]{:S(2)}) %copy-start.1) | copy-done | bytes 6291480
  22.3 0.0 copy-start.2
  22.3 0.9 split_factors.1
  23.2 0.7 pad_add_fusion.1.info
  23.9 0.0 collective-permute-done.2.refs_3_
  23.9 0.0 collective-permute-done.3.refs_4_
  23.9 0.0 collective-permute-done.4.refs_5_
  23.9 0.0 collective-permute-done.5.refs_6_
  23.9 0.0 collective-permute-done.6.refs_7_
  23.9 0.0 copy-done.2
  24.0 12.2 %ladder.1 = f32[16,128,128]{2,1,0:T(8,128)S(1)} custom-call(s32[16,16]{1,0:T(8,128)S(1)} %fusion.8.codes, s32[16,16]{1,0:T(8,128)S(1)} %reshape.107.touched, s32[3]{0:T(128)S(1)} %pad_add_fusion.info, f32[2,128,128]{2,1,0:T(8,128)S(1)} %copy-done.2, f32[2,128,128]{2,1,0:T(8,128)S(1)} %collective-permute-done.refs_1_, ...), custom_call_target="tpu_custom_call" | custom-call | flops 6442450944 | bytes 4194304 | tf_op jit(solution)/shard_map/ladder/pallas_call | solution.py:196
  36.2 43.5 %all_to_all.10.blocks = f32[256,8,128]{2,1,0:T(8,128)S(1)} all-to-all(f32[256,8,128]{2,1,0:T(8,128)S(1)} %bitcast.35), channel_id=1, replica_groups=mesh['pair'=32,'virt'=8] {'virt','pair'}, dimensions={0} | all-to-all | bytes 2097152 | tf_op jit(solution)/shard_map/all_to_all | solution.py:359
  79.6 1.0 join_pairs.1
  80.7 56.1 %all_to_all.11 = f32[512,8,128]{2,1,0:T(8,128)S(1)} all-to-all(f32[512,8,128]{2,1,0:T(8,128)S(1)} %join_pairs.1), channel_id=1, replica_groups=mesh['pair'=32,'virt'=8] {'pair'}, dimensions={0} | all-to-all | bytes 4194304 | tf_op jit(solution)/shard_map/all_to_all | solution.py:361
  136.8 2.6 %settle.1 = f32[2,16,128,128]{3,2,1,0:T(8,128)} custom-call(s32[2]{0:T(128)S(1)} %pad_add_fusion.1.info, f32[32,16,8,128]{3,2,1,0:T(8,128)S(1)} %bitcast.34), custom_call_target="tpu_custom_call" | custom-call | flops 262144 | bytes 4194304 | tf_op jit(solution)/shard_map/settle/pallas_call | solution.py:291
  (6 shorter events, 0.1 us)
Async XLA Ops:
  0.0 14.7 %copy-start = (s32[6,16,16,3]{2,1,3,0:T(8,128)S(1)}, s32[6,16,16,3]{2,1,3,0:T(8,128)}, u32[]{:S(2)}) copy-start(s32[6,16,16,3]{2,1,3,0:T(8,128)} %param.7) | copy-start | bytes 55300
  3.4 14.0 %collective-permute-start = (f32[2,128,128]{2,1,0:T(8,128)}, f32[2,128,128]{2,1,0:T(8,128)S(1)}, u32[]{:S(2)}, u32[]{:S(2)}) collective-permute-start(f32[2,128,128]{2,1,0:T(8,128)} %get-tuple-element.31), channel_id=1, source_target_pairs={{0,1},{1,2},{2,3},{3,4},{4,5},{5,6},{6,7},{7,0},{8,9},{9,10},{10,1... | collective-permute-start | bytes 393224 | tf_op jit(solution)/shard_map/ppermute | solution.py:351
  3.4 15.4 %collective-permute-start.1 = (f32[2,128,128]{2,1,0:T(8,128)}, f32[2,128,128]{2,1,0:T(8,128)S(1)}, u32[]{:S(2)}, u32[]{:S(2)}) collective-permute-start(f32[2,128,128]{2,1,0:T(8,128)} %get-tuple-element.32), channel_id=1, source_target_pairs={{0,2},{1,3},{2,4},{3,5},{4,6},{5,7},{6,0},{7,1},{8,10},{9,11},{10,... | collective-permute-start | bytes 393224 | tf_op jit(solution)/shard_map/ppermute | solution.py:351
  5.0 18.9 %collective-permute-start.2 = (f32[2,128,128]{2,1,0:T(8,128)}, f32[2,128,128]{2,1,0:T(8,128)S(1)}, u32[]{:S(2)}, u32[]{:S(2)}) collective-permute-start(f32[2,128,128]{2,1,0:T(8,128)} %get-tuple-element.33), channel_id=1, source_target_pairs={{0,3},{1,4},{2,5},{3,6},{4,7},{5,0},{6,1},{7,2},{8,11},{9,12},{10,... | collective-permute-start | bytes 393224 | tf_op jit(solution)/shard_map/ppermute | solution.py:351
  7.2 16.7 %collective-permute-start.3 = (f32[2,128,128]{2,1,0:T(8,128)}, f32[2,128,128]{2,1,0:T(8,128)S(1)}, u32[]{:S(2)}, u32[]{:S(2)}) collective-permute-start(f32[2,128,128]{2,1,0:T(8,128)} %get-tuple-element.34), channel_id=1, source_target_pairs={{0,4},{1,5},{2,6},{3,7},{4,0},{5,1},{6,2},{7,3},{8,12},{9,13},{10,... | collective-permute-start | bytes 393224 | tf_op jit(solution)/shard_map/ppermute | solution.py:351
  9.1 14.8 %collective-permute-start.4 = (f32[2,128,128]{2,1,0:T(8,128)}, f32[2,128,128]{2,1,0:T(8,128)S(1)}, u32[]{:S(2)}, u32[]{:S(2)}) collective-permute-start(f32[2,128,128]{2,1,0:T(8,128)} %get-tuple-element.35), channel_id=1, source_target_pairs={{0,5},{1,6},{2,7},{3,0},{4,1},{5,2},{6,3},{7,4},{8,13},{9,14},{10,... | collective-permute-start | bytes 393224 | tf_op jit(solution)/shard_map/ppermute | solution.py:351
  17.4 6.5 %collective-permute-start.5 = (f32[2,128,128]{2,1,0:T(8,128)}, f32[2,128,128]{2,1,0:T(8,128)S(1)}, u32[]{:S(2)}, u32[]{:S(2)}) collective-permute-start(f32[2,128,128]{2,1,0:T(8,128)} %get-tuple-element.36), channel_id=1, source_target_pairs={{0,6},{1,7},{2,0},{3,1},{4,2},{5,3},{6,4},{7,5},{8,14},{9,15},{10,... | collective-permute-start | bytes 393224 | tf_op jit(solution)/shard_map/ppermute | solution.py:351
  18.7 5.2 %collective-permute-start.6 = (f32[2,128,128]{2,1,0:T(8,128)}, f32[2,128,128]{2,1,0:T(8,128)S(1)}, u32[]{:S(2)}, u32[]{:S(2)}) collective-permute-start(f32[2,128,128]{2,1,0:T(8,128)} %get-tuple-element.37), channel_id=1, source_target_pairs={{0,7},{1,0},{2,1},{3,2},{4,3},{5,4},{6,5},{7,6},{8,15},{9,8},{10,9... | collective-permute-start | bytes 393224 | tf_op jit(solution)/shard_map/ppermute | solution.py:351
  19.5 2.8 %copy-start.1 = (f32[6,16,128,128]{3,2,1,0:T(8,128)S(1)}, f32[6,16,128,128]{3,2,1,0:T(8,128)}, u32[]{:S(2)}) copy-start(f32[6,16,128,128]{3,2,1,0:T(8,128)} %fac.1) | copy-start | bytes 18874372
  22.3 1.7 %copy-start.2 = (f32[2,128,128]{2,1,0:T(8,128)S(1)}, f32[2,128,128]{2,1,0:T(8,128)}, u32[]{:S(2)}) copy-start(f32[2,128,128]{2,1,0:T(8,128)} %get-tuple-element.45.refs_0_) | copy-start | bytes 393220

commit v6 on v5

--- a/solution.py
+++ b/solution.py
@@ -19,41 +19,38 @@
     return high, (x - high.astype(F32)).astype(BF16)
 
 
-def split_body(info, fac, f_pair, f_turn):
-    slots, n = fac.shape[1], fac.shape[2]
+def split_body(fac, f_pair, f_turn):
+    slots, n, _ = fac.shape
     for l in range(slots):
-        tile = fac[0, l]
+        tile = fac[l]
         rows = slice(l * n, (l + 1) * n)
         f_pair[rows, :n], f_pair[rows, n:] = halves(tile)
         f_turn[rows, :n], f_turn[rows, n:] = halves(tile.T)
 
 
-def split_factors(info, factors):
-    _, slots, n, _ = factors.shape
+def split_factors(factors):
+    slots, n, _ = factors.shape
     shape = jax.ShapeDtypeStruct((slots * n, 2 * n), BF16)
-    spec = pl.BlockSpec(shape.shape, lambda i, *_: (0, 0))
+    spec = pl.BlockSpec(shape.shape, lambda i: (0, 0))
     return pl.pallas_call(
         split_body,
         out_shape=[shape, shape],
-        grid_spec=pltpu.PrefetchScalarGridSpec(
-            num_scalar_prefetch=1,
-            grid=(1,),
-            in_specs=[pl.BlockSpec((1, slots, n, n), lambda i, info: (info[0], 0, 0, 0))],
-            out_specs=[spec, spec],
-        ),
+        grid=(1,),
+        in_specs=[pl.BlockSpec((slots, n, n), lambda i: (0, 0, 0))],
+        out_specs=[spec, spec],
         compiler_params=pltpu.CompilerParams(vmem_limit_bytes=16 << 20),
         cost_estimate=pl.CostEstimate(flops=1 << 20, bytes_accessed=3 << 20, transcendentals=0),
         name="split_factors",
-    )(info, factors)
-
-
-def deal_body(info, source, *refs):
+    )(factors)
+
+
+def deal_body(source, *refs):
     outs, held, sems = refs[:-2], refs[-2], refs[-1]
     count = len(outs)
     local = source.shape[0]
     taken, given = [], []
     for d, out in enumerate(outs):
-        to = lax.rem(info[2] + d, count)
+        to = lax.rem(lax.axis_index("virt") + d, count)
         taken.append(
             [
                 pltpu.make_async_copy(source.at[i, to], held.at[d, i], sems.at[d, i])
@@ -72,36 +69,32 @@
         copy.wait()
 
 
-def deal(info, amplitudes):
+def deal(amplitudes):
     local, count, n, _ = amplitudes.shape
     anywhere = pl.BlockSpec(memory_space=pl.ANY)
     return pl.pallas_call(
         deal_body,
         out_shape=[jax.ShapeDtypeStruct((local, n, n), F32)] * count,
-        grid_spec=pltpu.PrefetchScalarGridSpec(
-            num_scalar_prefetch=1,
-            grid=(1,),
-            in_specs=[anywhere],
-            out_specs=[anywhere] * count,
-            scratch_shapes=[
-                pltpu.VMEM((count, local, n, n), F32),
-                pltpu.SemaphoreType.DMA((count, local + 1)),
-            ],
-        ),
+        in_specs=[anywhere],
+        out_specs=[anywhere] * count,
+        scratch_shapes=[
+            pltpu.VMEM((count, local, n, n), F32),
+            pltpu.SemaphoreType.DMA((count, local + 1)),
+        ],
         compiler_params=pltpu.CompilerParams(vmem_limit_bytes=56 << 20),
         cost_estimate=pl.CostEstimate(flops=0, bytes_accessed=2 << 20, transcendentals=0),
         name="deal",
-    )(info, amplitudes)
+    )(amplitudes)
 
 
 def ladder_body(
-    codes, touched, info, *refs
+    codes, touched, *refs
 ):
     f_pair, f_turn, out, amp_high, amp_low, prod_a, prod_b, grouped = refs[-8:]
     amps = refs[:-8]
     slots, n, _ = out.shape
     entries = codes.shape[1]
-    mirrored = info[1]
+    mirrored = (lax.axis_index("pair") >= lax.axis_size("pair") // 2).astype(jnp.int32)
 
     def put(v, i, tile):
         high, low = halves(tile)
@@ -110,7 +103,7 @@
         amp_low[v, :, i * n : (i + 1) * n] = low
 
     count = len(amps)
-    origins = [lax.rem(info[2] + (count - d), count) for d in range(count)]
+    origins = [lax.rem(lax.axis_index("virt") + (count - d), count) for d in range(count)]
 
     @pl.when(mirrored == 0)
     def _():
@@ -186,7 +179,7 @@
         out[g : g + step] = total.reshape(step, n, n)
 
 
-def ladder(codes, touched, info, amps, f_pair, f_turn):
+def ladder(codes, touched, amps, f_pair, f_turn):
     local, n, _ = amps[0].shape
     slots = local * len(amps)
     wide = slots * n
@@ -197,7 +190,7 @@
         ladder_body,
         out_shape=jax.ShapeDtypeStruct((slots, n, n), F32),
         grid_spec=pltpu.PrefetchScalarGridSpec(
-            num_scalar_prefetch=3,
+            num_scalar_prefetch=2,
             grid=(1,),
             in_specs=[few] * len(amps) + [table, table],
             out_specs=whole,
@@ -214,7 +207,7 @@
             flops=12 * wide * wide * n, bytes_accessed=4 << 20, transcendentals=0
         ),
         name="ladder",
-    )(codes, touched, info, *amps, f_pair, f_turn)
+    )(codes, touched, *amps, f_pair, f_turn)
 
 
 def pairs_body(spot, blocks, out, *, per_home):
@@ -254,13 +247,13 @@
     )(spot, blocks)
 
 
-def settle(info, blocks, own_most, local_slots, n, group):
+def settle(held, blocks, own_most, local_slots, n, group):
     parts = blocks.shape[0]
     per = parts // local_slots
 
-    def body(info, src, out):
-        plain = info[0]
-        swap = info[1]
+    def body(held, src, out):
+        plain = held[0]
+        swap = (lax.axis_index("virt") * local_slots < OFF_DIAG).astype(jnp.int32)
         first = pl.program_id(0) * group
 
         def as_is(g):
@@ -304,7 +297,7 @@
         compiler_params=pltpu.CompilerParams(vmem_limit_bytes=16 << 20),
         cost_estimate=pl.CostEstimate(flops=1 << 18, bytes_accessed=4 << 20, transcendentals=0),
         name="settle",
-    )(info, blocks)
+    )(held, blocks)
 
 
 def on_device(amplitudes, factors, integral_quadruple_table, pair_region, owner_map):
@@ -326,7 +319,6 @@
     codes = jnp.where(
         mirrored != 0, partner * 256 + right * 16 + left, o * 256 + left * 16 + right
     )
-    info = jnp.stack([region, mirrored, my_virt])
     group = ((codes >> 8) * 16 + (codes & 15)).reshape(-1)
     place = jnp.arange(group.shape[0])
     met = (group[:, None] == group[None, :]) & (place[None, :] < place[:, None])
@@ -341,26 +333,25 @@
     spot = owner_map * own_most + jnp.sum(same.astype(jnp.int32), axis=1)
 
     plain = jnp.sum((owner_map[:half] == my_pair).astype(jnp.int32))
-    swap = (my_virt * local_slots < OFF_DIAG).astype(jnp.int32)
-    settle_info = jnp.stack([plain, swap])
-
-    pieces = deal(jnp.stack([my_virt] * 3), amplitudes)
+    held = plain.reshape(1)
+
+    pieces = deal(amplitudes)
     amps = {0: pieces[0]}
     for d in sorted(range(1, virt_count), key=lambda d: -min(d, virt_count - d)):
         route = [(i, (i + d) % virt_count) for i in range(virt_count)]
         amps[d] = lax.ppermute(pieces[d], "virt", route)
     amps = [amps[d] for d in range(virt_count)]
-    f_pair, f_turn = split_factors(info, factors)
-    amps, codes, touched, info, f_pair, f_turn, spot, settle_info = lax.optimization_barrier(
-        (amps, codes, touched, info, f_pair, f_turn, spot, settle_info)
-    )
-    result = ladder(codes, touched, info, amps, f_pair, f_turn)
+    f_pair, f_turn = split_factors(lax.dynamic_index_in_dim(factors, region, 0, keepdims=False))
+    amps, codes, touched, f_pair, f_turn, spot, held = lax.optimization_barrier(
+        (amps, codes, touched, f_pair, f_turn, spot, held)
+    )
+    result = ladder(codes, touched, amps, f_pair, f_turn)
     sheets = result.reshape(virt_count * pair_count, -1, n)
     spread = lax.all_to_all(sheets, ("virt", "pair"), split_axis=0, concat_axis=0, tiled=True)
     joined = join_pairs(spot, spread, pair_count * own_most, per_home)
     arrived = lax.all_to_all(joined, "pair", split_axis=0, concat_axis=0, tiled=True)
     return settle(
-        settle_info,
+        held,
         arrived.reshape(pair_count, own_most, -1, n),
         own_most,
         local_slots,

time: 140 us -> 137 us (0.979)
  other arithmetic: 4.61 us -> 2.51 us
  local copies, waits for them, and re-layouts: 4.99 us -> 3 us
  waiting for transfers between devices: 0.02 us -> 1.77 us
  Pallas kernels: 19.5 us -> 18 us
  blocking collectives: 99.6 us -> 101 us
    unnamed x6, local copies, waits for them, and re-layouts: 2.8 us -> 0.01 us
    ppermute x7, waiting for transfers between devices: 0.02 us -> 1.77 us  [on_device(): amps[d] = lax.ppermute(pieces[d], 'virt', route)]
  transfers between devices with their start and end apart: 7 -> 7, of which waited for: 0 -> 2; matrix products, arithmetic and copies ran while one was open for 4% -> 4% of each run, Pallas kernels for 1% -> 0%
where the time goes in v6:
time: 137 us
  blocking collectives  101 us (74%)
  Pallas kernels  18 us (13%)
  starting transfers between devices  8.89 us (6%)
  local copies, waits for them, and re-layouts  3 us (2%)
  other arithmetic  2.51 us (2%)
  between operations  2.04 us (1%)
  waiting for transfers between devices  1.77 us (1%)
    all_to_all x1, blocking collectives, on_device(): lax.all_to_all(joined, 'pair', split_axis=0, concat_axis=0, tiled=True)  56.1 us
    all_to_all x1, blocking collectives, on_device(): lax.all_to_all(sheets, ('virt', 'pair'), split_axis=0, concat_axis=0, til...  44.5 us
    pallas_call x1, Pallas kernels, ladder(): pl.pallas_call(ladder_body, out_shape=jax.ShapeDtypeStruct((slots, n, n),...  12.1 us
    ppermute x7, starting transfers between devices, on_device(): amps[d] = lax.ppermute(pieces[d], 'virt', route)  8.89 us
  transfers between devices with their start and end apart: 7, of which 2 were waited for; matrix products, arithmetic and copies ran while one was open for 4% of the time, Pallas kernels for 0%

profile of v6, /device:TPU:2, one launch (start us, length us, event | category | flops | bytes accessed | tf_op | source)
XLA Modules:
  0.0 136.8 jit_solution(7059110093591041518)
XLA Ops:
  0.0 0.0 copy-start
  0.0 0.0 copy-start.2
  0.0 2.1 %deal.1 = (f32[2,128,128]{2,1,0:T(8,128)}, f32[2,128,128]{2,1,0:T(8,128)}, f32[2,128,128]{2,1,0:T(8,128)}, f32[2,128,128]{2,1,0:T(8,128)}, f32[2,128,128]{2,1,0:...) custom-call(f32[2,8,128,128]{3,2,1,0:T(8,128)} %source.1), custom_call_target="tpu_custom_call" | custom-call | bytes 2097152 | tf_op jit(solution)/shard_map/deal/pallas_call | solution.py:75
  2.1 0.0 copy-start.1
  2.2 0.0 collective-permute-start
  2.2 1.7 %collective-permute-start.1 = (f32[2,128,128]{2,1,0:T(8,128)}, f32[2,128,128]{2,1,0:T(8,128)S(1)}, u32[]{:S(2)}, u32[]{:S(2)}) collective-permute-start(f32[2,128,128]{2,1,0:T(8,128)} %get-tuple-element.31), channel_id=1, source_target_pairs={{0,2},{1,3},{2,4},{3,5},{4,6},{5,7},{6,0},{7,1},{8,10},{9,11},{10,... | collective-permute-start | bytes 393224 | tf_op jit(solution)/shard_map/ppermute | solution.py:342
  3.8 2.2 %collective-permute-start.2 = (f32[2,128,128]{2,1,0:T(8,128)}, f32[2,128,128]{2,1,0:T(8,128)S(1)}, u32[]{:S(2)}, u32[]{:S(2)}) collective-permute-start(f32[2,128,128]{2,1,0:T(8,128)} %get-tuple-element.32), channel_id=1, source_target_pairs={{0,3},{1,4},{2,5},{3,6},{4,7},{5,0},{6,1},{7,2},{8,11},{9,12},{10,... | collective-permute-start | bytes 393224 | tf_op jit(solution)/shard_map/ppermute | solution.py:342
  6.0 1.8 %collective-permute-start.3 = (f32[2,128,128]{2,1,0:T(8,128)}, f32[2,128,128]{2,1,0:T(8,128)S(1)}, u32[]{:S(2)}, u32[]{:S(2)}) collective-permute-start(f32[2,128,128]{2,1,0:T(8,128)} %get-tuple-element.33), channel_id=1, source_target_pairs={{0,4},{1,5},{2,6},{3,7},{4,0},{5,1},{6,2},{7,3},{8,12},{9,13},{10,... | collective-permute-start | bytes 393224 | tf_op jit(solution)/shard_map/ppermute | solution.py:342
  7.9 1.8 %collective-permute-start.4 = (f32[2,128,128]{2,1,0:T(8,128)}, f32[2,128,128]{2,1,0:T(8,128)S(1)}, u32[]{:S(2)}, u32[]{:S(2)}) collective-permute-start(f32[2,128,128]{2,1,0:T(8,128)} %get-tuple-element.34), channel_id=1, source_target_pairs={{0,5},{1,6},{2,7},{3,0},{4,1},{5,2},{6,3},{7,4},{8,13},{9,14},{10,... | collective-permute-start | bytes 393224 | tf_op jit(solution)/shard_map/ppermute | solution.py:342
  9.7 1.3 dynamic_slice.10
  12.9 0.0 copy-done
  12.9 0.1 squeeze.31
  13.0 0.1 squeeze.32
  13.1 0.1 squeeze.30
  13.2 0.2 fusion.3
  13.4 0.1 select_n.67
  13.5 0.9 convert_reduce_fusion
  14.4 0.7 multiply_add_fusion.spot
  15.1 0.0 collective-permute-done.refs_1_
  15.1 1.3 collective-permute-start.5
  16.5 0.0 collective-permute-done.1.refs_2_
  16.5 0.0 collective-permute-start.6
  16.5 1.3 dynamic-slice_bitcast_fusion.fac
  17.8 0.1 reshape.109.touched
  17.9 0.4 split_factors.1
  18.3 0.0 copy-done.2
  18.3 0.6 fusion.15
  18.9 0.0 collective-permute-done.2.refs_3_
  18.9 0.0 collective-permute-done.3.refs_4_
  18.9 0.0 collective-permute-done.4.refs_5_
  18.9 1.4 %collective-permute-done.5.refs_6_ = f32[2,128,128]{2,1,0:T(8,128)S(1)} collective-permute-done((f32[2,128,128]{2,1,0:T(8,128)}, f32[2,128,128]{2,1,0:T(8,128)S(1)}, u32[]{:S(2)}, u32[]{:S(2)}) %collective-permute-start.5) | collective-permute-done | bytes 131104 | tf_op jit(solution)/shard_map/ppermute | solution.py:342
  20.3 0.4 collective-permute-done.6.refs_7_
  20.7 0.0 copy-done.1
  20.7 12.1 %ladder.1 = f32[16,128,128]{2,1,0:T(8,128)S(1)} custom-call(s32[16,16]{1,0:T(8,128)S(1)} %fusion.8.codes, s32[16,16]{1,0:T(8,128)S(1)} %reshape.109.touched, f32[2,128,128]{2,1,0:T(8,128)S(1)} %copy-done.1, f32[2,128,128]{2,1,0:T(8,128)S(1)} %collective-permute-done.refs_1_, f32[2,128,128]{2,1,0:T(8,128)S(1)} %collective-permute-done.1.refs_2_, ...), custom_call_target="tpu_custom_call" | custom-call | flops 6442450944 | bytes 4194304 | tf_op jit(solution)/shard_map/ladder/pallas_call | solution.py:189
  32.8 44.5 %all_to_all.10.blocks = f32[256,8,128]{2,1,0:T(8,128)S(1)} all-to-all(f32[256,8,128]{2,1,0:T(8,128)S(1)} %bitcast.34), channel_id=1, replica_groups=mesh['pair'=32,'virt'=8] {'virt','pair'}, dimensions={0} | all-to-all | bytes 2097152 | tf_op jit(solution)/shard_map/all_to_all | solution.py:350
  77.2 1.0 join_pairs.1
  78.3 56.1 %all_to_all.11 = f32[512,8,128]{2,1,0:T(8,128)S(1)} all-to-all(f32[512,8,128]{2,1,0:T(8,128)S(1)} %join_pairs.1), channel_id=1, replica_groups=mesh['pair'=32,'virt'=8] {'pair'}, dimensions={0} | all-to-all | bytes 4194304 | tf_op jit(solution)/shard_map/all_to_all | solution.py:352
  134.4 2.4 %settle.1 = f32[2,16,128,128]{3,2,1,0:T(8,128)} custom-call(s32[1]{0:T(128)} %bitcast.6.held, f32[32,16,8,128]{3,2,1,0:T(8,128)S(1)} %bitcast.33), custom_call_target="tpu_custom_call" | custom-call | flops 262144 | bytes 4194304 | tf_op jit(solution)/shard_map/settle/pallas_call | solution.py:284
  (6 shorter events, 0.1 us)
Async XLA Ops:
  0.0 12.9 %copy-start = (s32[6,16,16,3]{2,1,3,0:T(8,128)S(1)}, s32[6,16,16,3]{2,1,3,0:T(8,128)}, u32[]{:S(2)}) copy-start(s32[6,16,16,3]{2,1,3,0:T(8,128)} %param.7) | copy-start | bytes 55300
  0.0 18.3 %copy-start.2 = (s32[256]{0:T(256)S(1)}, s32[256]{0:T(256)}, u32[]{:S(2)}) copy-start(s32[256]{0:T(256)} %param.9) | copy-start | bytes 3076
  2.1 18.5 %copy-start.1 = (f32[2,128,128]{2,1,0:T(8,128)S(1)}, f32[2,128,128]{2,1,0:T(8,128)}, u32[]{:S(2)}) copy-start(f32[2,128,128]{2,1,0:T(8,128)} %get-tuple-element.43.refs_0_) | copy-start | bytes 393220
  2.2 13.0 %collective-permute-start = (f32[2,128,128]{2,1,0:T(8,128)}, f32[2,128,128]{2,1,0:T(8,128)S(1)}, u32[]{:S(2)}, u32[]{:S(2)}) collective-permute-start(f32[2,128,128]{2,1,0:T(8,128)} %get-tuple-element.30), channel_id=1, source_target_pairs={{0,1},{1,2},{2,3},{3,4},{4,5},{5,6},{6,7},{7,0},{8,9},{9,10},{10,1... | collective-permute-start | bytes 393224 | tf_op jit(solution)/shard_map/ppermute | solution.py:342
  2.2 14.3 %collective-permute-start.1 = (f32[2,128,128]{2,1,0:T(8,128)}, f32[2,128,128]{2,1,0:T(8,128)S(1)}, u32[]{:S(2)}, u32[]{:S(2)}) collective-permute-start(f32[2,128,128]{2,1,0:T(8,128)} %get-tuple-element.31), channel_id=1, source_target_pairs={{0,2},{1,3},{2,4},{3,5},{4,6},{5,7},{6,0},{7,1},{8,10},{9,11},{10,... | collective-permute-start | bytes 393224 | tf_op jit(solution)/shard_map/ppermute | solution.py:342
  3.8 15.1 %collective-permute-start.2 = (f32[2,128,128]{2,1,0:T(8,128)}, f32[2,128,128]{2,1,0:T(8,128)S(1)}, u32[]{:S(2)}, u32[]{:S(2)}) collective-permute-start(f32[2,128,128]{2,1,0:T(8,128)} %get-tuple-element.32), channel_id=1, source_target_pairs={{0,3},{1,4},{2,5},{3,6},{4,7},{5,0},{6,1},{7,2},{8,11},{9,12},{10,... | collective-permute-start | bytes 393224 | tf_op jit(solution)/shard_map/ppermute | solution.py:342
  6.0 12.9 %collective-permute-start.3 = (f32[2,128,128]{2,1,0:T(8,128)}, f32[2,128,128]{2,1,0:T(8,128)S(1)}, u32[]{:S(2)}, u32[]{:S(2)}) collective-permute-start(f32[2,128,128]{2,1,0:T(8,128)} %get-tuple-element.33), channel_id=1, source_target_pairs={{0,4},{1,5},{2,6},{3,7},{4,0},{5,1},{6,2},{7,3},{8,12},{9,13},{10,... | collective-permute-start | bytes 393224 | tf_op jit(solution)/shard_map/ppermute | solution.py:342
  7.9 11.0 %collective-permute-start.4 = (f32[2,128,128]{2,1,0:T(8,128)}, f32[2,128,128]{2,1,0:T(8,128)S(1)}, u32[]{:S(2)}, u32[]{:S(2)}) collective-permute-start(f32[2,128,128]{2,1,0:T(8,128)} %get-tuple-element.34), channel_id=1, source_target_pairs={{0,5},{1,6},{2,7},{3,0},{4,1},{5,2},{6,3},{7,4},{8,13},{9,14},{10,... | collective-permute-start | bytes 393224 | tf_op jit(solution)/shard_map/ppermute | solution.py:342
  15.1 5.2 %collective-permute-start.5 = (f32[2,128,128]{2,1,0:T(8,128)}, f32[2,128,128]{2,1,0:T(8,128)S(1)}, u32[]{:S(2)}, u32[]{:S(2)}) collective-permute-start(f32[2,128,128]{2,1,0:T(8,128)} %get-tuple-element.35), channel_id=1, source_target_pairs={{0,6},{1,7},{2,0},{3,1},{4,2},{5,3},{6,4},{7,5},{8,14},{9,15},{10,... | collective-permute-start | bytes 393224 | tf_op jit(solution)/shard_map/ppermute | solution.py:342
  16.5 4.2 %collective-permute-start.6 = (f32[2,128,128]{2,1,0:T(8,128)}, f32[2,128,128]{2,1,0:T(8,128)S(1)}, u32[]{:S(2)}, u32[]{:S(2)}) collective-permute-start(f32[2,128,128]{2,1,0:T(8,128)} %get-tuple-element.36), channel_id=1, source_target_pairs={{0,7},{1,0},{2,1},{3,2},{4,3},{5,4},{6,5},{7,6},{8,15},{9,8},{10,9... | collective-permute-start | bytes 393224 | tf_op jit(solution)/shard_map/ppermute | solution.py:342

commit v7 on v6

--- a/solution.py
+++ b/solution.py
@@ -310,6 +310,16 @@
     half = pair_total // 2
     own_most = 2 * per_home
 
+    pieces = deal(amplitudes)
+    amps = {0: pieces[0]}
+    for d in sorted(range(1, virt_count), key=lambda d: -min(d, virt_count - d)):
+        route = [(i, (i + d) % virt_count) for i in range(virt_count)]
+        amps[d] = lax.ppermute(pieces[d], "virt", route)
+    near = (1, virt_count - 1)
+    pair_region, *first = lax.optimization_barrier((pair_region, *(amps[d] for d in near)))
+    amps.update(zip(near, first))
+    amps = [amps[d] for d in range(virt_count)]
+
     pair = my_pair * per_home + my_virt
     mirrored = (pair >= half).astype(jnp.int32)
     region = pair_region[pair % half]
@@ -335,12 +345,6 @@
     plain = jnp.sum((owner_map[:half] == my_pair).astype(jnp.int32))
     held = plain.reshape(1)
 
-    pieces = deal(amplitudes)
-    amps = {0: pieces[0]}
-    for d in sorted(range(1, virt_count), key=lambda d: -min(d, virt_count - d)):
-        route = [(i, (i + d) % virt_count) for i in range(virt_count)]
-        amps[d] = lax.ppermute(pieces[d], "virt", route)
-    amps = [amps[d] for d in range(virt_count)]
     f_pair, f_turn = split_factors(lax.dynamic_index_in_dim(factors, region, 0, keepdims=False))
     amps, codes, touched, f_pair, f_turn, spot, held = lax.optimization_barrier(
         (amps, codes, touched, f_pair, f_turn, spot, held)

time: 137 us -> 137 us (level)
  waiting for transfers between devices: 1.77 us -> 0.02 us
  blocking collectives: 101 us -> 99.3 us
  starting transfers between devices: 8.89 us -> 10.5 us
    ppermute x7, waiting for transfers between devices: 1.77 us -> 0.02 us  [on_device(): amps[d] = lax.ppermute(pieces[d], 'virt', route)]
    ppermute x7, starting transfers between devices: 8.89 us -> 10.5 us  [on_device(): amps[d] = lax.ppermute(pieces[d], 'virt', route)]
  transfers between devices with their start and end apart: 7 -> 7, of which waited for: 2 -> 0; matrix products, arithmetic and copies ran while one was open for 4% -> 5% of each run, Pallas kernels for 0% -> 0%
where the time goes in v7:
time: 137 us; the launch traced here: 136 us
  blocking collectives  99.3 us (72%)
  Pallas kernels  17.9 us (13%)
  starting transfers between devices  10.5 us (8%)
  other arithmetic  3.24 us (2%)
  local copies, waits for them, and re-layouts  3.01 us (2%)
  between operations  2.06 us (2%)
    all_to_all x1, blocking collectives, on_device(): lax.all_to_all(joined, 'pair', split_axis=0, concat_axis=0, tiled=True)  56.1 us
    all_to_all x1, blocking collectives, on_device(): lax.all_to_all(sheets, ('virt', 'pair'), split_axis=0, concat_axis=0, til...  43.1 us
    pallas_call x1, Pallas kernels, ladder(): pl.pallas_call(ladder_body, out_shape=jax.ShapeDtypeStruct((slots, n, n),...  12.1 us
    ppermute x7, starting transfers between devices, on_device(): amps[d] = lax.ppermute(pieces[d], 'virt', route)  10.5 us
  transfers between devices with their start and end apart: 7, of which 0 were waited for; matrix products, arithmetic and copies ran while one was open for 5% of the time, Pallas kernels for 0%

profile of v7, /device:TPU:2, one launch (start us, length us, event | category | flops | bytes accessed | tf_op | source)
XLA Modules:
  0.0 136.0 jit_solution(16977432599513734738)
XLA Ops:
  0.0 0.0 copy-start
  0.0 2.1 %deal.1 = (f32[2,128,128]{2,1,0:T(8,128)}, f32[2,128,128]{2,1,0:T(8,128)}, f32[2,128,128]{2,1,0:T(8,128)}, f32[2,128,128]{2,1,0:T(8,128)}, f32[2,128,128]{2,1,0:...) custom-call(f32[2,8,128,128]{3,2,1,0:T(8,128)} %source.1), custom_call_target="tpu_custom_call" | custom-call | bytes 2097152 | tf_op jit(solution)/shard_map/deal/pallas_call | solution.py:75
  2.1 0.0 copy-start.1
  2.2 0.0 collective-permute-start
  2.2 2.9 %collective-permute-start.1 = (f32[2,128,128]{2,1,0:T(8,128)}, f32[2,128,128]{2,1,0:T(8,128)S(1)}, u32[]{:S(2)}, u32[]{:S(2)}) collective-permute-start(f32[2,128,128]{2,1,0:T(8,128)} %get-tuple-element.34), channel_id=1, source_target_pairs={{0,7},{1,0},{2,1},{3,2},{4,3},{5,4},{6,5},{7,6},{8,15},{9,8},{10,9... | collective-permute-start | bytes 393224 | tf_op jit(solution)/shard_map/ppermute | solution.py:317
  5.1 0.4 collective-permute-start.2
  5.5 0.6 collective-permute-start.3
  6.0 2.4 %collective-permute-start.4 = (f32[2,128,128]{2,1,0:T(8,128)}, f32[2,128,128]{2,1,0:T(8,128)S(1)}, u32[]{:S(2)}, u32[]{:S(2)}) collective-permute-start(f32[2,128,128]{2,1,0:T(8,128)} %get-tuple-element.38), channel_id=1, source_target_pairs={{0,4},{1,5},{2,6},{3,7},{4,0},{5,1},{6,2},{7,3},{8,12},{9,13},{10,... | collective-permute-start | bytes 393224 | tf_op jit(solution)/shard_map/ppermute | solution.py:317
  8.4 0.9 convert_reduce_fusion
  9.4 0.7 multiply_add_fusion.spot
  10.0 1.4 %fusion.15 = s32[]{:T(128)} fusion(s32[256]{0:T(256)} %param.9, s32[]{:T(128)S(6)} %axis_index.23), kind=kLoop, calls=%fused_computation.28 | loop fusion | flops 383 | bytes 520 | tf_op jit(solution)/shard_map/reduce_sum | solution.py:345
  11.4 0.0 collective-permute-done.refs_1_
  11.4 2.9 %collective-permute-start.5 = (f32[2,128,128]{2,1,0:T(8,128)}, f32[2,128,128]{2,1,0:T(8,128)S(1)}, u32[]{:S(2)}, u32[]{:S(2)}) collective-permute-start(f32[2,128,128]{2,1,0:T(8,128)} %get-tuple-element.39), channel_id=1, source_target_pairs={{0,5},{1,6},{2,7},{3,0},{4,1},{5,2},{6,3},{7,4},{8,13},{9,14},{10,... | collective-permute-start | bytes 393224 | tf_op jit(solution)/shard_map/ppermute | solution.py:317
  14.4 0.0 collective-permute-done.1.refs_7_
  14.4 1.3 collective-permute-start.6
  15.7 1.3 dynamic_slice.10
  18.9 0.0 copy-done
  18.9 0.1 squeeze.31
  19.0 0.1 squeeze.32
  19.1 0.1 squeeze.30
  19.2 0.2 fusion.3
  19.4 0.1 select_n.67
  19.5 0.1 reshape.109.touched
  19.6 1.3 dynamic-slice_bitcast_fusion.fac
  20.9 0.4 split_factors.1
  21.3 0.0 collective-permute-done.2.refs_2_
  21.3 0.0 collective-permute-done.3.refs_3_
  21.3 0.0 collective-permute-done.4.refs_4_
  21.3 0.0 collective-permute-done.5.refs_5_
  21.3 0.0 collective-permute-done.6.refs_6_
  21.3 0.0 copy-done.1
  21.4 12.1 %ladder.1 = f32[16,128,128]{2,1,0:T(8,128)S(1)} custom-call(s32[16,16]{1,0:T(8,128)S(1)} %fusion.8.codes, s32[16,16]{1,0:T(8,128)S(1)} %reshape.109.touched, f32[2,128,128]{2,1,0:T(8,128)S(1)} %copy-done.1, f32[2,128,128]{2,1,0:T(8,128)S(1)} %collective-permute-done.refs_1_, f32[2,128,128]{2,1,0:T(8,128)S(1)} %collective-permute-done.2.refs_2_, ...), custom_call_target="tpu_custom_call" | custom-call | flops 6442450944 | bytes 4194304 | tf_op jit(solution)/shard_map/ladder/pallas_call | solution.py:189
  33.5 43.1 %all_to_all.10.blocks = f32[256,8,128]{2,1,0:T(8,128)S(1)} all-to-all(f32[256,8,128]{2,1,0:T(8,128)S(1)} %bitcast.34), channel_id=1, replica_groups=mesh['pair'=32,'virt'=8] {'virt','pair'}, dimensions={0} | all-to-all | bytes 2097152 | tf_op jit(solution)/shard_map/all_to_all | solution.py:354
  76.6 1.0 join_pairs.1
  77.7 56.1 %all_to_all.11 = f32[512,8,128]{2,1,0:T(8,128)S(1)} all-to-all(f32[512,8,128]{2,1,0:T(8,128)S(1)} %join_pairs.1), channel_id=1, replica_groups=mesh['pair'=32,'virt'=8] {'pair'}, dimensions={0} | all-to-all | bytes 4194304 | tf_op jit(solution)/shard_map/all_to_all | solution.py:356
  133.8 2.2 %settle.1 = f32[2,16,128,128]{3,2,1,0:T(8,128)} custom-call(s32[1]{0:T(128)} %bitcast.6.held, f32[32,16,8,128]{3,2,1,0:T(8,128)S(1)} %bitcast.33), custom_call_target="tpu_custom_call" | custom-call | flops 262144 | bytes 4194304 | tf_op jit(solution)/shard_map/settle/pallas_call | solution.py:284
  (6 shorter events, 0.0 us)
Async XLA Ops:
  0.0 18.9 %copy-start = (s32[6,16,16,3]{2,1,3,0:T(8,128)S(1)}, s32[6,16,16,3]{2,1,3,0:T(8,128)}, u32[]{:S(2)}) copy-start(s32[6,16,16,3]{2,1,3,0:T(8,128)} %param.7) | copy-start | bytes 55300
  2.1 19.2 %copy-start.1 = (f32[2,128,128]{2,1,0:T(8,128)S(1)}, f32[2,128,128]{2,1,0:T(8,128)}, u32[]{:S(2)}) copy-start(f32[2,128,128]{2,1,0:T(8,128)} %get-tuple-element.49.refs_0_) | copy-start | bytes 393220
  2.2 9.3 %collective-permute-start = (f32[2,128,128]{2,1,0:T(8,128)}, f32[2,128,128]{2,1,0:T(8,128)S(1)}, u32[]{:S(2)}, u32[]{:S(2)}) collective-permute-start(f32[2,128,128]{2,1,0:T(8,128)} %get-tuple-element.33), channel_id=1, source_target_pairs={{0,1},{1,2},{2,3},{3,4},{4,5},{5,6},{6,7},{7,0},{8,9},{9,10},{10,1... | collective-permute-start | bytes 393224 | tf_op jit(solution)/shard_map/ppermute | solution.py:317
  2.2 12.2 %collective-permute-start.1 = (f32[2,128,128]{2,1,0:T(8,128)}, f32[2,128,128]{2,1,0:T(8,128)S(1)}, u32[]{:S(2)}, u32[]{:S(2)}) collective-permute-start(f32[2,128,128]{2,1,0:T(8,128)} %get-tuple-element.34), channel_id=1, source_target_pairs={{0,7},{1,0},{2,1},{3,2},{4,3},{5,4},{6,5},{7,6},{8,15},{9,8},{10,9... | collective-permute-start | bytes 393224 | tf_op jit(solution)/shard_map/ppermute | solution.py:317
  5.1 16.2 %collective-permute-start.2 = (f32[2,128,128]{2,1,0:T(8,128)}, f32[2,128,128]{2,1,0:T(8,128)S(1)}, u32[]{:S(2)}, u32[]{:S(2)}) collective-permute-start(f32[2,128,128]{2,1,0:T(8,128)} %get-tuple-element.36), channel_id=1, source_target_pairs={{0,2},{1,3},{2,4},{3,5},{4,6},{5,7},{6,0},{7,1},{8,10},{9,11},{10,... | collective-permute-start | bytes 393224 | tf_op jit(solution)/shard_map/ppermute | solution.py:317
  5.5 15.8 %collective-permute-start.3 = (f32[2,128,128]{2,1,0:T(8,128)}, f32[2,128,128]{2,1,0:T(8,128)S(1)}, u32[]{:S(2)}, u32[]{:S(2)}) collective-permute-start(f32[2,128,128]{2,1,0:T(8,128)} %get-tuple-element.37), channel_id=1, source_target_pairs={{0,3},{1,4},{2,5},{3,6},{4,7},{5,0},{6,1},{7,2},{8,11},{9,12},{10,... | collective-permute-start | bytes 393224 | tf_op jit(solution)/shard_map/ppermute | solution.py:317
  6.0 15.3 %collective-permute-start.4 = (f32[2,128,128]{2,1,0:T(8,128)}, f32[2,128,128]{2,1,0:T(8,128)S(1)}, u32[]{:S(2)}, u32[]{:S(2)}) collective-permute-start(f32[2,128,128]{2,1,0:T(8,128)} %get-tuple-element.38), channel_id=1, source_target_pairs={{0,4},{1,5},{2,6},{3,7},{4,0},{5,1},{6,2},{7,3},{8,12},{9,13},{10,... | collective-permute-start | bytes 393224 | tf_op jit(solution)/shard_map/ppermute | solution.py:317
  11.4 9.9 %collective-permute-start.5 = (f32[2,128,128]{2,1,0:T(8,128)}, f32[2,128,128]{2,1,0:T(8,128)S(1)}, u32[]{:S(2)}, u32[]{:S(2)}) collective-permute-start(f32[2,128,128]{2,1,0:T(8,128)} %get-tuple-element.39), channel_id=1, source_target_pairs={{0,5},{1,6},{2,7},{3,0},{4,1},{5,2},{6,3},{7,4},{8,13},{9,14},{10,... | collective-permute-start | bytes 393224 | tf_op jit(solution)/shard_map/ppermute | solution.py:317
  14.4 7.0 %collective-permute-start.6 = (f32[2,128,128]{2,1,0:T(8,128)}, f32[2,128,128]{2,1,0:T(8,128)S(1)}, u32[]{:S(2)}, u32[]{:S(2)}) collective-permute-start(f32[2,128,128]{2,1,0:T(8,128)} %get-tuple-element.40), channel_id=1, source_target_pairs={{0,6},{1,7},{2,0},{3,1},{4,2},{5,3},{6,4},{7,5},{8,14},{9,15},{10,... | collective-permute-start | bytes 393224 | tf_op jit(solution)/shard_map/ppermute | solution.py:317

commit v8 on v7

--- a/solution.py
+++ b/solution.py
@@ -19,8 +19,13 @@
     return high, (x - high.astype(F32)).astype(BF16)
 
 
-def split_body(fac, f_pair, f_turn):
+def split_body(pair_region, factors, f_pair, f_turn, fac, sem, *, per_home):
     slots, n, _ = fac.shape
+    pair = lax.axis_index("pair") * per_home + lax.axis_index("virt")
+    region = pair_region[lax.rem(pair, pair_region.shape[0])]
+    copy = pltpu.make_async_copy(factors.at[region], fac, sem)
+    copy.start()
+    copy.wait()
     for l in range(slots):
         tile = fac[l]
         rows = slice(l * n, (l + 1) * n)
@@ -28,44 +33,37 @@
         f_turn[rows, :n], f_turn[rows, n:] = halves(tile.T)
 
 
-def split_factors(factors):
-    slots, n, _ = factors.shape
+def split_factors(pair_region, factors, per_home):
+    _, slots, n, _ = factors.shape
     shape = jax.ShapeDtypeStruct((slots * n, 2 * n), BF16)
-    spec = pl.BlockSpec(shape.shape, lambda i: (0, 0))
-    return pl.pallas_call(
-        split_body,
+    spec = pl.BlockSpec(shape.shape, lambda i, *_: (0, 0))
+    return pl.pallas_call(
+        functools.partial(split_body, per_home=per_home),
         out_shape=[shape, shape],
-        grid=(1,),
-        in_specs=[pl.BlockSpec((slots, n, n), lambda i: (0, 0, 0))],
-        out_specs=[spec, spec],
+        grid_spec=pltpu.PrefetchScalarGridSpec(
+            num_scalar_prefetch=1,
+            grid=(1,),
+            in_specs=[pl.BlockSpec(memory_space=pltpu.HBM)],
+            out_specs=[spec, spec],
+            scratch_shapes=[pltpu.VMEM((slots, n, n), F32), pltpu.SemaphoreType.DMA(())],
+        ),
         compiler_params=pltpu.CompilerParams(vmem_limit_bytes=16 << 20),
         cost_estimate=pl.CostEstimate(flops=1 << 20, bytes_accessed=3 << 20, transcendentals=0),
         name="split_factors",
-    )(factors)
+    )(pair_region, pltpu.with_memory_space_constraint(factors, pltpu.HBM))
 
 
 def deal_body(source, *refs):
-    outs, held, sems = refs[:-2], refs[-2], refs[-1]
+    outs, sems = refs[:-1], refs[-1]
     count = len(outs)
-    local = source.shape[0]
-    taken, given = [], []
+    copies = []
     for d, out in enumerate(outs):
         to = lax.rem(lax.axis_index("virt") + d, count)
-        taken.append(
-            [
-                pltpu.make_async_copy(source.at[i, to], held.at[d, i], sems.at[d, i])
-                for i in range(local)
-            ]
-        )
-        given.append(pltpu.make_async_copy(held.at[d], out, sems.at[d, local]))
-    for copies in taken:
-        for copy in copies:
-            copy.start()
-    for copies, copy in zip(taken, given):
-        for each in copies:
-            each.wait()
+        for i in range(out.shape[0]):
+            copies.append(pltpu.make_async_copy(source.at[i, to], out.at[i], sems.at[d, i]))
+    for copy in copies:
         copy.start()
-    for copy in given:
+    for copy in copies:
         copy.wait()
 
 
@@ -77,14 +75,11 @@
         out_shape=[jax.ShapeDtypeStruct((local, n, n), F32)] * count,
         in_specs=[anywhere],
         out_specs=[anywhere] * count,
-        scratch_shapes=[
-            pltpu.VMEM((count, local, n, n), F32),
-            pltpu.SemaphoreType.DMA((count, local + 1)),
-        ],
-        compiler_params=pltpu.CompilerParams(vmem_limit_bytes=56 << 20),
+        scratch_shapes=[pltpu.SemaphoreType.DMA((count, local))],
+        compiler_params=pltpu.CompilerParams(vmem_limit_bytes=4 << 20),
         cost_estimate=pl.CostEstimate(flops=0, bytes_accessed=2 << 20, transcendentals=0),
         name="deal",
-    )(amplitudes)
+    )(pltpu.with_memory_space_constraint(amplitudes, pltpu.HBM))
 
 
 def ladder_body(
@@ -322,8 +317,10 @@
 
     pair = my_pair * per_home + my_virt
     mirrored = (pair >= half).astype(jnp.int32)
-    region = pair_region[pair % half]
-    rows = integral_quadruple_table[region]
+    mine = jnp.arange(half) == lax.rem(pair, half)
+    region = jnp.sum(jnp.where(mine, pair_region, 0))
+    here = jnp.arange(integral_quadruple_table.shape[0]) == region
+    rows = jnp.sum(jnp.where(here[:, None, None, None], integral_quadruple_table, 0), axis=0)
     o, left, right = rows[..., 0], rows[..., 1], rows[..., 2]
     partner = jnp.where(o < OFF_DIAG, o ^ 1, o)
     codes = jnp.where(
@@ -345,7 +342,7 @@
     plain = jnp.sum((owner_map[:half] == my_pair).astype(jnp.int32))
     held = plain.reshape(1)
 
-    f_pair, f_turn = split_factors(lax.dynamic_index_in_dim(factors, region, 0, keepdims=False))
+    f_pair, f_turn = split_factors(pair_region, factors, per_home)
     amps, codes, touched, f_pair, f_turn, spot, held = lax.optimization_barrier(
         (amps, codes, touched, f_pair, f_turn, spot, held)
     )

time: 137 us -> 137 us (level)
  other arithmetic: 3.24 us -> 6.19 us
  local copies, waits for them, and re-layouts: 3.01 us -> 1.06 us
  between operations: 2.06 us -> 0.13 us
    reduce_sum x0 -> x2, other arithmetic: none -> 2.29 us  [the longest x1 1.29 us: on_device(): region = jnp.sum(jnp.where(mine, pair_region, 0))]
    pallas_call x1, Pallas kernels: 0.36 us -> 2.15 us  [split_factors(): pl.pallas_call(functools.partial(split_body, per_home=per_home), out_shap...]
  transfers between devices with their start and end apart: 7 -> 7, of which waited for: 0 -> 0; matrix products, arithmetic and copies ran while one was open for 5% -> 5% of each run, Pallas kernels for 0% -> 2%
where the time goes in v8:
time: 137 us; the launch traced here: 136 us
  blocking collectives  99.1 us (72%)
  Pallas kernels  19.1 us (14%)
  starting transfers between devices  10.5 us (8%)
  other arithmetic  6.19 us (5%)
    all_to_all x1, blocking collectives, on_device(): lax.all_to_all(joined, 'pair', split_axis=0, concat_axis=0, tiled=True)  56.1 us
    all_to_all x1, blocking collectives, on_device(): lax.all_to_all(sheets, ('virt', 'pair'), split_axis=0, concat_axis=0, til...  43 us
    pallas_call x1, Pallas kernels, ladder(): pl.pallas_call(ladder_body, out_shape=jax.ShapeDtypeStruct((slots, n, n),...  12.1 us
    ppermute x7, starting transfers between devices, on_device(): amps[d] = lax.ppermute(pieces[d], 'virt', route)  10.5 us
  transfers between devices with their start and end apart: 7, of which 0 were waited for; matrix products, arithmetic and copies ran while one was open for 5% of the time, Pallas kernels for 2%

profile of v8, /device:TPU:2, one launch (start us, length us, event | category | flops | bytes accessed | tf_op | source)
XLA Modules:
  0.0 136.2 jit_solution(16025859075964151095)
XLA Ops:
  0.0 1.4 %deal.1 = (f32[2,128,128]{2,1,0:T(8,128)S(1)}, f32[2,128,128]{2,1,0:T(8,128)S(1)}, f32[2,128,128]{2,1,0:T(8,128)S(1)}, f32[2,128,128]{2,1,0:T(8,128)S(1)}, f32[2...) custom-call(f32[2,8,128,128]{3,2,1,0:T(8,128)} %source.1), custom_call_target="tpu_custom_call" | custom-call | bytes 2097152 | tf_op jit(solution)/shard_map/deal/pallas_call | solution.py:73
  1.4 0.0 collective-permute-start
  1.4 2.9 %collective-permute-start.1 = (f32[2,128,128]{2,1,0:T(8,128)S(1)}, f32[2,128,128]{2,1,0:T(8,128)S(1)}, u32[]{:S(2)}, u32[]{:S(2)}) collective-permute-start(f32[2,128,128]{2,1,0:T(8,128)S(1)} %get-tuple-element.34), channel_id=1, source_target_pairs={{0,7},{1,0},{2,1},{3,2},{4,3},{5,4},{6,5},{7,6},{8,15},{9,8},{10,9... | collective-permute-start | bytes 393224 | tf_op jit(solution)/shard_map/ppermute | solution.py:312
  4.3 0.4 collective-permute-start.2
  4.7 0.6 collective-permute-start.3
  5.3 2.4 %collective-permute-start.4 = (f32[2,128,128]{2,1,0:T(8,128)S(1)}, f32[2,128,128]{2,1,0:T(8,128)S(1)}, u32[]{:S(2)}, u32[]{:S(2)}) collective-permute-start(f32[2,128,128]{2,1,0:T(8,128)S(1)} %get-tuple-element.38), channel_id=1, source_target_pairs={{0,4},{1,5},{2,6},{3,7},{4,0},{5,1},{6,2},{7,3},{8,12},{9,13},{10,... | collective-permute-start | bytes 393224 | tf_op jit(solution)/shard_map/ppermute | solution.py:312
  7.7 0.9 convert_reduce_fusion
  8.6 0.7 multiply_add_fusion.spot
  9.3 1.4 %fusion.16 = s32[]{:T(128)} fusion(s32[256]{0:T(256)} %param.9, s32[]{:T(128)S(6)} %axis_index.23), kind=kLoop, calls=%fused_computation.29 | loop fusion | flops 383 | bytes 520 | tf_op jit(solution)/shard_map/reduce_sum | solution.py:342
  10.7 0.0 collective-permute-done.refs_1_
  10.7 2.9 %collective-permute-start.5 = (f32[2,128,128]{2,1,0:T(8,128)S(1)}, f32[2,128,128]{2,1,0:T(8,128)S(1)}, u32[]{:S(2)}, u32[]{:S(2)}) collective-permute-start(f32[2,128,128]{2,1,0:T(8,128)S(1)} %get-tuple-element.39), channel_id=1, source_target_pairs={{0,5},{1,6},{2,7},{3,0},{4,1},{5,2},{6,3},{7,4},{8,13},{9,14},{10,... | collective-permute-start | bytes 393224 | tf_op jit(solution)/shard_map/ppermute | solution.py:312
  13.6 0.0 collective-permute-done.1.refs_7_
  13.6 1.3 collective-permute-start.6
  15.0 1.3 fusion.15
  16.3 0.6 iota_compare_fusion.2
  16.9 1.0 select_reduce_fusion
  17.9 0.1 squeeze.18
  18.0 0.1 squeeze.20
  18.1 0.1 squeeze.19
  18.2 0.2 fusion.3
  18.4 0.1 select_n.59
  18.5 0.1 reshape.113.touched
  18.6 0.0 copy-start
  18.6 0.7 copy-done
  19.2 2.1 %split_factors.1 = (bf16[2048,256]{1,0:T(8,128)(2,1)S(1)}, bf16[2048,256]{1,0:T(8,128)(2,1)S(1)}) custom-call(s32[128]{0:T(128)S(1)} %copy-done, f32[6,16,128,128]{3,2,1,0:T(8,128)} %factors.1), custom_call_target="tpu_custom_call" | custom-call | flops 1048576 | bytes 3145728 | tf_op jit(solution)/shard_map/split_factors/pallas_call | solution.py:40
  21.4 0.0 collective-permute-done.2.refs_2_
  21.4 0.0 collective-permute-done.3.refs_3_
  21.4 0.0 collective-permute-done.4.refs_4_
  21.4 0.0 collective-permute-done.5.refs_5_
  21.4 0.0 collective-permute-done.6.refs_6_
  21.5 12.1 %ladder.1 = f32[16,128,128]{2,1,0:T(8,128)S(1)} custom-call(s32[16,16]{1,0:T(8,128)S(1)} %fusion.8.codes, s32[16,16]{1,0:T(8,128)S(1)} %reshape.113.touched, f32[2,128,128]{2,1,0:T(8,128)S(1)} %get-tuple-element.49.refs_0_, f32[2,128,128]{2,1,0:T(8,128)S(1)} %collective-permute-done.refs_1_, f32[2,128,128]{2,1,0:T(8,128)S(1)} %collective-permute-done.2.refs_2_, ...), custom_call_target="tpu_custom_call" | custom-call | flops 6442450944 | bytes 4194304 | tf_op jit(solution)/shard_map/ladder/pallas_call | solution.py:184
  33.5 43.0 %all_to_all.10.blocks = f32[256,8,128]{2,1,0:T(8,128)S(1)} all-to-all(f32[256,8,128]{2,1,0:T(8,128)S(1)} %bitcast.29), channel_id=1, replica_groups=mesh['pair'=32,'virt'=8] {'virt','pair'}, dimensions={0} | all-to-all | bytes 2097152 | tf_op jit(solution)/shard_map/all_to_all | solution.py:351
  76.5 1.0 join_pairs.1
  77.6 56.1 %all_to_all.11 = f32[512,8,128]{2,1,0:T(8,128)S(1)} all-to-all(f32[512,8,128]{2,1,0:T(8,128)S(1)} %join_pairs.1), channel_id=1, replica_groups=mesh['pair'=32,'virt'=8] {'pair'}, dimensions={0} | all-to-all | bytes 4194304 | tf_op jit(solution)/shard_map/all_to_all | solution.py:353
  133.7 2.5 %settle.1 = f32[2,16,128,128]{3,2,1,0:T(8,128)} custom-call(s32[1]{0:T(128)} %bitcast.3.held, f32[32,16,8,128]{3,2,1,0:T(8,128)S(1)} %bitcast.28), custom_call_target="tpu_custom_call" | custom-call | flops 262144 | bytes 4194304 | tf_op jit(solution)/shard_map/settle/pallas_call | solution.py:279
  (5 shorter events, 0.0 us)
Async XLA Ops:
  1.4 9.3 %collective-permute-start = (f32[2,128,128]{2,1,0:T(8,128)S(1)}, f32[2,128,128]{2,1,0:T(8,128)S(1)}, u32[]{:S(2)}, u32[]{:S(2)}) collective-permute-start(f32[2,128,128]{2,1,0:T(8,128)S(1)} %get-tuple-element.33), channel_id=1, source_target_pairs={{0,1},{1,2},{2,3},{3,4},{4,5},{5,6},{6,7},{7,0},{8,9},{9,10},{10,1... | collective-permute-start | bytes 393224 | tf_op jit(solution)/shard_map/ppermute | solution.py:312
  1.4 12.2 %collective-permute-start.1 = (f32[2,128,128]{2,1,0:T(8,128)S(1)}, f32[2,128,128]{2,1,0:T(8,128)S(1)}, u32[]{:S(2)}, u32[]{:S(2)}) collective-permute-start(f32[2,128,128]{2,1,0:T(8,128)S(1)} %get-tuple-element.34), channel_id=1, source_target_pairs={{0,7},{1,0},{2,1},{3,2},{4,3},{5,4},{6,5},{7,6},{8,15},{9,8},{10,9... | collective-permute-start | bytes 393224 | tf_op jit(solution)/shard_map/ppermute | solution.py:312
  4.3 17.1 %collective-permute-start.2 = (f32[2,128,128]{2,1,0:T(8,128)S(1)}, f32[2,128,128]{2,1,0:T(8,128)S(1)}, u32[]{:S(2)}, u32[]{:S(2)}) collective-permute-start(f32[2,128,128]{2,1,0:T(8,128)S(1)} %get-tuple-element.36), channel_id=1, source_target_pairs={{0,2},{1,3},{2,4},{3,5},{4,6},{5,7},{6,0},{7,1},{8,10},{9,11},{10,... | collective-permute-start | bytes 393224 | tf_op jit(solution)/shard_map/ppermute | solution.py:312
  4.7 16.7 %collective-permute-start.3 = (f32[2,128,128]{2,1,0:T(8,128)S(1)}, f32[2,128,128]{2,1,0:T(8,128)S(1)}, u32[]{:S(2)}, u32[]{:S(2)}) collective-permute-start(f32[2,128,128]{2,1,0:T(8,128)S(1)} %get-tuple-element.37), channel_id=1, source_target_pairs={{0,3},{1,4},{2,5},{3,6},{4,7},{5,0},{6,1},{7,2},{8,11},{9,12},{10,... | collective-permute-start | bytes 393224 | tf_op jit(solution)/shard_map/ppermute | solution.py:312
  5.3 16.2 %collective-permute-start.4 = (f32[2,128,128]{2,1,0:T(8,128)S(1)}, f32[2,128,128]{2,1,0:T(8,128)S(1)}, u32[]{:S(2)}, u32[]{:S(2)}) collective-permute-start(f32[2,128,128]{2,1,0:T(8,128)S(1)} %get-tuple-element.38), channel_id=1, source_target_pairs={{0,4},{1,5},{2,6},{3,7},{4,0},{5,1},{6,2},{7,3},{8,12},{9,13},{10,... | collective-permute-start | bytes 393224 | tf_op jit(solution)/shard_map/ppermute | solution.py:312
  10.7 10.8 %collective-permute-start.5 = (f32[2,128,128]{2,1,0:T(8,128)S(1)}, f32[2,128,128]{2,1,0:T(8,128)S(1)}, u32[]{:S(2)}, u32[]{:S(2)}) collective-permute-start(f32[2,128,128]{2,1,0:T(8,128)S(1)} %get-tuple-element.39), channel_id=1, source_target_pairs={{0,5},{1,6},{2,7},{3,0},{4,1},{5,2},{6,3},{7,4},{8,13},{9,14},{10,... | collective-permute-start | bytes 393224 | tf_op jit(solution)/shard_map/ppermute | solution.py:312
  13.6 7.8 %collective-permute-start.6 = (f32[2,128,128]{2,1,0:T(8,128)S(1)}, f32[2,128,128]{2,1,0:T(8,128)S(1)}, u32[]{:S(2)}, u32[]{:S(2)}) collective-permute-start(f32[2,128,128]{2,1,0:T(8,128)S(1)} %get-tuple-element.40), channel_id=1, source_target_pairs={{0,6},{1,7},{2,0},{3,1},{4,2},{5,3},{6,4},{7,5},{8,14},{9,15},{10,... | collective-permute-start | bytes 393224 | tf_op jit(solution)/shard_map/ppermute | solution.py:312
  18.6 0.7 copy-start

commit v9 on v8

--- a/solution.py
+++ b/solution.py
@@ -53,33 +53,37 @@
     )(pair_region, pltpu.with_memory_space_constraint(factors, pltpu.HBM))
 
 
-def deal_body(source, *refs):
-    outs, sems = refs[:-1], refs[-1]
+def deal_body(source, pair_region, owner_map, *refs):
+    *outs, regions, owners, sems, small = refs
     count = len(outs)
     copies = []
     for d, out in enumerate(outs):
         to = lax.rem(lax.axis_index("virt") + d, count)
         for i in range(out.shape[0]):
             copies.append(pltpu.make_async_copy(source.at[i, to], out.at[i], sems.at[d, i]))
+    copies.append(pltpu.make_async_copy(pair_region, regions, small.at[0]))
+    copies.append(pltpu.make_async_copy(owner_map, owners, small.at[1]))
     for copy in copies:
         copy.start()
     for copy in copies:
         copy.wait()
 
 
-def deal(amplitudes):
+def deal(amplitudes, pair_region, owner_map):
     local, count, n, _ = amplitudes.shape
     anywhere = pl.BlockSpec(memory_space=pl.ANY)
-    return pl.pallas_call(
+    *pieces, regions, owners = pl.pallas_call(
         deal_body,
-        out_shape=[jax.ShapeDtypeStruct((local, n, n), F32)] * count,
-        in_specs=[anywhere],
-        out_specs=[anywhere] * count,
-        scratch_shapes=[pltpu.SemaphoreType.DMA((count, local))],
+        out_shape=[jax.ShapeDtypeStruct((local, n, n), F32)] * count
+        + [jax.ShapeDtypeStruct(x.shape, x.dtype) for x in (pair_region, owner_map)],
+        in_specs=[anywhere] * 3,
+        out_specs=[anywhere] * (count + 2),
+        scratch_shapes=[pltpu.SemaphoreType.DMA((count, local)), pltpu.SemaphoreType.DMA((2,))],
         compiler_params=pltpu.CompilerParams(vmem_limit_bytes=4 << 20),
         cost_estimate=pl.CostEstimate(flops=0, bytes_accessed=2 << 20, transcendentals=0),
         name="deal",
-    )(pltpu.with_memory_space_constraint(amplitudes, pltpu.HBM))
+    )(*(pltpu.with_memory_space_constraint(x, pltpu.HBM) for x in (amplitudes, pair_region, owner_map)))
+    return pieces, regions, owners
 
 
 def ladder_body(
@@ -305,13 +309,15 @@
     half = pair_total // 2
     own_most = 2 * per_home
 
-    pieces = deal(amplitudes)
+    pieces, pair_region, owner_map = deal(amplitudes, pair_region, owner_map)
     amps = {0: pieces[0]}
     for d in sorted(range(1, virt_count), key=lambda d: -min(d, virt_count - d)):
         route = [(i, (i + d) % virt_count) for i in range(virt_count)]
         amps[d] = lax.ppermute(pieces[d], "virt", route)
     near = (1, virt_count - 1)
-    pair_region, *first = lax.optimization_barrier((pair_region, *(amps[d] for d in near)))
+    pair_region, owner_map, *first = lax.optimization_barrier(
+        (pair_region, owner_map, *(amps[d] for d in near))
+    )
     amps.update(zip(near, first))
     amps = [amps[d] for d in range(virt_count)]
 

time: 137 us -> 135 us (0.985)
  other arithmetic: 6.19 us -> 3.43 us
  transfers between devices with their start and end apart: 7 -> 7, of which waited for: 0 -> 1; matrix products, arithmetic and copies ran while one was open for 5% -> 3% of each run, Pallas kernels for 2% -> 2%
where the time goes in v9:
time: 135 us
  blocking collectives  100 us (74%)
  Pallas kernels  19.2 us (14%)
  starting transfers between devices  10.5 us (8%)
  other arithmetic  3.43 us (3%)
    all_to_all x1, blocking collectives, on_device(): lax.all_to_all(joined, 'pair', split_axis=0, concat_axis=0, tiled=True)  56.1 us
    all_to_all x1, blocking collectives, on_device(): lax.all_to_all(sheets, ('virt', 'pair'), split_axis=0, concat_axis=0, til...  44.1 us
    pallas_call x1, Pallas kernels, ladder(): pl.pallas_call(ladder_body, out_shape=jax.ShapeDtypeStruct((slots, n, n),...  12.1 us
    ppermute x7, starting transfers between devices, on_device(): amps[d] = lax.ppermute(pieces[d], 'virt', route)  10.5 us
  transfers between devices with their start and end apart: 7, of which 1 were waited for; matrix products, arithmetic and copies ran while one was open for 3% of the time, Pallas kernels for 2%

profile of v9, /device:TPU:2, one launch (start us, length us, event | category | flops | bytes accessed | tf_op | source)
XLA Modules:
  0.0 134.6 jit_solution(16273018192498920467)
XLA Ops:
  0.0 1.4 %deal.1 = (f32[2,128,128]{2,1,0:T(8,128)S(1)}, f32[2,128,128]{2,1,0:T(8,128)S(1)}, f32[2,128,128]{2,1,0:T(8,128)S(1)}, f32[2,128,128]{2,1,0:T(8,128)S(1)}, f32[2...) custom-call(f32[2,8,128,128]{3,2,1,0:T(8,128)} %source.1, ...), custom_call_target="tpu_custom_call" | custom-call | bytes 2097152 | tf_op jit(solution)/shard_map/deal/pallas_call | solution.py:75
  1.4 0.0 collective-permute-start
  1.4 2.9 %collective-permute-start.1 = (f32[2,128,128]{2,1,0:T(8,128)S(1)}, f32[2,128,128]{2,1,0:T(8,128)S(1)}, u32[]{:S(2)}, u32[]{:S(2)}) collective-permute-start(f32[2,128,128]{2,1,0:T(8,128)S(1)} %get-tuple-element.39), channel_id=1, source_target_pairs={{0,7},{1,0},{2,1},{3,2},{4,3},{5,4},{6,5},{7,6},{8,15},{9,8},{10,9... | collective-permute-start | bytes 393224 | tf_op jit(solution)/shard_map/ppermute | solution.py:316
  4.4 0.4 collective-permute-start.2
  4.7 0.6 collective-permute-start.3
  5.3 2.4 %collective-permute-start.4 = (f32[2,128,128]{2,1,0:T(8,128)S(1)}, f32[2,128,128]{2,1,0:T(8,128)S(1)}, u32[]{:S(2)}, u32[]{:S(2)}) collective-permute-start(f32[2,128,128]{2,1,0:T(8,128)S(1)} %get-tuple-element.43), channel_id=1, source_target_pairs={{0,4},{1,5},{2,6},{3,7},{4,0},{5,1},{6,2},{7,3},{8,12},{9,13},{10,... | collective-permute-start | bytes 393224 | tf_op jit(solution)/shard_map/ppermute | solution.py:316
  7.7 0.0 collective-permute-done.refs_1_
  7.7 2.9 %collective-permute-start.5 = (f32[2,128,128]{2,1,0:T(8,128)S(1)}, f32[2,128,128]{2,1,0:T(8,128)S(1)}, u32[]{:S(2)}, u32[]{:S(2)}) collective-permute-start(f32[2,128,128]{2,1,0:T(8,128)S(1)} %get-tuple-element.44), channel_id=1, source_target_pairs={{0,5},{1,6},{2,7},{3,0},{4,1},{5,2},{6,3},{7,4},{8,13},{9,14},{10,... | collective-permute-start | bytes 393224 | tf_op jit(solution)/shard_map/ppermute | solution.py:316
  10.6 0.0 collective-permute-done.1.refs_7_
  10.6 1.3 %collective-permute-start.6 = (f32[2,128,128]{2,1,0:T(8,128)S(1)}, f32[2,128,128]{2,1,0:T(8,128)S(1)}, u32[]{:S(2)}, u32[]{:S(2)}) collective-permute-start(f32[2,128,128]{2,1,0:T(8,128)S(1)} %get-tuple-element.45), channel_id=1, source_target_pairs={{0,6},{1,7},{2,0},{3,1},{4,2},{5,3},{6,4},{7,5},{8,14},{9,15},{10,... | collective-permute-start | bytes 393224 | tf_op jit(solution)/shard_map/ppermute | solution.py:316
  12.0 0.6 fusion.15
  12.6 0.6 iota_compare_fusion.2
  13.3 0.2 convert_reduce_fusion
  13.4 1.0 select_reduce_fusion
  14.5 0.1 squeeze.18
  14.5 0.1 squeeze.20
  14.6 0.1 squeeze.19
  14.7 0.2 fusion.3
  14.9 0.1 select_n.59
  15.1 0.1 reshape.113.touched
  15.1 2.2 %split_factors.1 = (bf16[2048,256]{1,0:T(8,128)(2,1)S(1)}, bf16[2048,256]{1,0:T(8,128)(2,1)S(1)}) custom-call(s32[128]{0:T(128)S(1)} %get-tuple-element.47.pair_region, f32[6,16,128,128]{3,2,1,0:T(8,128)} %factors.1), custom_call_target="tpu_custom_call" | custom-call | flops 1048576 | bytes 3145728 | tf_op jit(solution)/shard_map/split_factors/pallas_call | solution.py:40
  17.3 0.7 fusion.16
  18.0 0.0 collective-permute-done.2.refs_2_
  18.0 0.0 collective-permute-done.3.refs_3_
  18.0 0.0 collective-permute-done.4.refs_4_
  18.0 0.0 collective-permute-done.5.refs_5_
  18.0 0.6 collective-permute-done.6.refs_6_
  18.7 12.1 %ladder.1 = f32[16,128,128]{2,1,0:T(8,128)S(1)} custom-call(s32[16,16]{1,0:T(8,128)S(1)} %fusion.8.codes, s32[16,16]{1,0:T(8,128)S(1)} %reshape.113.touched, f32[2,128,128]{2,1,0:T(8,128)S(1)} %get-tuple-element.55.refs_0_, f32[2,128,128]{2,1,0:T(8,128)S(1)} %collective-permute-done.refs_1_, f32[2,128,128]{2,1,0:T(8,128)S(1)} %collective-permute-done.2.refs_2_, ...), custom_call_target="tpu_custom_call" | custom-call | flops 6442450944 | bytes 4194304 | tf_op jit(solution)/shard_map/ladder/pallas_call | solution.py:188
  30.8 44.1 %all_to_all.10.blocks = f32[256,8,128]{2,1,0:T(8,128)S(1)} all-to-all(f32[256,8,128]{2,1,0:T(8,128)S(1)} %bitcast.29), channel_id=1, replica_groups=mesh['pair'=32,'virt'=8] {'virt','pair'}, dimensions={0} | all-to-all | bytes 2097152 | tf_op jit(solution)/shard_map/all_to_all | solution.py:357
  74.9 1.0 join_pairs.1
  75.9 56.1 %all_to_all.11 = f32[512,8,128]{2,1,0:T(8,128)S(1)} all-to-all(f32[512,8,128]{2,1,0:T(8,128)S(1)} %join_pairs.1), channel_id=1, replica_groups=mesh['pair'=32,'virt'=8] {'pair'}, dimensions={0} | all-to-all | bytes 4194304 | tf_op jit(solution)/shard_map/all_to_all | solution.py:359
  132.0 2.6 %settle.1 = f32[2,16,128,128]{3,2,1,0:T(8,128)} custom-call(s32[1]{0:T(128)} %bitcast.3.held, f32[32,16,8,128]{3,2,1,0:T(8,128)S(1)} %bitcast.28), custom_call_target="tpu_custom_call" | custom-call | flops 262144 | bytes 4194304 | tf_op jit(solution)/shard_map/settle/pallas_call | solution.py:283
  (6 shorter events, 0.0 us)
Async XLA Ops:
  1.4 6.3 %collective-permute-start = (f32[2,128,128]{2,1,0:T(8,128)S(1)}, f32[2,128,128]{2,1,0:T(8,128)S(1)}, u32[]{:S(2)}, u32[]{:S(2)}) collective-permute-start(f32[2,128,128]{2,1,0:T(8,128)S(1)} %get-tuple-element.38), channel_id=1, source_target_pairs={{0,1},{1,2},{2,3},{3,4},{4,5},{5,6},{6,7},{7,0},{8,9},{9,10},{10,1... | collective-permute-start | bytes 393224 | tf_op jit(solution)/shard_map/ppermute | solution.py:316
  1.4 9.2 %collective-permute-start.1 = (f32[2,128,128]{2,1,0:T(8,128)S(1)}, f32[2,128,128]{2,1,0:T(8,128)S(1)}, u32[]{:S(2)}, u32[]{:S(2)}) collective-permute-start(f32[2,128,128]{2,1,0:T(8,128)S(1)} %get-tuple-element.39), channel_id=1, source_target_pairs={{0,7},{1,0},{2,1},{3,2},{4,3},{5,4},{6,5},{7,6},{8,15},{9,8},{10,9... | collective-permute-start | bytes 393224 | tf_op jit(solution)/shard_map/ppermute | solution.py:316
  4.4 13.6 %collective-permute-start.2 = (f32[2,128,128]{2,1,0:T(8,128)S(1)}, f32[2,128,128]{2,1,0:T(8,128)S(1)}, u32[]{:S(2)}, u32[]{:S(2)}) collective-permute-start(f32[2,128,128]{2,1,0:T(8,128)S(1)} %get-tuple-element.41), channel_id=1, source_target_pairs={{0,2},{1,3},{2,4},{3,5},{4,6},{5,7},{6,0},{7,1},{8,10},{9,11},{10,... | collective-permute-start | bytes 393224 | tf_op jit(solution)/shard_map/ppermute | solution.py:316
  4.7 13.3 %collective-permute-start.3 = (f32[2,128,128]{2,1,0:T(8,128)S(1)}, f32[2,128,128]{2,1,0:T(8,128)S(1)}, u32[]{:S(2)}, u32[]{:S(2)}) collective-permute-start(f32[2,128,128]{2,1,0:T(8,128)S(1)} %get-tuple-element.42), channel_id=1, source_target_pairs={{0,3},{1,4},{2,5},{3,6},{4,7},{5,0},{6,1},{7,2},{8,11},{9,12},{10,... | collective-permute-start | bytes 393224 | tf_op jit(solution)/shard_map/ppermute | solution.py:316
  5.3 12.7 %collective-permute-start.4 = (f32[2,128,128]{2,1,0:T(8,128)S(1)}, f32[2,128,128]{2,1,0:T(8,128)S(1)}, u32[]{:S(2)}, u32[]{:S(2)}) collective-permute-start(f32[2,128,128]{2,1,0:T(8,128)S(1)} %get-tuple-element.43), channel_id=1, source_target_pairs={{0,4},{1,5},{2,6},{3,7},{4,0},{5,1},{6,2},{7,3},{8,12},{9,13},{10,... | collective-permute-start | bytes 393224 | tf_op jit(solution)/shard_map/ppermute | solution.py:316
  7.7 10.3 %collective-permute-start.5 = (f32[2,128,128]{2,1,0:T(8,128)S(1)}, f32[2,128,128]{2,1,0:T(8,128)S(1)}, u32[]{:S(2)}, u32[]{:S(2)}) collective-permute-start(f32[2,128,128]{2,1,0:T(8,128)S(1)} %get-tuple-element.44), channel_id=1, source_target_pairs={{0,5},{1,6},{2,7},{3,0},{4,1},{5,2},{6,3},{7,4},{8,13},{9,14},{10,... | collective-permute-start | bytes 393224 | tf_op jit(solution)/shard_map/ppermute | solution.py:316
  10.6 8.0 %collective-permute-start.6 = (f32[2,128,128]{2,1,0:T(8,128)S(1)}, f32[2,128,128]{2,1,0:T(8,128)S(1)}, u32[]{:S(2)}, u32[]{:S(2)}) collective-permute-start(f32[2,128,128]{2,1,0:T(8,128)S(1)} %get-tuple-element.45), channel_id=1, source_target_pairs={{0,6},{1,7},{2,0},{3,1},{4,2},{5,3},{6,4},{7,5},{8,14},{9,15},{10,... | collective-permute-start | bytes 393224 | tf_op jit(solution)/shard_map/ppermute | solution.py:316

commit v10 on v9

--- a/solution.py
+++ b/solution.py
@@ -87,7 +87,7 @@
 
 
 def ladder_body(
-    codes, touched, *refs
+    codes, touched, *refs, steps
 ):
     f_pair, f_turn, out, amp_high, amp_low, prod_a, prod_b, grouped = refs[-8:]
     amps = refs[:-8]
@@ -102,7 +102,7 @@
         amp_low[v, :, i * n : (i + 1) * n] = low
 
     count = len(amps)
-    origins = [lax.rem(lax.axis_index("virt") + (count - d), count) for d in range(count)]
+    origins = [lax.rem(lax.axis_index("virt") + (count - d), count) for d in steps]
 
     @pl.when(mirrored == 0)
     def _():
@@ -178,7 +178,7 @@
         out[g : g + step] = total.reshape(step, n, n)
 
 
-def ladder(codes, touched, amps, f_pair, f_turn):
+def ladder(codes, touched, amps, steps, f_pair, f_turn):
     local, n, _ = amps[0].shape
     slots = local * len(amps)
     wide = slots * n
@@ -186,7 +186,7 @@
     whole = pl.BlockSpec((slots, n, n), lambda i, *_: (0, 0, 0))
     table = pl.BlockSpec((wide, 2 * n), lambda i, *_: (0, 0))
     return pl.pallas_call(
-        ladder_body,
+        functools.partial(ladder_body, steps=steps),
         out_shape=jax.ShapeDtypeStruct((slots, n, n), F32),
         grid_spec=pltpu.PrefetchScalarGridSpec(
             num_scalar_prefetch=2,
@@ -319,7 +319,8 @@
         (pair_region, owner_map, *(amps[d] for d in near))
     )
     amps.update(zip(near, first))
-    amps = [amps[d] for d in range(virt_count)]
+    steps = (0, *near, *sorted(set(range(1, virt_count)) - set(near), key=lambda d: -min(d, virt_count - d)))
+    amps = [amps[d] for d in steps]
 
     pair = my_pair * per_home + my_virt
     mirrored = (pair >= half).astype(jnp.int32)
@@ -352,7 +353,7 @@
     amps, codes, touched, f_pair, f_turn, spot, held = lax.optimization_barrier(
         (amps, codes, touched, f_pair, f_turn, spot, held)
     )
-    result = ladder(codes, touched, amps, f_pair, f_turn)
+    result = ladder(codes, touched, amps, steps, f_pair, f_turn)
     sheets = result.reshape(virt_count * pair_count, -1, n)
     spread = lax.all_to_all(sheets, ("virt", "pair"), split_axis=0, concat_axis=0, tiled=True)
     joined = join_pairs(spot, spread, pair_count * own_most, per_home)

time: 135 us -> 134 us (level)
  transfers between devices with their start and end apart: 7 -> 7, of which waited for: 1 -> 0; matrix products, arithmetic and copies ran while one was open for 3% -> 3% of each run, Pallas kernels for 2% -> 2%
where the time goes in v10:
time: 134 us
  blocking collectives  99.4 us (74%)
  Pallas kernels  19.2 us (14%)
  starting transfers between devices  11.4 us (9%)
  other arithmetic  3.43 us (3%)
    all_to_all x1, blocking collectives, on_device(): lax.all_to_all(joined, 'pair', split_axis=0, concat_axis=0, tiled=True)  56.1 us
    all_to_all x1, blocking collectives, on_device(): lax.all_to_all(sheets, ('virt', 'pair'), split_axis=0, concat_axis=0, til...  43.2 us
    pallas_call x1, Pallas kernels, ladder(): pl.pallas_call(functools.partial(ladder_body, steps=steps), out_shape=jax...  12.1 us
    ppermute x7, starting transfers between devices, on_device(): amps[d] = lax.ppermute(pieces[d], 'virt', route)  11.4 us
  transfers between devices with their start and end apart: 7, of which 0 were waited for; matrix products, arithmetic and copies ran while one was open for 3% of the time, Pallas kernels for 2%

profile of v10, /device:TPU:2, one launch (start us, length us, event | category | flops | bytes accessed | tf_op | source)
XLA Modules:
  0.0 134.0 jit_solution(15808016603126190424)
XLA Ops:
  0.0 1.4 %deal.1 = (f32[2,128,128]{2,1,0:T(8,128)S(1)}, f32[2,128,128]{2,1,0:T(8,128)S(1)}, f32[2,128,128]{2,1,0:T(8,128)S(1)}, f32[2,128,128]{2,1,0:T(8,128)S(1)}, f32[2...) custom-call(f32[2,8,128,128]{3,2,1,0:T(8,128)} %source.1, ...), custom_call_target="tpu_custom_call" | custom-call | bytes 2097152 | tf_op jit(solution)/shard_map/deal/pallas_call | solution.py:75
  1.4 0.0 collective-permute-start
  1.4 2.9 %collective-permute-start.1 = (f32[2,128,128]{2,1,0:T(8,128)S(1)}, f32[2,128,128]{2,1,0:T(8,128)S(1)}, u32[]{:S(2)}, u32[]{:S(2)}) collective-permute-start(f32[2,128,128]{2,1,0:T(8,128)S(1)} %get-tuple-element.39), channel_id=1, source_target_pairs={{0,7},{1,0},{2,1},{3,2},{4,3},{5,4},{6,5},{7,6},{8,15},{9,8},{10,9... | collective-permute-start | bytes 393224 | tf_op jit(solution)/shard_map/ppermute | solution.py:316
  4.4 2.0 %collective-permute-start.2 = (f32[2,128,128]{2,1,0:T(8,128)S(1)}, f32[2,128,128]{2,1,0:T(8,128)S(1)}, u32[]{:S(2)}, u32[]{:S(2)}) collective-permute-start(f32[2,128,128]{2,1,0:T(8,128)S(1)} %get-tuple-element.42), channel_id=1, source_target_pairs={{0,4},{1,5},{2,6},{3,7},{4,0},{5,1},{6,2},{7,3},{8,12},{9,13},{10,... | collective-permute-start | bytes 393224 | tf_op jit(solution)/shard_map/ppermute | solution.py:316
  6.4 0.0 collective-permute-start.3
  6.4 3.2 %collective-permute-start.4 = (f32[2,128,128]{2,1,0:T(8,128)S(1)}, f32[2,128,128]{2,1,0:T(8,128)S(1)}, u32[]{:S(2)}, u32[]{:S(2)}) collective-permute-start(f32[2,128,128]{2,1,0:T(8,128)S(1)} %get-tuple-element.44), channel_id=1, source_target_pairs={{0,5},{1,6},{2,7},{3,0},{4,1},{5,2},{6,3},{7,4},{8,13},{9,14},{10,... | collective-permute-start | bytes 393224 | tf_op jit(solution)/shard_map/ppermute | solution.py:316
  9.6 0.0 collective-permute-done.refs_1_
  9.6 0.7 collective-permute-start.5
  10.3 0.0 collective-permute-done.1.refs_2_
  10.3 2.6 %collective-permute-start.6 = (f32[2,128,128]{2,1,0:T(8,128)S(1)}, f32[2,128,128]{2,1,0:T(8,128)S(1)}, u32[]{:S(2)}, u32[]{:S(2)}) collective-permute-start(f32[2,128,128]{2,1,0:T(8,128)S(1)} %get-tuple-element.46), channel_id=1, source_target_pairs={{0,6},{1,7},{2,0},{3,1},{4,2},{5,3},{6,4},{7,5},{8,14},{9,15},{10,... | collective-permute-start | bytes 393224 | tf_op jit(solution)/shard_map/ppermute | solution.py:316
  12.9 0.6 fusion.15
  13.5 0.6 iota_compare_fusion.2
  14.1 0.2 convert_reduce_fusion
  14.3 1.0 select_reduce_fusion
  15.3 0.1 squeeze.18
  15.4 0.1 squeeze.20
  15.5 0.1 squeeze.19
  15.6 0.2 fusion.3
  15.8 0.1 select_n.59
  15.9 0.1 reshape.113.touched
  16.0 2.2 %split_factors.1 = (bf16[2048,256]{1,0:T(8,128)(2,1)S(1)}, bf16[2048,256]{1,0:T(8,128)(2,1)S(1)}) custom-call(s32[128]{0:T(128)S(1)} %get-tuple-element.47.pair_region, f32[6,16,128,128]{3,2,1,0:T(8,128)} %factors.1), custom_call_target="tpu_custom_call" | custom-call | flops 1048576 | bytes 3145728 | tf_op jit(solution)/shard_map/split_factors/pallas_call | solution.py:40
  18.2 0.7 fusion.16
  18.9 0.0 collective-permute-done.2.refs_3_
  18.9 0.0 collective-permute-done.3.refs_4_
  18.9 0.0 collective-permute-done.4.refs_5_
  18.9 0.0 collective-permute-done.5.refs_6_
  18.9 0.0 collective-permute-done.6.refs_7_
  18.9 12.1 %ladder.1 = f32[16,128,128]{2,1,0:T(8,128)S(1)} custom-call(s32[16,16]{1,0:T(8,128)S(1)} %fusion.8.codes, s32[16,16]{1,0:T(8,128)S(1)} %reshape.113.touched, f32[2,128,128]{2,1,0:T(8,128)S(1)} %get-tuple-element.55.refs_0_, f32[2,128,128]{2,1,0:T(8,128)S(1)} %collective-permute-done.refs_1_, f32[2,128,128]{2,1,0:T(8,128)S(1)} %collective-permute-done.1.refs_2_, ...), custom_call_target="tpu_custom_call" | custom-call | flops 6442450944 | bytes 4194304 | tf_op jit(solution)/shard_map/ladder/pallas_call | solution.py:188
  31.0 43.2 %all_to_all.10.blocks = f32[256,8,128]{2,1,0:T(8,128)S(1)} all-to-all(f32[256,8,128]{2,1,0:T(8,128)S(1)} %bitcast.29), channel_id=1, replica_groups=mesh['pair'=32,'virt'=8] {'virt','pair'}, dimensions={0} | all-to-all | bytes 2097152 | tf_op jit(solution)/shard_map/all_to_all | solution.py:358
  74.3 1.0 join_pairs.1
  75.3 56.1 %all_to_all.11 = f32[512,8,128]{2,1,0:T(8,128)S(1)} all-to-all(f32[512,8,128]{2,1,0:T(8,128)S(1)} %join_pairs.1), channel_id=1, replica_groups=mesh['pair'=32,'virt'=8] {'pair'}, dimensions={0} | all-to-all | bytes 4194304 | tf_op jit(solution)/shard_map/all_to_all | solution.py:360
  131.4 2.6 %settle.1 = f32[2,16,128,128]{3,2,1,0:T(8,128)} custom-call(s32[1]{0:T(128)} %bitcast.3.held, f32[32,16,8,128]{3,2,1,0:T(8,128)S(1)} %bitcast.28), custom_call_target="tpu_custom_call" | custom-call | flops 262144 | bytes 4194304 | tf_op jit(solution)/shard_map/settle/pallas_call | solution.py:283
  (6 shorter events, 0.0 us)
Async XLA Ops:
  1.4 8.2 %collective-permute-start = (f32[2,128,128]{2,1,0:T(8,128)S(1)}, f32[2,128,128]{2,1,0:T(8,128)S(1)}, u32[]{:S(2)}, u32[]{:S(2)}) collective-permute-start(f32[2,128,128]{2,1,0:T(8,128)S(1)} %get-tuple-element.38), channel_id=1, source_target_pairs={{0,1},{1,2},{2,3},{3,4},{4,5},{5,6},{6,7},{7,0},{8,9},{9,10},{10,1... | collective-permute-start | bytes 393224 | tf_op jit(solution)/shard_map/ppermute | solution.py:316
  1.4 8.9 %collective-permute-start.1 = (f32[2,128,128]{2,1,0:T(8,128)S(1)}, f32[2,128,128]{2,1,0:T(8,128)S(1)}, u32[]{:S(2)}, u32[]{:S(2)}) collective-permute-start(f32[2,128,128]{2,1,0:T(8,128)S(1)} %get-tuple-element.39), channel_id=1, source_target_pairs={{0,7},{1,0},{2,1},{3,2},{4,3},{5,4},{6,5},{7,6},{8,15},{9,8},{10,9... | collective-permute-start | bytes 393224 | tf_op jit(solution)/shard_map/ppermute | solution.py:316
  4.4 14.5 %collective-permute-start.2 = (f32[2,128,128]{2,1,0:T(8,128)S(1)}, f32[2,128,128]{2,1,0:T(8,128)S(1)}, u32[]{:S(2)}, u32[]{:S(2)}) collective-permute-start(f32[2,128,128]{2,1,0:T(8,128)S(1)} %get-tuple-element.42), channel_id=1, source_target_pairs={{0,4},{1,5},{2,6},{3,7},{4,0},{5,1},{6,2},{7,3},{8,12},{9,13},{10,... | collective-permute-start | bytes 393224 | tf_op jit(solution)/shard_map/ppermute | solution.py:316
  6.4 12.5 %collective-permute-start.3 = (f32[2,128,128]{2,1,0:T(8,128)S(1)}, f32[2,128,128]{2,1,0:T(8,128)S(1)}, u32[]{:S(2)}, u32[]{:S(2)}) collective-permute-start(f32[2,128,128]{2,1,0:T(8,128)S(1)} %get-tuple-element.43), channel_id=1, source_target_pairs={{0,3},{1,4},{2,5},{3,6},{4,7},{5,0},{6,1},{7,2},{8,11},{9,12},{10,... | collective-permute-start | bytes 393224 | tf_op jit(solution)/shard_map/ppermute | solution.py:316
  6.4 12.5 %collective-permute-start.4 = (f32[2,128,128]{2,1,0:T(8,128)S(1)}, f32[2,128,128]{2,1,0:T(8,128)S(1)}, u32[]{:S(2)}, u32[]{:S(2)}) collective-permute-start(f32[2,128,128]{2,1,0:T(8,128)S(1)} %get-tuple-element.44), channel_id=1, source_target_pairs={{0,5},{1,6},{2,7},{3,0},{4,1},{5,2},{6,3},{7,4},{8,13},{9,14},{10,... | collective-permute-start | bytes 393224 | tf_op jit(solution)/shard_map/ppermute | solution.py:316
  9.6 9.3 %collective-permute-start.5 = (f32[2,128,128]{2,1,0:T(8,128)S(1)}, f32[2,128,128]{2,1,0:T(8,128)S(1)}, u32[]{:S(2)}, u32[]{:S(2)}) collective-permute-start(f32[2,128,128]{2,1,0:T(8,128)S(1)} %get-tuple-element.45), channel_id=1, source_target_pairs={{0,2},{1,3},{2,4},{3,5},{4,6},{5,7},{6,0},{7,1},{8,10},{9,11},{10,... | collective-permute-start | bytes 393224 | tf_op jit(solution)/shard_map/ppermute | solution.py:316
  10.3 8.6 %collective-permute-start.6 = (f32[2,128,128]{2,1,0:T(8,128)S(1)}, f32[2,128,128]{2,1,0:T(8,128)S(1)}, u32[]{:S(2)}, u32[]{:S(2)}) collective-permute-start(f32[2,128,128]{2,1,0:T(8,128)S(1)} %get-tuple-element.46), channel_id=1, source_target_pairs={{0,6},{1,7},{2,0},{3,1},{4,2},{5,3},{6,4},{7,5},{8,14},{9,15},{10,... | collective-permute-start | bytes 393224 | tf_op jit(solution)/shard_map/ppermute | solution.py:316

commit v11 on v10

--- a/solution.py
+++ b/solution.py
@@ -19,14 +19,21 @@
     return high, (x - high.astype(F32)).astype(BF16)
 
 
-def split_body(pair_region, factors, f_pair, f_turn, fac, sem, *, per_home):
+def split_body(pair_region, factors, f_pair, f_turn, fac, sems, *, per_home):
     slots, n, _ = fac.shape
     pair = lax.axis_index("pair") * per_home + lax.axis_index("virt")
     region = pair_region[lax.rem(pair, pair_region.shape[0])]
-    copy = pltpu.make_async_copy(factors.at[region], fac, sem)
-    copy.start()
-    copy.wait()
+    parts = sems.shape[0]
+    few = slots // parts
+    copies = []
+    for q in range(parts):
+        tiles = pl.ds(q * few, few)
+        copy = pltpu.make_async_copy(factors.at[region, tiles], fac.at[tiles], sems.at[q])
+        copy.start()
+        copies.append(copy)
     for l in range(slots):
+        if l % few == 0:
+            copies[l // few].wait()
         tile = fac[l]
         rows = slice(l * n, (l + 1) * n)
         f_pair[rows, :n], f_pair[rows, n:] = halves(tile)
@@ -45,7 +52,7 @@
             grid=(1,),
             in_specs=[pl.BlockSpec(memory_space=pltpu.HBM)],
             out_specs=[spec, spec],
-            scratch_shapes=[pltpu.VMEM((slots, n, n), F32), pltpu.SemaphoreType.DMA(())],
+            scratch_shapes=[pltpu.VMEM((slots, n, n), F32), pltpu.SemaphoreType.DMA((4,))],
         ),
         compiler_params=pltpu.CompilerParams(vmem_limit_bytes=16 << 20),
         cost_estimate=pl.CostEstimate(flops=1 << 20, bytes_accessed=3 << 20, transcendentals=0),

time: 134 us -> 134 us (level)
  no operation moved by 1% of the time
where the time goes in v11:
time: 134 us
  blocking collectives  99.4 us (74%)
  Pallas kernels  19.2 us (14%)
  starting transfers between devices  11.4 us (9%)
  other arithmetic  3.43 us (3%)
    all_to_all x1, blocking collectives, on_device(): lax.all_to_all(joined, 'pair', split_axis=0, concat_axis=0, tiled=True)  56.1 us
    all_to_all x1, blocking collectives, on_device(): lax.all_to_all(sheets, ('virt', 'pair'), split_axis=0, concat_axis=0, til...  43.2 us
    pallas_call x1, Pallas kernels, ladder(): pl.pallas_call(functools.partial(ladder_body, steps=steps), out_shape=jax...  12.1 us
    ppermute x7, starting transfers between devices, on_device(): amps[d] = lax.ppermute(pieces[d], 'virt', route)  11.4 us
  transfers between devices with their start and end apart: 7, of which 0 were waited for; matrix products, arithmetic and copies ran while one was open for 3% of the time, Pallas kernels for 2%

profile of v11, /device:TPU:2, one launch (start us, length us, event | category | flops | bytes accessed | tf_op | source)
XLA Modules:
  0.0 134.0 jit_solution(6316634043833497114)
XLA Ops:
  0.0 1.4 %deal.1 = (f32[2,128,128]{2,1,0:T(8,128)S(1)}, f32[2,128,128]{2,1,0:T(8,128)S(1)}, f32[2,128,128]{2,1,0:T(8,128)S(1)}, f32[2,128,128]{2,1,0:T(8,128)S(1)}, f32[2...) custom-call(f32[2,8,128,128]{3,2,1,0:T(8,128)} %source.1, ...), custom_call_target="tpu_custom_call" | custom-call | bytes 2097152 | tf_op jit(solution)/shard_map/deal/pallas_call | solution.py:82
  1.4 0.0 collective-permute-start
  1.4 2.9 %collective-permute-start.1 = (f32[2,128,128]{2,1,0:T(8,128)S(1)}, f32[2,128,128]{2,1,0:T(8,128)S(1)}, u32[]{:S(2)}, u32[]{:S(2)}) collective-permute-start(f32[2,128,128]{2,1,0:T(8,128)S(1)} %get-tuple-element.39), channel_id=1, source_target_pairs={{0,7},{1,0},{2,1},{3,2},{4,3},{5,4},{6,5},{7,6},{8,15},{9,8},{10,9... | collective-permute-start | bytes 393224 | tf_op jit(solution)/shard_map/ppermute | solution.py:323
  4.4 2.0 %collective-permute-start.2 = (f32[2,128,128]{2,1,0:T(8,128)S(1)}, f32[2,128,128]{2,1,0:T(8,128)S(1)}, u32[]{:S(2)}, u32[]{:S(2)}) collective-permute-start(f32[2,128,128]{2,1,0:T(8,128)S(1)} %get-tuple-element.42), channel_id=1, source_target_pairs={{0,4},{1,5},{2,6},{3,7},{4,0},{5,1},{6,2},{7,3},{8,12},{9,13},{10,... | collective-permute-start | bytes 393224 | tf_op jit(solution)/shard_map/ppermute | solution.py:323
  6.4 0.0 collective-permute-start.3
  6.4 3.2 %collective-permute-start.4 = (f32[2,128,128]{2,1,0:T(8,128)S(1)}, f32[2,128,128]{2,1,0:T(8,128)S(1)}, u32[]{:S(2)}, u32[]{:S(2)}) collective-permute-start(f32[2,128,128]{2,1,0:T(8,128)S(1)} %get-tuple-element.44), channel_id=1, source_target_pairs={{0,5},{1,6},{2,7},{3,0},{4,1},{5,2},{6,3},{7,4},{8,13},{9,14},{10,... | collective-permute-start | bytes 393224 | tf_op jit(solution)/shard_map/ppermute | solution.py:323
  9.6 0.0 collective-permute-done.refs_1_
  9.6 0.7 collective-permute-start.5
  10.3 0.0 collective-permute-done.1.refs_2_
  10.3 2.6 %collective-permute-start.6 = (f32[2,128,128]{2,1,0:T(8,128)S(1)}, f32[2,128,128]{2,1,0:T(8,128)S(1)}, u32[]{:S(2)}, u32[]{:S(2)}) collective-permute-start(f32[2,128,128]{2,1,0:T(8,128)S(1)} %get-tuple-element.46), channel_id=1, source_target_pairs={{0,6},{1,7},{2,0},{3,1},{4,2},{5,3},{6,4},{7,5},{8,14},{9,15},{10,... | collective-permute-start | bytes 393224 | tf_op jit(solution)/shard_map/ppermute | solution.py:323
  12.9 0.6 fusion.15
  13.5 0.6 iota_compare_fusion.2
  14.1 0.2 convert_reduce_fusion
  14.3 1.0 select_reduce_fusion
  15.3 0.1 squeeze.18
  15.4 0.1 squeeze.20
  15.5 0.1 squeeze.19
  15.6 0.2 fusion.3
  15.8 0.1 select_n.59
  15.9 0.1 reshape.113.touched
  16.0 2.1 %split_factors.1 = (bf16[2048,256]{1,0:T(8,128)(2,1)S(1)}, bf16[2048,256]{1,0:T(8,128)(2,1)S(1)}) custom-call(s32[128]{0:T(128)S(1)} %get-tuple-element.47.pair_region, f32[6,16,128,128]{3,2,1,0:T(8,128)} %factors.1), custom_call_target="tpu_custom_call" | custom-call | flops 1048576 | bytes 3145728 | tf_op jit(solution)/shard_map/split_factors/pallas_call | solution.py:47
  18.1 0.7 fusion.16
  18.9 0.0 collective-permute-done.2.refs_3_
  18.9 0.0 collective-permute-done.3.refs_4_
  18.9 0.0 collective-permute-done.4.refs_5_
  18.9 0.0 collective-permute-done.5.refs_6_
  18.9 0.0 collective-permute-done.6.refs_7_
  18.9 12.1 %ladder.1 = f32[16,128,128]{2,1,0:T(8,128)S(1)} custom-call(s32[16,16]{1,0:T(8,128)S(1)} %fusion.8.codes, s32[16,16]{1,0:T(8,128)S(1)} %reshape.113.touched, f32[2,128,128]{2,1,0:T(8,128)S(1)} %get-tuple-element.55.refs_0_, f32[2,128,128]{2,1,0:T(8,128)S(1)} %collective-permute-done.refs_1_, f32[2,128,128]{2,1,0:T(8,128)S(1)} %collective-permute-done.1.refs_2_, ...), custom_call_target="tpu_custom_call" | custom-call | flops 6442450944 | bytes 4194304 | tf_op jit(solution)/shard_map/ladder/pallas_call | solution.py:195
  31.0 43.2 %all_to_all.10.blocks = f32[256,8,128]{2,1,0:T(8,128)S(1)} all-to-all(f32[256,8,128]{2,1,0:T(8,128)S(1)} %bitcast.29), channel_id=1, replica_groups=mesh['pair'=32,'virt'=8] {'virt','pair'}, dimensions={0} | all-to-all | bytes 2097152 | tf_op jit(solution)/shard_map/all_to_all | solution.py:365
  74.2 1.0 join_pairs.1
  75.3 56.1 %all_to_all.11 = f32[512,8,128]{2,1,0:T(8,128)S(1)} all-to-all(f32[512,8,128]{2,1,0:T(8,128)S(1)} %join_pairs.1), channel_id=1, replica_groups=mesh['pair'=32,'virt'=8] {'pair'}, dimensions={0} | all-to-all | bytes 4194304 | tf_op jit(solution)/shard_map/all_to_all | solution.py:367
  131.4 2.6 %settle.1 = f32[2,16,128,128]{3,2,1,0:T(8,128)} custom-call(s32[1]{0:T(128)} %bitcast.3.held, f32[32,16,8,128]{3,2,1,0:T(8,128)S(1)} %bitcast.28), custom_call_target="tpu_custom_call" | custom-call | flops 262144 | bytes 4194304 | tf_op jit(solution)/shard_map/settle/pallas_call | solution.py:290
  (6 shorter events, 0.0 us)
Async XLA Ops:
  1.4 8.2 %collective-permute-start = (f32[2,128,128]{2,1,0:T(8,128)S(1)}, f32[2,128,128]{2,1,0:T(8,128)S(1)}, u32[]{:S(2)}, u32[]{:S(2)}) collective-permute-start(f32[2,128,128]{2,1,0:T(8,128)S(1)} %get-tuple-element.38), channel_id=1, source_target_pairs={{0,1},{1,2},{2,3},{3,4},{4,5},{5,6},{6,7},{7,0},{8,9},{9,10},{10,1... | collective-permute-start | bytes 393224 | tf_op jit(solution)/shard_map/ppermute | solution.py:323
  1.4 8.9 %collective-permute-start.1 = (f32[2,128,128]{2,1,0:T(8,128)S(1)}, f32[2,128,128]{2,1,0:T(8,128)S(1)}, u32[]{:S(2)}, u32[]{:S(2)}) collective-permute-start(f32[2,128,128]{2,1,0:T(8,128)S(1)} %get-tuple-element.39), channel_id=1, source_target_pairs={{0,7},{1,0},{2,1},{3,2},{4,3},{5,4},{6,5},{7,6},{8,15},{9,8},{10,9... | collective-permute-start | bytes 393224 | tf_op jit(solution)/shard_map/ppermute | solution.py:323
  4.4 14.5 %collective-permute-start.2 = (f32[2,128,128]{2,1,0:T(8,128)S(1)}, f32[2,128,128]{2,1,0:T(8,128)S(1)}, u32[]{:S(2)}, u32[]{:S(2)}) collective-permute-start(f32[2,128,128]{2,1,0:T(8,128)S(1)} %get-tuple-element.42), channel_id=1, source_target_pairs={{0,4},{1,5},{2,6},{3,7},{4,0},{5,1},{6,2},{7,3},{8,12},{9,13},{10,... | collective-permute-start | bytes 393224 | tf_op jit(solution)/shard_map/ppermute | solution.py:323
  6.4 12.5 %collective-permute-start.3 = (f32[2,128,128]{2,1,0:T(8,128)S(1)}, f32[2,128,128]{2,1,0:T(8,128)S(1)}, u32[]{:S(2)}, u32[]{:S(2)}) collective-permute-start(f32[2,128,128]{2,1,0:T(8,128)S(1)} %get-tuple-element.43), channel_id=1, source_target_pairs={{0,3},{1,4},{2,5},{3,6},{4,7},{5,0},{6,1},{7,2},{8,11},{9,12},{10,... | collective-permute-start | bytes 393224 | tf_op jit(solution)/shard_map/ppermute | solution.py:323
  6.4 12.5 %collective-permute-start.4 = (f32[2,128,128]{2,1,0:T(8,128)S(1)}, f32[2,128,128]{2,1,0:T(8,128)S(1)}, u32[]{:S(2)}, u32[]{:S(2)}) collective-permute-start(f32[2,128,128]{2,1,0:T(8,128)S(1)} %get-tuple-element.44), channel_id=1, source_target_pairs={{0,5},{1,6},{2,7},{3,0},{4,1},{5,2},{6,3},{7,4},{8,13},{9,14},{10,... | collective-permute-start | bytes 393224 | tf_op jit(solution)/shard_map/ppermute | solution.py:323
  9.6 9.3 %collective-permute-start.5 = (f32[2,128,128]{2,1,0:T(8,128)S(1)}, f32[2,128,128]{2,1,0:T(8,128)S(1)}, u32[]{:S(2)}, u32[]{:S(2)}) collective-permute-start(f32[2,128,128]{2,1,0:T(8,128)S(1)} %get-tuple-element.45), channel_id=1, source_target_pairs={{0,2},{1,3},{2,4},{3,5},{4,6},{5,7},{6,0},{7,1},{8,10},{9,11},{10,... | collective-permute-start | bytes 393224 | tf_op jit(solution)/shard_map/ppermute | solution.py:323
  10.3 8.6 %collective-permute-start.6 = (f32[2,128,128]{2,1,0:T(8,128)S(1)}, f32[2,128,128]{2,1,0:T(8,128)S(1)}, u32[]{:S(2)}, u32[]{:S(2)}) collective-permute-start(f32[2,128,128]{2,1,0:T(8,128)S(1)} %get-tuple-element.46), channel_id=1, source_target_pairs={{0,6},{1,7},{2,0},{3,1},{4,2},{5,3},{6,4},{7,5},{8,14},{9,15},{10,... | collective-permute-start | bytes 393224 | tf_op jit(solution)/shard_map/ppermute | solution.py:323
